TPU v7x, 512 devices: a whole 4x4x16 slice. The times are simulated.
512 devices in a mesh: section: 16 (over z), chan: 32 (over y, x, core).
Axes of the slice: x: 4, y: 4, z: 16, core: 2. Of those that a mesh axis runs over, the one named last changes fastest.
Arguments:
- inputs: bfloat16 [4, 512, 256], P(None, 'chan'), may hold values from -6 to 6
- front: bfloat16 [16, 512, 256], P('section', 'chan'), may hold values from -6 to 6
- back: bfloat16 [16, 512, 256], P('section', 'chan'), may hold values from -6 to 6
- saved: bfloat16 [16, 4, 512, 256], P('section', None, 'chan'), may hold values from -6 to 6
- weights: bfloat16 [16, 512, 27, 512], P('section', 'chan'), may hold values from -0.1875 to 0.1875
- cotangent: bfloat16 [4, 512, 256], P(None, 'chan'), may hold values from -6 to 6
Outputs:
- acts: bfloat16 [16, 4, 512, 256], P('section', None, 'chan')
- grads: bfloat16 [16, 4, 512, 256], P('section', None, 'chan')
- weight_grads: float32 [16, 512, 27, 512], P('section', 'chan')
All inputs are finite; a program needn't handle non-finite values.
Results may differ from a plain program's by a relative error of at most 0.035.
Values may be sent and summed in bfloat16 or wider, within the bound.
No kernel may reach another device: no remote copies, remote signals or barrier semaphores. Data moves between devices by JAX's collectives and lax.ppermute only.
A program may use at most 128 MiB of HBM per device.

v0:
```python
import jax
import jax.numpy as jnp
from jax import lax
from jax.sharding import PartitionSpec as P

SX = 4
SY = 8
SZ = 8


TAP_OFFSETS = [(i - 1, j - 1, l - 1) for i in range(3) for j in range(3) for l in range(3)]


def from_behind(value, axis, steps):
    count = lax.axis_size(axis)
    first, last = (max(0, -steps), min(count, count - steps))
    return lax.ppermute(value, axis, [(source, source + steps) for source in range(first, last)])


def shifted_view(values, offset):
    cell_count = SX * SY * SZ
    margin = SY * SZ + SZ + 1
    lead = values.ndim - 1
    padded = jnp.pad(values, [(0, 0)] * lead + [(margin, margin)])
    delta = offset[0] * SY * SZ + offset[1] * SZ + offset[2]
    moved = padded[..., margin + delta : margin + delta + cell_count]
    index = jnp.arange(cell_count, dtype=jnp.int32)
    first_pos = index // (SY * SZ) + offset[0]
    second_pos = index // SZ % SY + offset[1]
    third_pos = index % SZ + offset[2]
    inside = (
        (first_pos >= 0)
        & (first_pos < SX)
        & (second_pos >= 0)
        & (second_pos < SY)
        & (third_pos >= 0)
        & (third_pos < SZ)
    )
    return jnp.where(inside, moved, jnp.zeros_like(moved))


def tap_sum(taps):
    accum = shifted_view(taps[..., 0, :], TAP_OFFSETS[0])
    for index in range(1, 27):
        accum = accum + shifted_view(taps[..., index, :], TAP_OFFSETS[index])
    return accum


def tap_spread(values):
    return jnp.stack([shifted_view(values, (-o[0], -o[1], -o[2])) for o in TAP_OFFSETS], axis=-2)


def silu_slope(pre):
    logistic = jax.nn.sigmoid(pre)
    return logistic * (1.0 + pre * (1.0 - logistic))


def body(inputs, front, back, saved, weights, cotangent):
    section_count = lax.axis_size("section")
    section_index = lax.axis_index("section")
    first_section = section_index == 0
    last_section = section_index == section_count - 1
    round_count, own_filters, cell_count = inputs.shape
    channels = weights.shape[3]
    weight_rows = weights.reshape(own_filters * 27, channels)
    acts_list = []
    grads_list = []
    filter_grad = jnp.zeros((own_filters * 27, channels), jnp.float32)
    forward_recv = front[0]
    backward_recv = back[0]
    for round_index in range(round_count):
        layer_in = jnp.where(first_section, inputs[round_index], forward_recv)
        taps = jnp.dot(
            weight_rows,
            lax.all_gather(layer_in, "chan", axis=0, tiled=True),
            preferred_element_type=jnp.float32,
        )
        pre = tap_sum(taps.reshape(own_filters, 27, cell_count))
        layer_out = jax.nn.silu(pre).astype(jnp.bfloat16)
        acts_list.append(layer_out)
        if round_index + 1 < round_count:
            forward_recv = from_behind(layer_out, "section", 1)
        whole_in = lax.all_gather(saved[0, round_index], "chan", axis=0, tiled=True)
        back_taps = jnp.dot(weight_rows, whole_in, preferred_element_type=jnp.float32)
        pre_back = tap_sum(back_taps.reshape(own_filters, 27, cell_count))
        grad_out = jnp.where(last_section, cotangent[round_index], backward_recv)
        dpre = (grad_out.astype(jnp.float32) * silu_slope(pre_back)).astype(jnp.bfloat16)
        spread = tap_spread(dpre).reshape(own_filters * 27, cell_count)
        grad_in = lax.psum_scatter(
            lax.dot_general(
                weight_rows, spread, (((0,), (0,)), ((), ())), preferred_element_type=jnp.float32
            ).astype(jnp.bfloat16),
            "chan",
            scatter_dimension=0,
            tiled=True,
        )
        filter_grad = filter_grad + lax.dot_general(
            spread, whole_in, (((1,), (1,)), ((), ())), preferred_element_type=jnp.float32
        )
        grads_list.append(grad_in)
        if round_index + 1 < round_count:
            backward_recv = from_behind(grad_in, "section", -1)
    acts = jnp.stack(acts_list, axis=0)[None]
    grads = jnp.stack(grads_list, axis=0)[None]
    return (acts, grads, filter_grad.reshape(1, own_filters, 27, channels))


def solution(mesh):
    return jax.shard_map(
        body,
        mesh=mesh,
        in_specs=(
            P(None, "chan", None),
            P("section", "chan", None),
            P("section", "chan", None),
            P("section", None, "chan", None),
            P("section", "chan", None, None),
            P(None, "chan", None),
        ),
        out_specs=(
            P("section", None, "chan", None),
            P("section", None, "chan", None),
            P("section", "chan", None, None),
        ),
        check_vma=False,
    )
```

profile of v0, /device:TPU:32, one launch (start us, length us, event | category | flops | bytes accessed | tf_op | source)
XLA Modules:
  0.0 543.6 jit_solution(12856307479175917620)
XLA Ops:
  7.2 0.8 fusion.670
  8.0 25.1 %all-gather.1 = bf16[1,1,512,256]{3,2,1,0:T(8,128)(2,1)S(1)} all-gather(bf16[1,1,16,256]{3,2,1,0:T(8,128)(2,1)S(1)} %get-tuple-element.222), channel_id=3, replica_groups=mesh['section'=16,'chan'=32] {'chan'}, dimensions={2}, use_global_device_ids=true | all-gather | bytes 270336 | tf_op jit(solution)/shard_map/all_gather | solution.py:83
  33.0 1.4 fusion.4
  36.6 0.9 fusion.443
  39.9 1.1 fusion
  41.8 24.1 %all-gather = bf16[1,512,256]{2,1,0:T(8,128)(2,1)S(1)} all-gather(bf16[1,16,256]{2,1,0:T(8,128)(2,1)S(1)} %slice_select_fusion), channel_id=2, replica_groups=mesh['section'=16,'chan'=32] {'chan'}, dimensions={1}, use_global_device_ids=true | all-gather | bytes 270336 | tf_op jit(solution)/shard_map/all_gather | solution.py:75
  67.2 3.8 collective-permute-start
  71.0 22.6 %all-gather.2 = bf16[1,1,512,256]{3,2,1,0:T(8,128)(2,1)S(1)} all-gather(bf16[1,1,16,256]{3,2,1,0:T(8,128)(2,1)S(1)} %get-tuple-element.223), channel_id=4, replica_groups=mesh['section'=16,'chan'=32] {'chan'}, dimensions={2}, use_global_device_ids=true | all-gather | bytes 270336 | tf_op jit(solution)/shard_map/all_gather | solution.py:83
  93.8 0.9 slice_bitcast_fusion.80
  95.7 24.1 %all-gather.3 = bf16[1,1,512,256]{3,2,1,0:T(8,128)(2,1)S(1)} all-gather(bf16[1,1,16,256]{3,2,1,0:T(8,128)(2,1)S(1)} %get-tuple-element.225), channel_id=5, replica_groups=mesh['section'=16,'chan'=32] {'chan'}, dimensions={2}, use_global_device_ids=true | all-gather | bytes 270336 | tf_op jit(solution)/shard_map/all_gather | solution.py:83
  120.1 0.9 slice_bitcast_fusion.53
  121.0 22.7 %all-gather.4 = bf16[1,1,512,256]{3,2,1,0:T(8,128)(2,1)S(1)} all-gather(bf16[1,1,16,256]{3,2,1,0:T(8,128)(2,1)S(1)} %get-tuple-element.224), channel_id=6, replica_groups=mesh['section'=16,'chan'=32] {'chan'}, dimensions={2}, use_global_device_ids=true | all-gather | bytes 270336 | tf_op jit(solution)/shard_map/all_gather | solution.py:83
  144.0 0.9 slice_bitcast_fusion.26
  145.5 24.2 %all_gather.25 = bf16[512,256]{1,0:T(8,128)(2,1)S(1)} all-gather(bf16[16,256]{1,0:T(8,128)(2,1)S(1)} %bitcast_select_fusion.5), channel_id=1, replica_groups=mesh['section'=16,'chan'=32] {'chan'}, dimensions={0}, use_global_device_ids=true | all-gather | bytes 270336 | tf_op jit(solution)/shard_map/all_gather | solution.py:75
  171.8 3.8 collective-permute-start.1
  176.3 1.0 collective-permute-done.1
  178.0 22.5 %all_gather.26 = bf16[512,256]{1,0:T(8,128)(2,1)S(1)} all-gather(bf16[16,256]{1,0:T(8,128)(2,1)S(1)} %bitcast_select_fusion.4), channel_id=1, replica_groups=mesh['section'=16,'chan'=32] {'chan'}, dimensions={0}, use_global_device_ids=true | all-gather | bytes 270336 | tf_op jit(solution)/shard_map/all_gather | solution.py:75
  201.6 1.9 collective-permute-start.3
  204.0 4.7 collective-permute-start.2
  209.4 0.9 multiply_convert_fusion.2
  212.6 1.1 fusion.1
  214.4 24.1 %all_gather.27 = bf16[512,256]{1,0:T(8,128)(2,1)S(1)} all-gather(bf16[16,256]{1,0:T(8,128)(2,1)S(1)} %bitcast_select_fusion.3), channel_id=1, replica_groups=mesh['section'=16,'chan'=32] {'chan'}, dimensions={0}, use_global_device_ids=true | all-gather | bytes 270336 | tf_op jit(solution)/shard_map/all_gather | solution.py:75
  238.9 76.2 %reduce-scatter.7.cloned.1.call-done = bf16[16,256]{1,0:T(8,128)(2,1)} async-done(((bf16[512,256]{1,0:T(8,128)(2,1)}), bf16[16,256]{1,0:T(8,128)(2,1)}) %reduce-scatter.7.cloned.1.call-update) | async-done | bytes 8208 | tf_op jit(solution)/shard_map/reduce_scatter | solution.py:89
  315.0 2.6 collective-permute-start.4
  318.0 0.9 fusion.662
  318.9 1.9 collective-permute-done.4
  321.5 1.1 multiply_convert_fusion.1
  324.8 1.1 fusion.2
  326.7 0.7 copy-done.72
  327.4 0.7 copy-done.71
  328.1 0.7 copy-done.70
  328.8 0.7 copy-done.69
  329.5 0.7 copy-done.68
  330.3 0.7 copy-done.67
  331.0 0.7 copy-done.66
  331.7 0.7 copy-done.65
  332.4 0.7 copy-done.64
  333.1 0.7 copy-done.63
  333.8 0.7 copy-done.62
  334.6 0.7 copy-done.61
  336.8 88.7 %reduce-scatter.9.cloned.1.call-done = bf16[16,256]{1,0:T(8,128)(2,1)} async-done(((bf16[512,256]{1,0:T(8,128)(2,1)}), bf16[16,256]{1,0:T(8,128)(2,1)}) %reduce-scatter.9.cloned.1.call-update) | async-done | bytes 8208 | tf_op jit(solution)/shard_map/reduce_scatter | solution.py:89
  425.5 2.4 collective-permute-start.5
  428.4 2.8 collective-permute-done.5
  432.0 0.9 multiply_convert_fusion
  435.1 1.1 fusion.3
  437.0 1.4 copy.461
  438.4 97.3 %reduce-scatter.11.cloned.1.call-done = bf16[16,256]{1,0:T(8,128)(2,1)} async-done(((bf16[512,256]{1,0:T(8,128)(2,1)}), bf16[16,256]{1,0:T(8,128)(2,1)}) %reduce-scatter.11.cloned.1.call-update) | async-done | bytes 8208 | tf_op jit(solution)/shard_map/reduce_scatter | solution.py:89
  535.7 1.3 maximum_bitcast_fusion.1
  (591 shorter events, 24.9 us)
Async XLA Ops:
  7.2 194.4 %reduce-scatter.5.cloned.1.call-start = ((), (), s32[]{:S(2)}) async-start(), calls=%async_computation.4 | async-start | bytes 270336 | tf_op jit(solution)/shard_map/reduce_scatter | solution.py:89
  34.9 31.8 %copy-start.55 = (pred[256]{0:T(512)(128)(4,1)}, pred[256]{0:T(512)(128)(4,1)S(1)}, u32[]{:S(2)}) copy-start(pred[256]{0:T(512)(128)(4,1)S(1)} %get-tuple-element.253) | copy-start | bytes 772
  34.9 31.8 %copy-start.58 = (pred[256]{0:T(512)(128)(4,1)}, pred[256]{0:T(512)(128)(4,1)S(1)}, u32[]{:S(2)}) copy-start(pred[256]{0:T(512)(128)(4,1)S(1)} %get-tuple-element.252) | copy-start | bytes 772
  34.9 31.8 %copy-start.49 = (pred[256]{0:T(512)(128)(4,1)}, pred[256]{0:T(512)(128)(4,1)S(1)}, u32[]{:S(2)}) copy-start(pred[256]{0:T(512)(128)(4,1)S(1)} %get-tuple-element.255) | copy-start | bytes 772
  34.9 31.8 %copy-start.52 = (pred[256]{0:T(512)(128)(4,1)}, pred[256]{0:T(512)(128)(4,1)S(1)}, u32[]{:S(2)}) copy-start(pred[256]{0:T(512)(128)(4,1)S(1)} %get-tuple-element.254) | copy-start | bytes 772
  35.0 31.8 %copy-start.43 = (pred[256]{0:T(512)(128)(4,1)}, pred[256]{0:T(512)(128)(4,1)S(1)}, u32[]{:S(2)}) copy-start(pred[256]{0:T(512)(128)(4,1)S(1)} %get-tuple-element.257) | copy-start | bytes 772
  35.0 31.8 %copy-start.46 = (pred[256]{0:T(512)(128)(4,1)}, pred[256]{0:T(512)(128)(4,1)S(1)}, u32[]{:S(2)}) copy-start(pred[256]{0:T(512)(128)(4,1)S(1)} %get-tuple-element.256) | copy-start | bytes 772
  35.0 31.8 %copy-start.37 = (pred[256]{0:T(512)(128)(4,1)}, pred[256]{0:T(512)(128)(4,1)S(1)}, u32[]{:S(2)}) copy-start(pred[256]{0:T(512)(128)(4,1)S(1)} %get-tuple-element.259) | copy-start | bytes 772
  35.0 31.8 %copy-start.40 = (pred[256]{0:T(512)(128)(4,1)}, pred[256]{0:T(512)(128)(4,1)S(1)}, u32[]{:S(2)}) copy-start(pred[256]{0:T(512)(128)(4,1)S(1)} %get-tuple-element.258) | copy-start | bytes 772
  35.0 31.8 %copy-start.31 = (pred[256]{0:T(512)(128)(4,1)}, pred[256]{0:T(512)(128)(4,1)S(1)}, u32[]{:S(2)}) copy-start(pred[256]{0:T(512)(128)(4,1)S(1)} %get-tuple-element.261) | copy-start | bytes 772
  35.0 31.8 %copy-start.34 = (pred[256]{0:T(512)(128)(4,1)}, pred[256]{0:T(512)(128)(4,1)S(1)}, u32[]{:S(2)}) copy-start(pred[256]{0:T(512)(128)(4,1)S(1)} %get-tuple-element.260) | copy-start | bytes 772
  35.1 31.8 %copy-start.25 = (pred[256]{0:T(512)(128)(4,1)}, pred[256]{0:T(512)(128)(4,1)S(1)}, u32[]{:S(2)}) copy-start(pred[256]{0:T(512)(128)(4,1)S(1)} %get-tuple-element.263) | copy-start | bytes 772
  35.1 31.8 %copy-start.28 = (pred[256]{0:T(512)(128)(4,1)}, pred[256]{0:T(512)(128)(4,1)S(1)}, u32[]{:S(2)}) copy-start(pred[256]{0:T(512)(128)(4,1)S(1)} %get-tuple-element.262) | copy-start | bytes 772
  35.1 31.8 %copy-start.19 = (pred[256]{0:T(512)(128)(4,1)}, pred[256]{0:T(512)(128)(4,1)S(1)}, u32[]{:S(2)}) copy-start(pred[256]{0:T(512)(128)(4,1)S(1)} %get-tuple-element.265) | copy-start | bytes 772
  35.1 31.8 %copy-start.22 = (pred[256]{0:T(512)(128)(4,1)}, pred[256]{0:T(512)(128)(4,1)S(1)}, u32[]{:S(2)}) copy-start(pred[256]{0:T(512)(128)(4,1)S(1)} %get-tuple-element.264) | copy-start | bytes 772
  35.1 31.7 %copy-start.13 = (pred[256]{0:T(512)(128)(4,1)}, pred[256]{0:T(512)(128)(4,1)S(1)}, u32[]{:S(2)}) copy-start(pred[256]{0:T(512)(128)(4,1)S(1)} %get-tuple-element.267) | copy-start | bytes 772
  35.1 31.7 %copy-start.16 = (pred[256]{0:T(512)(128)(4,1)}, pred[256]{0:T(512)(128)(4,1)S(1)}, u32[]{:S(2)}) copy-start(pred[256]{0:T(512)(128)(4,1)S(1)} %get-tuple-element.266) | copy-start | bytes 772
  35.2 31.7 %copy-start.7 = (pred[256]{0:T(512)(128)(4,1)}, pred[256]{0:T(512)(128)(4,1)S(1)}, u32[]{:S(2)}) copy-start(pred[256]{0:T(512)(128)(4,1)S(1)} %get-tuple-element.269) | copy-start | bytes 772
  35.2 31.7 %copy-start.10 = (pred[256]{0:T(512)(128)(4,1)}, pred[256]{0:T(512)(128)(4,1)S(1)}, u32[]{:S(2)}) copy-start(pred[256]{0:T(512)(128)(4,1)S(1)} %get-tuple-element.268) | copy-start | bytes 772
  35.2 31.7 %copy-start.4 = (pred[256]{0:T(512)(128)(4,1)}, pred[256]{0:T(512)(128)(4,1)S(1)}, u32[]{:S(2)}) copy-start(pred[256]{0:T(512)(128)(4,1)S(1)} %get-tuple-element.270) | copy-start | bytes 772
  41.0 274.0 %reduce-scatter.7.cloned.1.call-start = ((), (), s32[]{:S(2)}) async-start(), calls=%async_computation.5 | async-start | bytes 270336 | tf_op jit(solution)/shard_map/reduce_scatter | solution.py:89
  67.1 26.4 %copy-start.147 = (bf16[16,256]{1,0:T(8,128)(2,1)}, bf16[16,256]{1,0:T(8,128)(2,1)S(1)}, u32[]{:S(2)}) copy-start(bf16[16,256]{1,0:T(8,128)(2,1)S(1)} %multiply_convert_fusion.6) | copy-start | bytes 24580
  67.2 78.3 %collective-permute-start = (bf16[16,256]{1,0:T(8,128)(2,1)S(1)}, bf16[16,256]{1,0:T(8,128)(2,1)S(1)}, u32[]{:S(2)}, u32[]{:S(2)}) collective-permute-start(bf16[16,256]{1,0:T(8,128)(2,1)S(1)} %multiply_convert_fusion.6), channel_id=1, source_target_pairs={{0,32},{32,64},{64,96},{96,128},{128,160},{160,192},{192,224},{224... | collective-permute-start | bytes 24584 | tf_op jit(solution)/shard_map/ppermute | solution.py:17
  120.1 24.7 %copy-start.2 = (f32[16,27,256]{2,0,1:T(8,128)}, f32[16,27,256]{2,0,1:T(8,128)S(1)}, u32[]{:S(2)}) copy-start(f32[16,27,256]{2,0,1:T(8,128)S(1)} %fusion.8) | copy-start | bytes 1327108
  144.0 31.6 %copy-start.1 = (f32[16,27,256]{2,0,1:T(8,128)}, f32[16,27,256]{2,0,1:T(8,128)S(1)}, u32[]{:S(2)}) copy-start(f32[16,27,256]{2,0,1:T(8,128)S(1)} %fusion.6) | copy-start | bytes 1327108
  171.8 5.5 %collective-permute-start.1 = (bf16[16,256]{1,0:T(8,128)(2,1)S(1)}, bf16[16,256]{1,0:T(8,128)(2,1)S(1)}, u32[]{:S(2)}, u32[]{:S(2)}) collective-permute-start(bf16[16,256]{1,0:T(8,128)(2,1)S(1)} %multiply_convert_fusion.5), channel_id=1, source_target_pairs={{0,32},{32,64},{64,96},{96,128},{128,160},{160,192},{192,224},{224... | collective-permute-start | bytes 24584 | tf_op jit(solution)/shard_map/ppermute | solution.py:17
  201.6 7.1 %collective-permute-start.3 = (bf16[16,256]{1,0:T(8,128)(2,1)}, bf16[16,256]{1,0:T(8,128)(2,1)S(1)}, u32[]{:S(2)}, u32[]{:S(2)}) collective-permute-start(bf16[16,256]{1,0:T(8,128)(2,1)} %reduce-scatter.5.cloned.1.call-done), channel_id=1, source_target_pairs={{32,0},{64,32},{96,64},{128,96},{160,128},{192,160},{224,192},{256... | collective-permute-start | bytes 24584 | tf_op jit(solution)/shard_map/ppermute | solution.py:17
  203.5 5.2 copy-start.91
  203.5 5.2 copy-start.92
  203.5 5.2 copy-start.93
  203.5 5.2 copy-start.94
  203.5 5.2 copy-start.128
  203.5 5.2 copy-start.129
  203.5 5.2 copy-start.130
  203.6 5.2 copy-start.131
  203.6 5.2 copy-start.132
  203.6 5.2 copy-start.133
  203.6 5.2 copy-start.134
  203.6 5.2 copy-start.135
  203.6 5.2 copy-start.136
  204.0 9.7 %collective-permute-start.2 = (bf16[16,256]{1,0:T(8,128)(2,1)S(1)}, bf16[16,256]{1,0:T(8,128)(2,1)S(1)}, u32[]{:S(2)}, u32[]{:S(2)}) collective-permute-start(bf16[16,256]{1,0:T(8,128)(2,1)S(1)} %multiply_convert_fusion.4), channel_id=1, source_target_pairs={{0,32},{32,64},{64,96},{96,128},{128,160},{160,192},{192,224},{224... | collective-permute-start | bytes 24584 | tf_op jit(solution)/shard_map/ppermute | solution.py:17
  213.6 211.8 %reduce-scatter.9.cloned.1.call-start = ((), (), s32[]{:S(2)}) async-start(), calls=%async_computation.6 | async-start | bytes 270336 | tf_op jit(solution)/shard_map/reduce_scatter | solution.py:89
  315.0 5.7 %collective-permute-start.4 = (bf16[16,256]{1,0:T(8,128)(2,1)}, bf16[16,256]{1,0:T(8,128)(2,1)S(1)}, u32[]{:S(2)}, u32[]{:S(2)}) collective-permute-start(bf16[16,256]{1,0:T(8,128)(2,1)} %reduce-scatter.7.cloned.1.call-done), channel_id=1, source_target_pairs={{32,0},{64,32},{96,64},{128,96},{160,128},{192,160},{224,192},{256... | collective-permute-start | bytes 24584 | tf_op jit(solution)/shard_map/ppermute | solution.py:17
  325.9 209.8 %reduce-scatter.11.cloned.1.call-start = ((), (), s32[]{:S(2)}) async-start(), calls=%async_computation.7 | async-start | bytes 270336 | tf_op jit(solution)/shard_map/reduce_scatter | solution.py:89
  425.5 5.7 %collective-permute-start.5 = (bf16[16,256]{1,0:T(8,128)(2,1)}, bf16[16,256]{1,0:T(8,128)(2,1)S(1)}, u32[]{:S(2)}, u32[]{:S(2)}) collective-permute-start(bf16[16,256]{1,0:T(8,128)(2,1)} %reduce-scatter.9.cloned.1.call-done), channel_id=1, source_target_pairs={{32,0},{64,32},{96,64},{128,96},{160,128},{192,160},{224,192},{256... | collective-permute-start | bytes 24584 | tf_op jit(solution)/shard_map/ppermute | solution.py:17
  437.0 98.8 %copy-start.156 = (bf16[16,256]{1,0:T(8,128)(2,1)S(1)}, bf16[16,256]{1,0:T(8,128)(2,1)}, u32[]{:S(2)}) copy-start(bf16[16,256]{1,0:T(8,128)(2,1)} %reduce-scatter.5.cloned.1.call-done) | copy-start | bytes 24580
  437.0 98.8 %copy-start.157 = (bf16[16,256]{1,0:T(8,128)(2,1)S(1)}, bf16[16,256]{1,0:T(8,128)(2,1)}, u32[]{:S(2)}) copy-start(bf16[16,256]{1,0:T(8,128)(2,1)} %reduce-scatter.7.cloned.1.call-done) | copy-start | bytes 24580
  437.0 98.8 %copy-start.158 = (bf16[16,256]{1,0:T(8,128)(2,1)S(1)}, bf16[16,256]{1,0:T(8,128)(2,1)}, u32[]{:S(2)}) copy-start(bf16[16,256]{1,0:T(8,128)(2,1)} %reduce-scatter.9.cloned.1.call-done) | copy-start | bytes 24580
  (121 other events, 285.6 us)
Sparse Core Ops, SparseCore 0:
  41.1 101.9 reduce-scatter.4
  213.8 101.2 reduce-scatter.6
  326.1 99.3 reduce-scatter.8
  436.3 99.3 reduce-scatter.10
where the time goes:
time: 547 us; the launch traced here: 544 us
  waiting for transfers between devices  268 us (49%)
  blocking collectives  189 us (35%)
  local copies, waits for them, and re-layouts  24.7 us (5%)
  starting transfers between devices  19.4 us (4%)
  between operations  17 us (3%)
  other arithmetic  16.3 us (3%)
  matrix products  8.86 us (2%)
    reduce_scatter x4, waiting for transfers between devices, body(): lax.psum_scatter(lax.dot_general(weight_rows, spread, (((0,), (0,)), ((),...  262 us
    all_gather x4, blocking collectives, body(): lax.all_gather(layer_in, 'chan', axis=0, tiled=True)  94.9 us
    all_gather x4, blocking collectives, body(): whole_in = lax.all_gather(saved[0, round_index], 'chan', axis=0, tiled=True)  94.5 us
    ppermute x6, starting transfers between devices, from_behind(): lax.ppermute(value, axis, [(source, source + steps) for source in range(f...  19.2 us
    unnamed x398, local copies, waits for them, and re-layouts  15.7 us
  transfers between devices with their start and end apart: 10, of which 6 were waited for; matrix products, arithmetic and copies ran while one was open for 3% of the time, Pallas kernels for 0%

commit v1 on v0

v1 whole, which is shorter than its diff:
```python
import jax
import jax.numpy as jnp
from jax import lax
from jax.experimental import pallas as pl
from jax.experimental.pallas import tpu as pltpu
from jax.sharding import Mesh, PartitionSpec as P


SX, SY, SZ = 4, 8, 8
CELLS = SX * SY * SZ
TAPS = 27
OWN = 16
PAIR = 32
ROUNDS = 4
CHANNELS = 512
ROWS = TAPS * OWN
STEPS = (SY * SZ, SZ, 1)
EXTENT = (SX, SY, SZ)
VMEM_LIMIT = 48 * 1024 * 1024


def coordinates(rows):
    cell = lax.broadcasted_iota(jnp.int32, (rows, CELLS), 1)
    return (cell >> 6, (cell >> 3) & 7, cell & 7)


def moved(value, where, axis, step):
    if step == 0:
        return value
    rolled = pltpu.roll(value, (-step * STEPS[axis]) % CELLS, 1)
    place = where[axis]
    inside = place < EXTENT[axis] - 1 if step > 0 else place > 0
    return jnp.where(inside, rolled, 0.0)


def tap_total(taps, base, where):
    total = None
    for i in range(3):
        plane = None
        for j in range(3):
            line = None
            for l in range(3):
                start = base + OWN * (9 * i + 3 * j + l)
                term = moved(taps[start : start + OWN, :], where, 2, l - 1)
                line = term if line is None else line + term
            line = moved(line, where, 1, j - 1)
            plane = line if plane is None else plane + line
        plane = moved(plane, where, 0, i - 1)
        total = plane if total is None else total + plane
    return total


def spread_into(spread, base, value, where):
    for i in range(3):
        plane = moved(value, where, 0, 1 - i)
        for j in range(3):
            line = moved(plane, where, 1, 1 - j)
            for l in range(3):
                start = base + OWN * (9 * i + 3 * j + l)
                spread[start : start + OWN, :] = moved(line, where, 2, 1 - l).astype(jnp.bfloat16)


def slope_kernel(filters, stored, slope, taps):
    where = coordinates(OWN)
    for r in range(stored.shape[1]):
        whole = stored[:, r].reshape(CHANNELS, CELLS)
        taps[...] = jnp.dot(filters[...], whole, preferred_element_type=jnp.float32)
        for c in range(2):
            pre = tap_total(taps, ROWS * c, where)
            logistic = 1.0 / (1.0 + jnp.exp(-pre))
            slope[r, OWN * c : OWN * (c + 1), :] = logistic * (1.0 + pre * (1.0 - logistic))


def finish_kernel(flags, arrived, filters, out, taps):
    @pl.when(flags[0] == 0)
    def _():
        where = coordinates(OWN)
        whole = arrived[...].reshape(CHANNELS, CELLS)
        taps[...] = jnp.dot(filters[...], whole, preferred_element_type=jnp.float32)
        for c in range(2):
            pre = tap_total(taps, ROWS * c, where)
            out[OWN * c : OWN * (c + 1), :] = (pre / (1.0 + jnp.exp(-pre))).astype(jnp.bfloat16)

    @pl.when(flags[0] != 0)
    def _():
        total = arrived[0].astype(jnp.float32)
        for p in range(1, arrived.shape[0]):
            total = total + arrived[p].astype(jnp.float32)
        out[...] = total.astype(jnp.bfloat16)


def start_kernel(edge_slot, flags, received, outside, slope, filters, sent, dpre, spread):
    take = flags[edge_slot] != 0
    value = jnp.where(take, outside[...].astype(jnp.float32), received[...].astype(jnp.float32))

    @pl.when(flags[0] == 0)
    def _():
        copy = value.astype(jnp.bfloat16)
        dpre[...] = copy
        for p in range(sent.shape[0]):
            sent[p] = copy

    @pl.when(flags[0] != 0)
    def _():
        where = coordinates(OWN)
        rounded = (value * slope[...]).astype(jnp.bfloat16)
        dpre[...] = rounded
        wide = rounded.astype(jnp.float32)
        for c in range(2):
            spread_into(spread, ROWS * c, wide[OWN * c : OWN * (c + 1), :], where)
        part = lax.dot_general(
            filters[...], spread[...], (((0,), (0,)), ((), ())), preferred_element_type=jnp.float32
        )
        sent[...] = part.astype(jnp.bfloat16).reshape(sent.shape)


def filter_kernel(dpre, first, later, out, spread):
    where = coordinates(OWN)
    for r in range(ROUNDS):
        spread_into(spread, 0, dpre[r].astype(jnp.float32), where)
        stored = first[:, 0] if r == 0 else later[:, r - 1]
        term = lax.dot_general(
            spread[...],
            stored.reshape(CHANNELS, CELLS),
            (((1,), (1,)), ((), ())),
            preferred_element_type=jnp.float32,
        )
        if r == 0:
            out[...] = term
        else:
            out[...] += term


def local_call(kernel, outs, kinds, scratch):
    spaces = {"s": pltpu.SMEM, "v": pltpu.VMEM}
    specs = [pl.BlockSpec(memory_space=spaces[kind]) for kind in kinds]
    result = jax.tree.map(lambda _: pl.BlockSpec(memory_space=pltpu.VMEM), outs)
    return pl.pallas_call(
        kernel,
        out_shape=outs,
        in_specs=specs,
        out_specs=result,
        scratch_shapes=scratch,
        compiler_params=pltpu.CompilerParams(vmem_limit_bytes=VMEM_LIMIT),
    )


def shape(dims, dtype=jnp.bfloat16):
    return jax.ShapeDtypeStruct(dims, dtype)


def gathered(block, axes, count):
    copies = jnp.broadcast_to(block[None], (count,) + block.shape)
    return lax.all_to_all(copies, axes, 0, 0)


def body(sections, inputs, front, back, saved, weights, cotangent):
    chips = CHANNELS // PAIR
    section = lax.axis_index("section")
    core = lax.axis_index("core")
    forward = core == 0
    at_edge = jnp.where(forward, section == 0, section == sections - 1)
    flags = jnp.stack([core, at_edge.astype(jnp.int32), jnp.int32(1)]).astype(jnp.int32)
    hop_pairs = []
    for s in range(sections):
        for p in range(chips):
            here = (s * chips + p) * 2
            if s + 1 < sections:
                hop_pairs.append((here, here + 2 * chips))
            if s > 0:
                hop_pairs.append((here + 1, here + 1 - 2 * chips))

    everyone = ("chip", "core")
    stored_first = gathered(saved[0, :1], everyone, 2 * chips)
    stored_later = gathered(saved[0, 1:], everyone, 2 * chips)

    filters = lax.all_gather(
        jnp.transpose(weights[0], (1, 0, 2)).reshape(ROWS, CHANNELS), "core", axis=0, tiled=True
    )
    ends = jnp.concatenate(
        [
            jnp.where(section == 0, inputs[:1], front),
            inputs[1:],
            jnp.where(section == sections - 1, cotangent[:1], back),
            cotangent[1:],
        ]
    )
    ends = lax.all_gather(ends, "core", axis=1, tiled=True)
    outside = jnp.where(forward, ends[:ROUNDS], ends[ROUNDS:])

    taps_scratch = pltpu.VMEM((2 * ROWS, CELLS), jnp.float32)
    spread_scratch = pltpu.VMEM((2 * ROWS, CELLS), jnp.bfloat16)
    slope_of = lambda stored, n: local_call(
        slope_kernel, shape((n, PAIR, CELLS), jnp.float32), "vv", [taps_scratch]
    )(filters, stored)
    slopes = [slope_of(stored_first, 1)[0]]

    outs, dpres = [], []
    received = outside[0]
    for r in range(ROUNDS):
        edge_slot = 2 if r == 0 else 1
        sent, dpre = local_call(
            lambda *refs: start_kernel(edge_slot, *refs),
            (shape((chips, PAIR, CELLS)), shape((PAIR, CELLS))),
            "svvvv",
            [spread_scratch],
        )(flags, received, outside[r], slopes[r], filters)
        dpres.append(dpre)
        arrived = lax.all_to_all(sent, "chip", 0, 0)
        if r == 0:
            rest = slope_of(stored_later, ROUNDS - 1)
            slopes.extend(rest[n] for n in range(ROUNDS - 1))
        out = local_call(finish_kernel, shape((PAIR, CELLS)), "svv", [taps_scratch])(flags, arrived, filters)
        outs.append(out)
        if r + 1 < ROUNDS:
            received = lax.ppermute(out, ("section", "chip", "core"), hop_pairs)

    both = jnp.stack(dpres)
    for_other = lax.ppermute(both[:, :OWN], "core", [(1, 0)])
    dpre_own = jnp.where(forward, for_other, both[:, OWN:])
    filter_grad = local_call(
        filter_kernel, shape((ROWS, CHANNELS), jnp.float32), "vvv", [pltpu.VMEM((ROWS, CELLS), jnp.bfloat16)]
    )(dpre_own, stored_first, stored_later)

    chain = jnp.stack(outs)
    swapped = lax.ppermute(jnp.where(forward, chain[:, OWN:], chain[:, :OWN]), "core", [(0, 1), (1, 0)])
    acts = jnp.where(forward, chain[:, :OWN], swapped)
    grads = jnp.where(forward, swapped, chain[:, OWN:])
    filter_grad = jnp.transpose(filter_grad.reshape(TAPS, OWN, CHANNELS), (1, 0, 2))
    return acts[None], grads[None], filter_grad[None]


def solution(mesh):
    sections = mesh.shape["section"]
    fine = Mesh(mesh.devices.reshape(sections, -1, 2), ("section", "chip", "core"))
    chan = ("chip", "core")
    return jax.shard_map(
        lambda *arrays: body(sections, *arrays),
        mesh=fine,
        in_specs=(
            P(None, chan, None),
            P("section", chan, None),
            P("section", chan, None),
            P("section", None, chan, None),
            P("section", chan, None, None),
            P(None, chan, None),
        ),
        out_specs=(
            P("section", None, chan, None),
            P("section", None, chan, None),
            P("section", chan, None, None),
        ),
        check_vma=False,
    )
```

time: 547 us -> 117 us (0.21)
  the two profiles are of different devices: /device:TPU:32 before, /device:TPU:385 now
where the time goes in v1:
time: 117 us
  starting transfers between devices  45.5 us (39%)
  blocking collectives  27 us (23%)
  waiting for transfers between devices  26.4 us (23%)
  Pallas kernels  13.6 us (12%)
  local copies, waits for them, and re-layouts  2.41 us (2%)
    all_to_all x2, blocking collectives, body(): arrived = lax.all_to_all(sent, 'chip', 0, 0)  22.5 us
    all_to_all x2, waiting for transfers between devices, gathered(): return lax.all_to_all(copies, axes, 0, 0)  14.1 us
    ppermute x3, starting transfers between devices, body(): received = lax.ppermute(out, ('section', 'chip', 'core'), hop_pairs)  13.3 us
    all_to_all x2, starting transfers between devices, gathered(): return lax.all_to_all(copies, axes, 0, 0)  11.9 us
    all_to_all x2, waiting for transfers between devices, body(): arrived = lax.all_to_all(sent, 'chip', 0, 0)  10.6 us
    ppermute x1, starting transfers between devices, body(): lax.ppermute(jnp.where(forward, chain[:, OWN:], chain[:, :OWN]), 'core',...  7.41 us
    all_to_all x2, starting transfers between devices, body(): arrived = lax.all_to_all(sent, 'chip', 0, 0)  7.2 us
    pallas_call x4, Pallas kernels, body(): local_call(lambda *refs: start_kernel(edge_slot, *refs), (shape((chips, P...  7.14 us
  transfers between devices with their start and end apart: 9, of which 6 were waited for; matrix products, arithmetic and copies ran while one was open for 0% of the time, Pallas kernels for 4%

profile of v1, /device:TPU:385, one launch (start us, length us, event | category | flops | bytes accessed | tf_op | source)
XLA Modules:
  0.0 116.6 jit_solution(10677812616383412758)
XLA Ops:
  0.6 0.7 slice_bitcast_fusion.8
  1.3 0.7 broadcast_in_dim.24
  2.1 0.0 slice-start
  2.1 0.0 slice-start.1
  2.1 7.9 %all-to-all-start = ((bf16[32,1,16,256]{3,2,1,0:T(8,128)(2,1)}), bf16[32,1,16,256]{3,2,1,0:T(8,128)(2,1)S(1)}, u32[]{:S(2)}, u32[]{:S(2)}) async-start(bf16[32,1,16,256]{3,2,1,0:T(8,128)(2,1)} %broadcast_in_dim.24), calls=%async_computation | async-start | bytes 524288 | tf_op jit(solution)/shard_map/all_to_all | solution.py:154
  10.0 0.0 copy-start
  10.0 0.0 copy-done.1
  10.0 0.0 copy-done.2
  10.0 0.0 copy-done.4
  10.1 0.0 copy-done.5
  10.1 0.0 slice-done
  10.1 0.0 slice-done.1
  10.1 2.0 %all_gather.6 = bf16[8,32,256]{2,1,0:T(8,128)(2,1)S(1)} all-gather(bf16[8,16,256]{2,1,0:T(8,128)(2,1)S(1)} %pad_maximum_fusion), channel_id=1, replica_groups=mesh['section'=16,'chip'=16,'core'=2] {'core'}, dimensions={1}, use_global_device_ids=true | all-gather | bytes 196608 | tf_op jit(solution)/shard_map/all_gather | solution.py:188
  12.2 0.0 copy-done
  12.2 2.4 %all_gather.7.filters.refs_4_ = bf16[864,512]{1,0:T(8,128)(2,1)S(1)} all-gather(bf16[432,512]{1,0:T(8,128)(2,1)S(1)} %bitcast.53), channel_id=1, replica_groups=mesh['section'=16,'chip'=16,'core'=2] {'core'}, dimensions={0}, use_global_device_ids=true | all-gather | bytes 1327104 | tf_op jit(solution)/shard_map/all_gather | solution.py:177
  14.6 0.1 pad_add_fusion.refs_0_.flags
  14.7 4.2 %all-to-all-done.stored.first = bf16[32,1,16,256]{3,2,1,0:T(8,128)(2,1)S(1)} async-done(((bf16[32,1,16,256]{3,2,1,0:T(8,128)(2,1)}), bf16[32,1,16,256]{3,2,1,0:T(8,128)(2,1)S(1)}, u32[]{:S(2)}, u32[]{:S(2)}) %all-to-all-start) | async-done | bytes 262176 | tf_op jit(solution)/shard_map/all_to_all | solution.py:154
  18.9 0.6 shard_map.85
  19.5 2.1 %shard_map.86 = (bf16[16,32,256]{2,1,0:T(8,128)(2,1)}, bf16[32,256]{1,0:T(8,128)(2,1)S(1)}) custom-call(s32[3]{0:T(128)S(1)} %pad_add_fusion.refs_0_.flags, bf16[32,256]{1,0:T(8,128)(2,1)S(1)} %get-tuple-element.27.refs_1_.refs_2_, bf16[32,256]{1,0:T(8,128)(2,1)S(1)} %get-tuple-element.27.refs_1_.refs_2_, f32[32,256]{1,0:T(8,128)S(1)} %bitcast.43, ...), custom_call_target="tpu_custom_call" | custom-call | tf_op jit(solution)/shard_map/pallas_call | solution.py:202
  21.7 3.7 %all-to-all-start.1 = ((bf16[16,32,256]{2,1,0:T(8,128)(2,1)}), bf16[16,32,256]{2,1,0:T(8,128)(2,1)S(1)}, u32[]{:S(2)}, u32[]{:S(2)}) async-start(bf16[16,32,256]{2,1,0:T(8,128)(2,1)} %get-tuple-element.11), calls=%async_computation.1 | async-start | bytes 524288 | tf_op jit(solution)/shard_map/all_to_all | solution.py:209
  25.4 8.9 %all-to-all-done.1.arrived = bf16[16,32,256]{2,1,0:T(8,128)(2,1)S(1)} async-done(((bf16[16,32,256]{2,1,0:T(8,128)(2,1)}), bf16[16,32,256]{2,1,0:T(8,128)(2,1)S(1)}, u32[]{:S(2)}, u32[]{:S(2)}) %all-to-all-start.1) | async-done | bytes 262176 | tf_op jit(solution)/shard_map/all_to_all | solution.py:209
  34.2 0.9 broadcast_in_dim.26
  35.1 4.0 %all-to-all-start.2 = ((bf16[32,3,16,256]{3,2,1,0:T(8,128)(2,1)}), bf16[32,3,16,256]{3,2,1,0:T(8,128)(2,1)S(1)}, u32[]{:S(2)}, u32[]{:S(2)}) async-start(bf16[32,3,16,256]{3,2,1,0:T(8,128)(2,1)} %broadcast_in_dim.26), calls=%async_computation.2 | async-start | bytes 1572864 | tf_op jit(solution)/shard_map/all_to_all | solution.py:154
  39.1 0.6 shard_map.87
  39.7 3.8 %collective-permute-start = (bf16[32,256]{1,0:T(8,128)(2,1)S(1)}, bf16[32,256]{1,0:T(8,128)(2,1)S(1)}, u32[]{:S(2)}, u32[]{:S(2)}) collective-permute-start(bf16[32,256]{1,0:T(8,128)(2,1)S(1)} %shard_map.87), channel_id=1, source_target_pairs={{0,32},{2,34},{4,36},{6,38},{8,40},{10,42},{12,44},{14,46},{16,48}... | collective-permute-start | bytes 49160 | tf_op jit(solution)/shard_map/ppermute | solution.py:216
  43.6 9.9 %all-to-all-done.2.stored.later = bf16[32,3,16,256]{3,2,1,0:T(8,128)(2,1)S(1)} async-done(((bf16[32,3,16,256]{3,2,1,0:T(8,128)(2,1)}), bf16[32,3,16,256]{3,2,1,0:T(8,128)(2,1)S(1)}, u32[]{:S(2)}, u32[]{:S(2)}) %all-to-all-start.2) | async-done | bytes 786464 | tf_op jit(solution)/shard_map/all_to_all | solution.py:154
  53.5 1.2 %shard_map.88 = f32[3,32,256]{2,1,0:T(8,128)S(1)} custom-call(bf16[864,512]{1,0:T(8,128)(2,1)S(1)} %all_gather.7.filters.refs_4_, bf16[32,3,16,256]{3,2,1,0:T(8,128)(2,1)S(1)} %all-to-all-done.2.stored.later), custom_call_target="tpu_custom_call" | custom-call | tf_op jit(solution)/shard_map/pallas_call | solution.py:193
  54.7 0.0 collective-permute-done.refs_1_
  54.7 1.4 %shard_map.89 = (bf16[16,32,256]{2,1,0:T(8,128)(2,1)S(1)}, bf16[32,256]{1,0:T(8,128)(2,1)S(1)}) custom-call(s32[3]{0:T(128)S(1)} %pad_add_fusion.refs_0_.flags, bf16[32,256]{1,0:T(8,128)(2,1)S(1)} %collective-permute-done.refs_1_, bf16[32,256]{1,0:T(8,128)(2,1)S(1)} %get-tuple-element.26.refs_2_, f32[32,256]{1,0:T(8,128)S(1)} %get-tuple-element.23.refs_3_, ...), custom_call_target="tpu_custom_call" | custom-call | tf_op jit(solution)/shard_map/pallas_call | solution.py:202
  56.1 12.3 %all_to_all.30.arrived = bf16[16,32,256]{2,1,0:T(8,128)(2,1)S(1)} all-to-all(bf16[16,32,256]{2,1,0:T(8,128)(2,1)S(1)} %get-tuple-element.12), channel_id=1, replica_groups=mesh['section'=16,'chip'=16,'core'=2] {'chip'}, dimensions={0} | all-to-all | bytes 524288 | tf_op jit(solution)/shard_map/all_to_all | solution.py:209
  68.4 0.6 shard_map.90
  69.0 3.9 %collective-permute-start.1 = (bf16[32,256]{1,0:T(8,128)(2,1)S(1)}, bf16[32,256]{1,0:T(8,128)(2,1)S(1)}, u32[]{:S(2)}, u32[]{:S(2)}) collective-permute-start(bf16[32,256]{1,0:T(8,128)(2,1)S(1)} %shard_map.90), channel_id=1, source_target_pairs={{0,32},{2,34},{4,36},{6,38},{8,40},{10,42},{12,44},{14,46},{16,48}... | collective-permute-start | bytes 49160 | tf_op jit(solution)/shard_map/ppermute | solution.py:216
  72.9 0.8 collective-permute-done.1.refs_1_
  73.7 1.4 %shard_map.91 = (bf16[16,32,256]{2,1,0:T(8,128)(2,1)S(1)}, bf16[32,256]{1,0:T(8,128)(2,1)S(1)}) custom-call(s32[3]{0:T(128)S(1)} %pad_add_fusion.refs_0_.flags, bf16[32,256]{1,0:T(8,128)(2,1)S(1)} %collective-permute-done.1.refs_1_, bf16[32,256]{1,0:T(8,128)(2,1)S(1)} %get-tuple-element.25.refs_2_, f32[32,256]{1,0:T(8,128)S(1)} %get-tuple-element.22.refs_3_, ...), custom_call_target="tpu_custom_call" | custom-call | tf_op jit(solution)/shard_map/pallas_call | solution.py:202
  75.2 10.2 %all_to_all.31.arrived = bf16[16,32,256]{2,1,0:T(8,128)(2,1)S(1)} all-to-all(bf16[16,32,256]{2,1,0:T(8,128)(2,1)S(1)} %get-tuple-element.13), channel_id=1, replica_groups=mesh['section'=16,'chip'=16,'core'=2] {'chip'}, dimensions={0} | all-to-all | bytes 524288 | tf_op jit(solution)/shard_map/all_to_all | solution.py:209
  85.4 0.6 shard_map.92
  86.0 5.6 %collective-permute-start.2 = (bf16[32,256]{1,0:T(8,128)(2,1)S(1)}, bf16[32,256]{1,0:T(8,128)(2,1)S(1)}, u32[]{:S(2)}, u32[]{:S(2)}) collective-permute-start(bf16[32,256]{1,0:T(8,128)(2,1)S(1)} %shard_map.92), channel_id=1, source_target_pairs={{0,32},{2,34},{4,36},{6,38},{8,40},{10,42},{12,44},{14,46},{16,48}... | collective-permute-start | bytes 49160 | tf_op jit(solution)/shard_map/ppermute | solution.py:216
  91.6 0.8 collective-permute-done.2.refs_1_
  92.4 2.1 %shard_map.93 = (bf16[16,32,256]{2,1,0:T(8,128)(2,1)}, bf16[32,256]{1,0:T(8,128)(2,1)S(1)}) custom-call(s32[3]{0:T(128)S(1)} %pad_add_fusion.refs_0_.flags, bf16[32,256]{1,0:T(8,128)(2,1)S(1)} %collective-permute-done.2.refs_1_, bf16[32,256]{1,0:T(8,128)(2,1)S(1)} %get-tuple-element.24.refs_2_, f32[32,256]{1,0:T(8,128)S(1)} %get-tuple-element.21.refs_3_, ...), custom_call_target="tpu_custom_call" | custom-call | tf_op jit(solution)/shard_map/pallas_call | solution.py:202
  94.6 3.5 %all-to-all-start.5 = ((bf16[16,32,256]{2,1,0:T(8,128)(2,1)}), bf16[16,32,256]{2,1,0:T(8,128)(2,1)S(1)}, u32[]{:S(2)}, u32[]{:S(2)}) async-start(bf16[16,32,256]{2,1,0:T(8,128)(2,1)} %get-tuple-element.14), calls=%async_computation.5 | async-start | bytes 524288 | tf_op jit(solution)/shard_map/all_to_all | solution.py:209
  98.2 5.7 %collective-permute-start.4 = (bf16[4,16,256]{2,1,0:T(8,128)(2,1)S(1)}, bf16[4,16,256]{2,1,0:T(8,128)(2,1)S(1)}, u32[]{:S(2)}, u32[]{:S(2)}) collective-permute-start(bf16[4,16,256]{2,1,0:T(8,128)(2,1)S(1)} %slice.90), channel_id=1, source_target_pairs={{1,0},{3,2},{5,4},{7,6},{9,8},{11,10},{13,12},{15,14},{17,16},{19,... | collective-permute-start | bytes 98312 | tf_op jit(solution)/shard_map/ppermute | solution.py:219
  103.8 1.8 %all-to-all-done.5.arrived = bf16[16,32,256]{2,1,0:T(8,128)(2,1)S(1)} async-done(((bf16[16,32,256]{2,1,0:T(8,128)(2,1)}), bf16[16,32,256]{2,1,0:T(8,128)(2,1)S(1)}, u32[]{:S(2)}, u32[]{:S(2)}) %all-to-all-start.5) | async-done | bytes 262176 | tf_op jit(solution)/shard_map/all_to_all | solution.py:209
  105.6 0.6 shard_map.94
  106.3 7.4 %collective-permute-start.3 = (bf16[4,16,256]{2,1,0:T(8,128)(2,1)S(1)}, bf16[4,16,256]{2,1,0:T(8,128)(2,1)S(1)}, u32[]{:S(2)}, u32[]{:S(2)}) collective-permute-start(bf16[4,16,256]{2,1,0:T(8,128)(2,1)S(1)} %broadcast_select_fusion), channel_id=1, source_target_pairs={{0,1},{1,0},{2,3},{3,2},{4,5},{5,4},{6,7},{7,6},{8,9},{9,8},{10,11... | collective-permute-start | bytes 98312 | tf_op jit(solution)/shard_map/ppermute | solution.py:226
  113.7 0.0 collective-permute-done.4
  113.7 2.2 %shard_map.95 = f32[432,512]{1,0:T(8,128)} custom-call(bf16[4,16,256]{2,1,0:T(8,128)(2,1)S(1)} %slice_select_fusion.1.dpre, bf16[32,1,16,256]{3,2,1,0:T(8,128)(2,1)S(1)} %all-to-all-done.stored.first, bf16[32,3,16,256]{3,2,1,0:T(8,128)(2,1)S(1)} %all-to-all-done.2.stored.later), custom_call_target="tpu_custom_call" | custom-call | tf_op jit(solution)/shard_map/pallas_call | solution.py:221
  115.9 0.0 collective-permute-done.3
  115.9 0.6 select_bitcast_fusion
  (17 shorter events, 0.1 us)
Async XLA Ops:
  2.1 8.0 %copy-start.1 = (bf16[4,16,256]{2,1,0:T(8,128)(2,1)S(1)}, bf16[4,16,256]{2,1,0:T(8,128)(2,1)}, u32[]{:S(2)}) copy-start(bf16[4,16,256]{2,1,0:T(8,128)(2,1)} %param.6) | copy-start | bytes 98308
  2.1 8.0 %copy-start.2 = (bf16[4,16,256]{2,1,0:T(8,128)(2,1)S(1)}, bf16[4,16,256]{2,1,0:T(8,128)(2,1)}, u32[]{:S(2)}) copy-start(bf16[4,16,256]{2,1,0:T(8,128)(2,1)} %param.11) | copy-start | bytes 98308
  2.1 8.0 %copy-start.4 = (bf16[1,16,256]{2,1,0:T(8,128)(2,1)S(1)}, bf16[1,16,256]{2,1,0:T(8,128)(2,1)}, u32[]{:S(2)}) copy-start(bf16[1,16,256]{2,1,0:T(8,128)(2,1)} %param.8) | copy-start | bytes 24580
  2.1 8.0 %copy-start.5 = (bf16[1,16,256]{2,1,0:T(8,128)(2,1)S(1)}, bf16[1,16,256]{2,1,0:T(8,128)(2,1)}, u32[]{:S(2)}) copy-start(bf16[1,16,256]{2,1,0:T(8,128)(2,1)} %param.7) | copy-start | bytes 24580
  2.1 8.0 %slice-start = ((bf16[4,16,256]{2,1,0:T(8,128)(2,1)}), bf16[3,16,256]{2,1,0:T(8,128)(2,1)S(1)}, s32[]{:S(2)}) async-start(bf16[4,16,256]{2,1,0:T(8,128)(2,1)} %param.6), calls=%async_computation.6 | async-start | bytes 49152 | tf_op jit(solution)/shard_map/slice | solution.py:183
  2.1 8.0 %slice-start.1 = ((bf16[4,16,256]{2,1,0:T(8,128)(2,1)}), bf16[3,16,256]{2,1,0:T(8,128)(2,1)S(1)}, s32[]{:S(2)}) async-start(bf16[4,16,256]{2,1,0:T(8,128)(2,1)} %param.11), calls=%async_computation.7 | async-start | bytes 49152 | tf_op jit(solution)/shard_map/slice | solution.py:185
  2.1 16.8 %all-to-all-start = ((bf16[32,1,16,256]{3,2,1,0:T(8,128)(2,1)}), bf16[32,1,16,256]{3,2,1,0:T(8,128)(2,1)S(1)}, u32[]{:S(2)}, u32[]{:S(2)}) async-start(bf16[32,1,16,256]{3,2,1,0:T(8,128)(2,1)} %broadcast_in_dim.24), calls=%async_computation | async-start | bytes 524288 | tf_op jit(solution)/shard_map/all_to_all | solution.py:154
  10.0 2.2 %copy-start = (bf16[1,16,27,512]{3,1,2,0:T(8,128)(2,1)S(1)}, bf16[1,16,27,512]{3,1,2,0:T(8,128)(2,1)}, u32[]{:S(2)}) copy-start(bf16[1,16,27,512]{3,1,2,0:T(8,128)(2,1)} %param.10) | copy-start | bytes 1327108
  21.7 3.7 %copy-start.3 = (bf16[1,4,16,256]{3,2,1,0:T(8,128)(2,1)S(1)}, bf16[1,4,16,256]{3,2,1,0:T(8,128)(2,1)}, u32[]{:S(2)}) copy-start(bf16[1,4,16,256]{3,2,1,0:T(8,128)(2,1)} %param.9) | copy-start | bytes 98308
  21.7 12.6 %all-to-all-start.1 = ((bf16[16,32,256]{2,1,0:T(8,128)(2,1)}), bf16[16,32,256]{2,1,0:T(8,128)(2,1)S(1)}, u32[]{:S(2)}, u32[]{:S(2)}) async-start(bf16[16,32,256]{2,1,0:T(8,128)(2,1)} %get-tuple-element.11), calls=%async_computation.1 | async-start | bytes 524288 | tf_op jit(solution)/shard_map/all_to_all | solution.py:209
  35.1 18.3 %all-to-all-start.2 = ((bf16[32,3,16,256]{3,2,1,0:T(8,128)(2,1)}), bf16[32,3,16,256]{3,2,1,0:T(8,128)(2,1)S(1)}, u32[]{:S(2)}, u32[]{:S(2)}) async-start(bf16[32,3,16,256]{3,2,1,0:T(8,128)(2,1)} %broadcast_in_dim.26), calls=%async_computation.2 | async-start | bytes 1572864 | tf_op jit(solution)/shard_map/all_to_all | solution.py:154
  39.7 15.0 %collective-permute-start = (bf16[32,256]{1,0:T(8,128)(2,1)S(1)}, bf16[32,256]{1,0:T(8,128)(2,1)S(1)}, u32[]{:S(2)}, u32[]{:S(2)}) collective-permute-start(bf16[32,256]{1,0:T(8,128)(2,1)S(1)} %shard_map.87), channel_id=1, source_target_pairs={{0,32},{2,34},{4,36},{6,38},{8,40},{10,42},{12,44},{14,46},{16,48}... | collective-permute-start | bytes 49160 | tf_op jit(solution)/shard_map/ppermute | solution.py:216
  69.0 4.7 %collective-permute-start.1 = (bf16[32,256]{1,0:T(8,128)(2,1)S(1)}, bf16[32,256]{1,0:T(8,128)(2,1)S(1)}, u32[]{:S(2)}, u32[]{:S(2)}) collective-permute-start(bf16[32,256]{1,0:T(8,128)(2,1)S(1)} %shard_map.90), channel_id=1, source_target_pairs={{0,32},{2,34},{4,36},{6,38},{8,40},{10,42},{12,44},{14,46},{16,48}... | collective-permute-start | bytes 49160 | tf_op jit(solution)/shard_map/ppermute | solution.py:216
  86.0 6.5 %collective-permute-start.2 = (bf16[32,256]{1,0:T(8,128)(2,1)S(1)}, bf16[32,256]{1,0:T(8,128)(2,1)S(1)}, u32[]{:S(2)}, u32[]{:S(2)}) collective-permute-start(bf16[32,256]{1,0:T(8,128)(2,1)S(1)} %shard_map.92), channel_id=1, source_target_pairs={{0,32},{2,34},{4,36},{6,38},{8,40},{10,42},{12,44},{14,46},{16,48}... | collective-permute-start | bytes 49160 | tf_op jit(solution)/shard_map/ppermute | solution.py:216
  94.6 11.0 %all-to-all-start.5 = ((bf16[16,32,256]{2,1,0:T(8,128)(2,1)}), bf16[16,32,256]{2,1,0:T(8,128)(2,1)S(1)}, u32[]{:S(2)}, u32[]{:S(2)}) async-start(bf16[16,32,256]{2,1,0:T(8,128)(2,1)} %get-tuple-element.14), calls=%async_computation.5 | async-start | bytes 524288 | tf_op jit(solution)/shard_map/all_to_all | solution.py:209
  98.2 15.5 %collective-permute-start.4 = (bf16[4,16,256]{2,1,0:T(8,128)(2,1)S(1)}, bf16[4,16,256]{2,1,0:T(8,128)(2,1)S(1)}, u32[]{:S(2)}, u32[]{:S(2)}) collective-permute-start(bf16[4,16,256]{2,1,0:T(8,128)(2,1)S(1)} %slice.90), channel_id=1, source_target_pairs={{1,0},{3,2},{5,4},{7,6},{9,8},{11,10},{13,12},{15,14},{17,16},{19,... | collective-permute-start | bytes 98312 | tf_op jit(solution)/shard_map/ppermute | solution.py:219
  106.3 9.7 %collective-permute-start.3 = (bf16[4,16,256]{2,1,0:T(8,128)(2,1)S(1)}, bf16[4,16,256]{2,1,0:T(8,128)(2,1)S(1)}, u32[]{:S(2)}, u32[]{:S(2)}) collective-permute-start(bf16[4,16,256]{2,1,0:T(8,128)(2,1)S(1)} %broadcast_select_fusion), channel_id=1, source_target_pairs={{0,1},{1,0},{2,3},{3,2},{4,5},{5,4},{6,7},{7,6},{8,9},{9,8},{10,11... | collective-permute-start | bytes 98312 | tf_op jit(solution)/shard_map/ppermute | solution.py:226

commit v2 on v1

--- a/solution.py
+++ b/solution.py
@@ -60,15 +60,22 @@
                 spread[start : start + OWN, :] = moved(line, where, 2, 1 - l).astype(jnp.bfloat16)
 
 
-def slope_kernel(filters, stored, slope, taps):
+def slope_of(filters, whole, taps, where):
+    taps[...] = jnp.dot(filters[...], whole.reshape(CHANNELS, CELLS), preferred_element_type=jnp.float32)
+    parts = []
+    for c in range(2):
+        pre = tap_total(taps, ROWS * c, where)
+        logistic = 1.0 / (1.0 + jnp.exp(-pre))
+        parts.append(logistic * (1.0 + pre * (1.0 - logistic)))
+    return parts
+
+
+def slope_kernel(filters, near, far, second, third, fourth, taps):
     where = coordinates(OWN)
-    for r in range(stored.shape[1]):
-        whole = stored[:, r].reshape(CHANNELS, CELLS)
-        taps[...] = jnp.dot(filters[...], whole, preferred_element_type=jnp.float32)
+    for stored, r, slope in ((near, 1, second), (far, 0, third), (far, 1, fourth)):
+        parts = slope_of(filters, stored[:, r], taps, where)
         for c in range(2):
-            pre = tap_total(taps, ROWS * c, where)
-            logistic = 1.0 / (1.0 + jnp.exp(-pre))
-            slope[r, OWN * c : OWN * (c + 1), :] = logistic * (1.0 + pre * (1.0 - logistic))
+            slope[OWN * c : OWN * (c + 1), :] = parts[c]
 
 
 def finish_kernel(flags, arrived, filters, out, taps):
@@ -89,43 +96,66 @@
         out[...] = total.astype(jnp.bfloat16)
 
 
-def start_kernel(edge_slot, flags, received, outside, slope, filters, sent, dpre, spread):
-    take = flags[edge_slot] != 0
+def send_copies(value, sent):
+    for p in range(sent.shape[0]):
+        sent[p] = value
+
+
+def send_parts(rounded, filters, sent, spread, where):
+    for c in range(2):
+        wide = rounded[OWN * c : OWN * (c + 1), :].astype(jnp.float32)
+        spread_into(spread, ROWS * c, wide, where)
+    part = lax.dot_general(
+        filters[...], spread[...], (((0,), (0,)), ((), ())), preferred_element_type=jnp.float32
+    )
+    sent[...] = part.astype(jnp.bfloat16).reshape(sent.shape)
+
+
+def first_kernel(flags, outside, near, filters, sent, dpre, spread, taps):
+    @pl.when(flags[0] == 0)
+    def _():
+        dpre[...] = outside[...]
+        send_copies(outside[...], sent)
+
+    @pl.when(flags[0] != 0)
+    def _():
+        where = coordinates(OWN)
+        parts = slope_of(filters, near[:, 0], taps, where)
+        for c in range(2):
+            rows = slice(OWN * c, OWN * (c + 1))
+            dpre[rows, :] = (outside[rows, :].astype(jnp.float32) * parts[c]).astype(jnp.bfloat16)
+        send_parts(dpre, filters, sent, spread, where)
+
+
+def start_kernel(flags, received, outside, slope, filters, sent, dpre, spread):
+    take = flags[1] != 0
     value = jnp.where(take, outside[...].astype(jnp.float32), received[...].astype(jnp.float32))
 
     @pl.when(flags[0] == 0)
     def _():
         copy = value.astype(jnp.bfloat16)
         dpre[...] = copy
-        for p in range(sent.shape[0]):
-            sent[p] = copy
+        send_copies(copy, sent)
 
     @pl.when(flags[0] != 0)
     def _():
-        where = coordinates(OWN)
-        rounded = (value * slope[...]).astype(jnp.bfloat16)
-        dpre[...] = rounded
-        wide = rounded.astype(jnp.float32)
-        for c in range(2):
-            spread_into(spread, ROWS * c, wide[OWN * c : OWN * (c + 1), :], where)
-        part = lax.dot_general(
-            filters[...], spread[...], (((0,), (0,)), ((), ())), preferred_element_type=jnp.float32
-        )
-        sent[...] = part.astype(jnp.bfloat16).reshape(sent.shape)
-
-
-def filter_kernel(dpre, first, later, out, spread):
+        dpre[...] = (value * slope[...]).astype(jnp.bfloat16)
+        send_parts(dpre, filters, sent, spread, coordinates(OWN))
+
+
+def filter_kernel(flags, dpre, near, far, out, spread):
     where = coordinates(OWN)
-    for r in range(ROUNDS):
-        spread_into(spread, 0, dpre[r].astype(jnp.float32), where)
-        stored = first[:, 0] if r == 0 else later[:, r - 1]
+    near_base = 2 * (1 - flags[0])
+    far_base = 2 * flags[0]
+    for n, (stored, r, base) in enumerate(((near, 0, near_base), (near, 1, near_base), (far, 0, far_base), (far, 1, far_base))):
+        spread_into(spread, 0, dpre[base + r].astype(jnp.float32), where)
         term = lax.dot_general(
             spread[...],
-            stored.reshape(CHANNELS, CELLS),
+            stored[:, r].reshape(CHANNELS, CELLS),
             (((1,), (1,)), ((), ())),
             preferred_element_type=jnp.float32,
         )
-        if r == 0:
+        if n == 0:
             out[...] = term
         else:
             out[...] += term
@@ -149,18 +179,13 @@
     return jax.ShapeDtypeStruct(dims, dtype)
 
 
-def gathered(block, axes, count):
-    copies = jnp.broadcast_to(block[None], (count,) + block.shape)
-    return lax.all_to_all(copies, axes, 0, 0)
-
-
 def body(sections, inputs, front, back, saved, weights, cotangent):
     chips = CHANNELS // PAIR
     section = lax.axis_index("section")
     core = lax.axis_index("core")
     forward = core == 0
     at_edge = jnp.where(forward, section == 0, section == sections - 1)
-    flags = jnp.stack([core, at_edge.astype(jnp.int32), jnp.int32(1)]).astype(jnp.int32)
+    flags = jnp.stack([core, at_edge.astype(jnp.int32)]).astype(jnp.int32)
     hop_pairs = []
     for s in range(sections):
         for p in range(chips):
@@ -170,9 +195,10 @@
             if s > 0:
                 hop_pairs.append((here + 1, here + 1 - 2 * chips))
 
-    everyone = ("chip", "core")
-    stored_first = gathered(saved[0, :1], everyone, 2 * chips)
-    stored_later = gathered(saved[0, 1:], everyone, 2 * chips)
+    stored = lax.all_gather(saved[0], "core", axis=1, tiled=True)
+    stored = jnp.where(forward, stored[2:], stored[:2])
+    near = lax.all_to_all(jnp.broadcast_to(stored[None], (chips,) + stored.shape), "chip", 0, 0)
+    far = lax.ppermute(near, "core", [(0, 1), (1, 0)])
 
     filters = lax.all_gather(
         jnp.transpose(weights[0], (1, 0, 2)).reshape(ROWS, CHANNELS), "core", axis=0, tiled=True
@@ -190,37 +216,37 @@
 
     taps_scratch = pltpu.VMEM((2 * ROWS, CELLS), jnp.float32)
     spread_scratch = pltpu.VMEM((2 * ROWS, CELLS), jnp.bfloat16)
-    slope_of = lambda stored, n: local_call(
-        slope_kernel, shape((n, PAIR, CELLS), jnp.float32), "vv", [taps_scratch]
-    )(filters, stored)
-    slopes = [slope_of(stored_first, 1)[0]]
+    to_send = (shape((chips, PAIR, CELLS)), shape((PAIR, CELLS)))
 
     outs, dpres = [], []
-    received = outside[0]
+    sent, dpre = local_call(first_kernel, to_send, "svvv", [spread_scratch, taps_scratch])(
+        flags, outside[0], near, filters
+    )
     for r in range(ROUNDS):
-        edge_slot = 2 if r == 0 else 1
-        sent, dpre = local_call(
-            lambda *refs: start_kernel(edge_slot, *refs),
-            (shape((chips, PAIR, CELLS)), shape((PAIR, CELLS))),
-            "svvvv",
-            [spread_scratch],
-        )(flags, received, outside[r], slopes[r], filters)
         dpres.append(dpre)
         arrived = lax.all_to_all(sent, "chip", 0, 0)
         if r == 0:
-            rest = slope_of(stored_later, ROUNDS - 1)
-            slopes.extend(rest[n] for n in range(ROUNDS - 1))
+            slopes = local_call(
+                slope_kernel, (shape((PAIR, CELLS), jnp.float32),) * 3, "vvv", [taps_scratch]
+            )(filters, near, far)
+        if r + 1 == ROUNDS:
+            both = jnp.stack(dpres)
+            for_other = lax.ppermute(both[:, :OWN], "core", [(1, 0)])
+            dpre_own = jnp.where(forward, for_other, both[:, OWN:])
+            filter_grad = local_call(
+                filter_kernel,
+                shape((ROWS, CHANNELS), jnp.float32),
+                "svvv",
+                [pltpu.VMEM((ROWS, CELLS), jnp.bfloat16)],
+            )(flags, dpre_own, near, far)
+            arrived, filter_grad = lax.optimization_barrier((arrived, filter_grad))
         out = local_call(finish_kernel, shape((PAIR, CELLS)), "svv", [taps_scratch])(flags, arrived, filters)
         outs.append(out)
         if r + 1 < ROUNDS:
             received = lax.ppermute(out, ("section", "chip", "core"), hop_pairs)
-
-    both = jnp.stack(dpres)
-    for_other = lax.ppermute(both[:, :OWN], "core", [(1, 0)])
-    dpre_own = jnp.where(forward, for_other, both[:, OWN:])
-    filter_grad = local_call(
-        filter_kernel, shape((ROWS, CHANNELS), jnp.float32), "vvv", [pltpu.VMEM((ROWS, CELLS), jnp.bfloat16)]
-    )(dpre_own, stored_first, stored_later)
+            sent, dpre = local_call(start_kernel, to_send, "svvvv", [spread_scratch])(
+                flags, received, outside[r + 1], slopes[r], filters
+            )
 
     chain = jnp.stack(outs)
     swapped = lax.ppermute(jnp.where(forward, chain[:, OWN:], chain[:, :OWN]), "core", [(0, 1), (1, 0)])

time: 117 us -> 108 us (0.923)
  the two profiles are of different devices: /device:TPU:385 before, /device:TPU:257 now
where the time goes in v2:
time: 108 us; the launch traced here: 107 us
  blocking collectives  38.3 us (35%)
  starting transfers between devices  37 us (34%)
  waiting for transfers between devices  15.9 us (15%)
  Pallas kernels  13.5 us (12%)
    all_to_all x3, blocking collectives, body(): arrived = lax.all_to_all(sent, 'chip', 0, 0)  31.1 us
    ppermute x3, starting transfers between devices, body(): received = lax.ppermute(out, ('section', 'chip', 'core'), hop_pairs)  10.7 us
    ppermute x1, starting transfers between devices, body(): for_other = lax.ppermute(both[:, :OWN], 'core', [(1, 0)])  9.42 us
    all_to_all x1, starting transfers between devices, body(): lax.all_to_all(jnp.broadcast_to(stored[None], (chips,) + stored.shape), '...  6.9 us
    all_to_all x1, waiting for transfers between devices, body(): arrived = lax.all_to_all(sent, 'chip', 0, 0)  6.09 us
    all_to_all x1, waiting for transfers between devices, body(): lax.all_to_all(jnp.broadcast_to(stored[None], (chips,) + stored.shape), '...  6 us
    pallas_call x3, Pallas kernels, body(): local_call(start_kernel, to_send, 'svvvv', [spread_scratch])  4.87 us
    ppermute x1, starting transfers between devices, body(): far = lax.ppermute(near, 'core', [(0, 1), (1, 0)])  3.64 us
  transfers between devices with their start and end apart: 8, of which 6 were waited for; matrix products, arithmetic and copies ran while one was open for 0% of the time, Pallas kernels for 6%

profile of v2, /device:TPU:257, one launch (start us, length us, event | category | flops | bytes accessed | tf_op | source)
XLA Modules:
  0.0 107.4 jit_solution(2952050048649124228)
XLA Ops:
  0.6 2.6 %all-gather = bf16[1,4,32,256]{3,2,1,0:T(8,128)(2,1)S(1)} all-gather(bf16[1,4,16,256]{3,2,1,0:T(8,128)(2,1)} %param.9), channel_id=2, replica_groups=mesh['section'=16,'chip'=16,'core'=2] {'core'}, dimensions={2}, use_global_device_ids=true | all-gather | bytes 98304 | tf_op jit(solution)/shard_map/all_gather | solution.py:198
  3.3 0.9 broadcast_in_dim.15
  4.1 0.0 copy-start.3
  4.1 0.0 copy-start.2
  4.1 0.0 copy-start.4
  4.1 0.0 slice-start
  4.1 0.0 slice-start.1
  4.1 6.9 %all-to-all-start = ((bf16[16,2,32,256]{3,2,1,0:T(8,128)(2,1)}), bf16[16,2,32,256]{3,2,1,0:T(8,128)(2,1)S(1)}, u32[]{:S(2)}, u32[]{:S(2)}) async-start(bf16[16,2,32,256]{3,2,1,0:T(8,128)(2,1)} %broadcast_in_dim.15), calls=%async_computation | async-start | bytes 1048576 | tf_op jit(solution)/shard_map/all_to_all | solution.py:200
  11.0 0.0 copy-start
  11.1 0.0 copy-done.1
  11.1 0.0 copy-done.3
  11.1 0.0 copy-done.2
  11.1 0.0 copy-done.4
  11.1 0.0 slice-done
  11.1 0.0 slice-done.1
  11.2 2.2 %all_gather.9 = bf16[8,32,256]{2,1,0:T(8,128)(2,1)S(1)} all-gather(bf16[8,16,256]{2,1,0:T(8,128)(2,1)S(1)} %pad_maximum_fusion), channel_id=1, replica_groups=mesh['section'=16,'chip'=16,'core'=2] {'core'}, dimensions={1}, use_global_device_ids=true | all-gather | bytes 196608 | tf_op jit(solution)/shard_map/all_gather | solution.py:214
  13.4 0.0 copy-done
  13.4 2.4 %all_gather.11.filters = bf16[864,512]{1,0:T(8,128)(2,1)S(1)} all-gather(bf16[432,512]{1,0:T(8,128)(2,1)S(1)} %bitcast.43), channel_id=1, replica_groups=mesh['section'=16,'chip'=16,'core'=2] {'core'}, dimensions={0}, use_global_device_ids=true | all-gather | bytes 1327104 | tf_op jit(solution)/shard_map/all_gather | solution.py:203
  15.8 6.0 %all-to-all-done.near = bf16[16,2,32,256]{3,2,1,0:T(8,128)(2,1)S(1)} async-done(((bf16[16,2,32,256]{3,2,1,0:T(8,128)(2,1)}), bf16[16,2,32,256]{3,2,1,0:T(8,128)(2,1)S(1)}, u32[]{:S(2)}, u32[]{:S(2)}) %all-to-all-start) | async-done | bytes 524320 | tf_op jit(solution)/shard_map/all_to_all | solution.py:200
  21.8 3.6 %collective-permute-start.1 = (bf16[16,2,32,256]{3,2,1,0:T(8,128)(2,1)S(1)}, bf16[16,2,32,256]{3,2,1,0:T(8,128)(2,1)S(1)}, u32[]{:S(2)}, u32[]{:S(2)}) collective-permute-start(bf16[16,2,32,256]{3,2,1,0:T(8,128)(2,1)S(1)} %all-to-all-done.near), channel_id=1, source_target_pairs={{0,1},{1,0},{2,3},{3,2},{4,5},{5,4},{6,7},{7,6},{8,9},{9,8},{10,11... | collective-permute-start | bytes 1572872 | tf_op jit(solution)/shard_map/ppermute | solution.py:201
  25.4 0.1 pad_add_fusion.flags
  25.5 2.3 %shard_map.85 = (bf16[16,32,256]{2,1,0:T(8,128)(2,1)S(1)}, bf16[32,256]{1,0:T(8,128)(2,1)S(1)}) custom-call(s32[2]{0:T(128)S(1)} %pad_add_fusion.flags, bf16[32,256]{1,0:T(8,128)(2,1)S(1)} %get-tuple-element.34.outside, bf16[16,2,32,256]{3,2,1,0:T(8,128)(2,1)S(1)} %all-to-all-done.near, bf16[864,512]{1,0:T(8,128)(2,1)S(1)} %all_gather.11.filters), custom_call_target="tpu_custom_call" | custom-call | tf_op jit(solution)/shard_map/pallas_call | solution.py:222
  27.8 10.7 %all_to_all.25.arrived = bf16[16,32,256]{2,1,0:T(8,128)(2,1)S(1)} all-to-all(bf16[16,32,256]{2,1,0:T(8,128)(2,1)S(1)} %get-tuple-element.16), channel_id=1, replica_groups=mesh['section'=16,'chip'=16,'core'=2] {'chip'}, dimensions={0} | all-to-all | bytes 524288 | tf_op jit(solution)/shard_map/all_to_all | solution.py:227
  38.5 0.6 shard_map.86
  39.1 1.9 %collective-permute-start = (bf16[32,256]{1,0:T(8,128)(2,1)S(1)}, bf16[32,256]{1,0:T(8,128)(2,1)S(1)}, u32[]{:S(2)}, u32[]{:S(2)}) collective-permute-start(bf16[32,256]{1,0:T(8,128)(2,1)S(1)} %shard_map.86), channel_id=1, source_target_pairs={{0,32},{2,34},{4,36},{6,38},{8,40},{10,42},{12,44},{14,46},{16,48}... | collective-permute-start | bytes 49160 | tf_op jit(solution)/shard_map/ppermute | solution.py:246
  41.0 0.0 collective-permute-done.1.far
  41.0 1.2 %shard_map.87 = (f32[32,256]{1,0:T(8,128)S(1)}, f32[32,256]{1,0:T(8,128)S(1)}, f32[32,256]{1,0:T(8,128)S(1)}) custom-call(bf16[864,512]{1,0:T(8,128)(2,1)S(1)} %all_gather.11.filters, bf16[16,2,32,256]{3,2,1,0:T(8,128)(2,1)S(1)} %all-to-all-done.near, bf16[16,2,32,256]{3,2,1,0:T(8,128)(2,1)S(1)} %collective-permute-done.1.far), custom_call_target="tpu_custom_call" | custom-call | tf_op jit(solution)/shard_map/pallas_call | solution.py:229
  42.2 1.3 %collective-permute-done.received = bf16[32,256]{1,0:T(8,128)(2,1)S(1)} collective-permute-done((bf16[32,256]{1,0:T(8,128)(2,1)S(1)}, bf16[32,256]{1,0:T(8,128)(2,1)S(1)}, u32[]{:S(2)}, u32[]{:S(2)}) %collective-permute-start) | collective-permute-done | bytes 16416 | tf_op jit(solution)/shard_map/ppermute | solution.py:246
  43.5 1.4 %shard_map.88 = (bf16[16,32,256]{2,1,0:T(8,128)(2,1)S(1)}, bf16[32,256]{1,0:T(8,128)(2,1)S(1)}) custom-call(s32[2]{0:T(128)S(1)} %pad_add_fusion.flags, bf16[32,256]{1,0:T(8,128)(2,1)S(1)} %collective-permute-done.received, bf16[32,256]{1,0:T(8,128)(2,1)S(1)} %get-tuple-element.33.outside, f32[32,256]{1,0:T(8,128)S(1)} %get-tuple-element.17.slope, ...), custom_call_target="tpu_custom_call" | custom-call | tf_op jit(solution)/shard_map/pallas_call | solution.py:247
  44.9 10.2 %all_to_all.26.arrived = bf16[16,32,256]{2,1,0:T(8,128)(2,1)S(1)} all-to-all(bf16[16,32,256]{2,1,0:T(8,128)(2,1)S(1)} %get-tuple-element.18), channel_id=1, replica_groups=mesh['section'=16,'chip'=16,'core'=2] {'chip'}, dimensions={0} | all-to-all | bytes 524288 | tf_op jit(solution)/shard_map/all_to_all | solution.py:227
  55.1 0.6 shard_map.89
  55.7 3.9 %collective-permute-start.2 = (bf16[32,256]{1,0:T(8,128)(2,1)S(1)}, bf16[32,256]{1,0:T(8,128)(2,1)S(1)}, u32[]{:S(2)}, u32[]{:S(2)}) collective-permute-start(bf16[32,256]{1,0:T(8,128)(2,1)S(1)} %shard_map.89), channel_id=1, source_target_pairs={{0,32},{2,34},{4,36},{6,38},{8,40},{10,42},{12,44},{14,46},{16,48}... | collective-permute-start | bytes 49160 | tf_op jit(solution)/shard_map/ppermute | solution.py:246
  59.6 0.8 collective-permute-done.2.received
  60.4 1.4 %shard_map.90 = (bf16[16,32,256]{2,1,0:T(8,128)(2,1)S(1)}, bf16[32,256]{1,0:T(8,128)(2,1)S(1)}) custom-call(s32[2]{0:T(128)S(1)} %pad_add_fusion.flags, bf16[32,256]{1,0:T(8,128)(2,1)S(1)} %collective-permute-done.2.received, bf16[32,256]{1,0:T(8,128)(2,1)S(1)} %get-tuple-element.32.outside, f32[32,256]{1,0:T(8,128)S(1)} %get-tuple-element.19.slope, ...), custom_call_target="tpu_custom_call" | custom-call | tf_op jit(solution)/shard_map/pallas_call | solution.py:247
  61.8 10.3 %all_to_all.27.arrived = bf16[16,32,256]{2,1,0:T(8,128)(2,1)S(1)} all-to-all(bf16[16,32,256]{2,1,0:T(8,128)(2,1)S(1)} %get-tuple-element.20), channel_id=1, replica_groups=mesh['section'=16,'chip'=16,'core'=2] {'chip'}, dimensions={0} | all-to-all | bytes 524288 | tf_op jit(solution)/shard_map/all_to_all | solution.py:227
  72.1 0.6 shard_map.91
  72.7 4.8 %collective-permute-start.3 = (bf16[32,256]{1,0:T(8,128)(2,1)S(1)}, bf16[32,256]{1,0:T(8,128)(2,1)S(1)}, u32[]{:S(2)}, u32[]{:S(2)}) collective-permute-start(bf16[32,256]{1,0:T(8,128)(2,1)S(1)} %shard_map.91), channel_id=1, source_target_pairs={{0,32},{2,34},{4,36},{6,38},{8,40},{10,42},{12,44},{14,46},{16,48}... | collective-permute-start | bytes 49160 | tf_op jit(solution)/shard_map/ppermute | solution.py:246
  77.5 0.8 collective-permute-done.3.received
  78.4 2.1 %shard_map.92 = (bf16[16,32,256]{2,1,0:T(8,128)(2,1)}, bf16[32,256]{1,0:T(8,128)(2,1)S(1)}) custom-call(s32[2]{0:T(128)S(1)} %pad_add_fusion.flags, bf16[32,256]{1,0:T(8,128)(2,1)S(1)} %collective-permute-done.3.received, bf16[32,256]{1,0:T(8,128)(2,1)S(1)} %get-tuple-element.31.outside, f32[32,256]{1,0:T(8,128)S(1)} %get-tuple-element.21.slope, ...), custom_call_target="tpu_custom_call" | custom-call | tf_op jit(solution)/shard_map/pallas_call | solution.py:247
  80.5 9.4 %collective-permute-start.4 = (bf16[4,16,256]{2,1,0:T(8,128)(2,1)S(1)}, bf16[4,16,256]{2,1,0:T(8,128)(2,1)S(1)}, u32[]{:S(2)}, u32[]{:S(2)}) collective-permute-start(bf16[4,16,256]{2,1,0:T(8,128)(2,1)S(1)} %slice.76), channel_id=1, source_target_pairs={{1,0},{3,2},{5,4},{7,6},{9,8},{11,10},{13,12},{15,14},{17,16},{19,... | collective-permute-start | bytes 98312 | tf_op jit(solution)/shard_map/ppermute | solution.py:234
  89.9 3.5 %all-to-all-start.4 = ((bf16[16,32,256]{2,1,0:T(8,128)(2,1)}), bf16[16,32,256]{2,1,0:T(8,128)(2,1)S(1)}, u32[]{:S(2)}, u32[]{:S(2)}) async-start(bf16[16,32,256]{2,1,0:T(8,128)(2,1)} %get-tuple-element.22), calls=%async_computation.4 | async-start | bytes 524288 | tf_op jit(solution)/shard_map/all_to_all | solution.py:227
  93.5 0.0 collective-permute-done.4
  93.5 2.8 %shard_map.93 = f32[432,512]{1,0:T(8,128)} custom-call(s32[2]{0:T(128)S(1)} %pad_add_fusion.flags, bf16[4,16,256]{2,1,0:T(8,128)(2,1)S(1)} %slice_select_fusion.1.dpre, bf16[16,2,32,256]{3,2,1,0:T(8,128)(2,1)S(1)} %all-to-all-done.near, bf16[16,2,32,256]{3,2,1,0:T(8,128)(2,1)S(1)} %collective-permute-done.1.far), custom_call_target="tpu_custom_call" | custom-call | tf_op jit(solution)/shard_map/pallas_call | solution.py:236
  96.3 6.1 %all-to-all-done.4.arrived = bf16[16,32,256]{2,1,0:T(8,128)(2,1)S(1)} async-done(((bf16[16,32,256]{2,1,0:T(8,128)(2,1)}), bf16[16,32,256]{2,1,0:T(8,128)(2,1)S(1)}, u32[]{:S(2)}, u32[]{:S(2)}) %all-to-all-start.4) | async-done | bytes 262176 | tf_op jit(solution)/shard_map/all_to_all | solution.py:227
  102.4 0.6 shard_map.94
  103.0 2.9 %collective-permute-start.5 = (bf16[4,16,256]{2,1,0:T(8,128)(2,1)S(1)}, bf16[4,16,256]{2,1,0:T(8,128)(2,1)S(1)}, u32[]{:S(2)}, u32[]{:S(2)}) collective-permute-start(bf16[4,16,256]{2,1,0:T(8,128)(2,1)S(1)} %broadcast_select_fusion), channel_id=1, source_target_pairs={{0,1},{1,0},{2,3},{3,2},{4,5},{5,4},{6,7},{7,6},{8,9},{9,8},{10,11... | collective-permute-start | bytes 98312 | tf_op jit(solution)/shard_map/ppermute | solution.py:252
  105.9 0.8 collective-permute-done.5
  106.7 0.6 select_bitcast_fusion
  (12 shorter events, 0.1 us)
Async XLA Ops:
  4.1 7.0 %copy-start.1 = (bf16[4,16,256]{2,1,0:T(8,128)(2,1)S(1)}, bf16[4,16,256]{2,1,0:T(8,128)(2,1)}, u32[]{:S(2)}) copy-start(bf16[4,16,256]{2,1,0:T(8,128)(2,1)} %param.6) | copy-start | bytes 98308
  4.1 7.0 %copy-start.3 = (bf16[1,16,256]{2,1,0:T(8,128)(2,1)S(1)}, bf16[1,16,256]{2,1,0:T(8,128)(2,1)}, u32[]{:S(2)}) copy-start(bf16[1,16,256]{2,1,0:T(8,128)(2,1)} %param.7) | copy-start | bytes 24580
  4.1 7.0 %copy-start.2 = (bf16[4,16,256]{2,1,0:T(8,128)(2,1)S(1)}, bf16[4,16,256]{2,1,0:T(8,128)(2,1)}, u32[]{:S(2)}) copy-start(bf16[4,16,256]{2,1,0:T(8,128)(2,1)} %param.11) | copy-start | bytes 98308
  4.1 7.0 %copy-start.4 = (bf16[1,16,256]{2,1,0:T(8,128)(2,1)S(1)}, bf16[1,16,256]{2,1,0:T(8,128)(2,1)}, u32[]{:S(2)}) copy-start(bf16[1,16,256]{2,1,0:T(8,128)(2,1)} %param.8) | copy-start | bytes 24580
  4.1 7.0 %slice-start = ((bf16[4,16,256]{2,1,0:T(8,128)(2,1)}), bf16[3,16,256]{2,1,0:T(8,128)(2,1)S(1)}, s32[]{:S(2)}) async-start(bf16[4,16,256]{2,1,0:T(8,128)(2,1)} %param.6), calls=%async_computation.5 | async-start | bytes 49152 | tf_op jit(solution)/shard_map/slice | solution.py:209
  4.1 7.0 %slice-start.1 = ((bf16[4,16,256]{2,1,0:T(8,128)(2,1)}), bf16[3,16,256]{2,1,0:T(8,128)(2,1)S(1)}, s32[]{:S(2)}) async-start(bf16[4,16,256]{2,1,0:T(8,128)(2,1)} %param.11), calls=%async_computation.6 | async-start | bytes 49152 | tf_op jit(solution)/shard_map/slice | solution.py:211
  4.1 17.7 %all-to-all-start = ((bf16[16,2,32,256]{3,2,1,0:T(8,128)(2,1)}), bf16[16,2,32,256]{3,2,1,0:T(8,128)(2,1)S(1)}, u32[]{:S(2)}, u32[]{:S(2)}) async-start(bf16[16,2,32,256]{3,2,1,0:T(8,128)(2,1)} %broadcast_in_dim.15), calls=%async_computation | async-start | bytes 1048576 | tf_op jit(solution)/shard_map/all_to_all | solution.py:200
  11.0 2.3 %copy-start = (bf16[1,16,27,512]{3,1,2,0:T(8,128)(2,1)S(1)}, bf16[1,16,27,512]{3,1,2,0:T(8,128)(2,1)}, u32[]{:S(2)}) copy-start(bf16[1,16,27,512]{3,1,2,0:T(8,128)(2,1)} %param.10) | copy-start | bytes 1327108
  21.8 19.2 %collective-permute-start.1 = (bf16[16,2,32,256]{3,2,1,0:T(8,128)(2,1)S(1)}, bf16[16,2,32,256]{3,2,1,0:T(8,128)(2,1)S(1)}, u32[]{:S(2)}, u32[]{:S(2)}) collective-permute-start(bf16[16,2,32,256]{3,2,1,0:T(8,128)(2,1)S(1)} %all-to-all-done.near), channel_id=1, source_target_pairs={{0,1},{1,0},{2,3},{3,2},{4,5},{5,4},{6,7},{7,6},{8,9},{9,8},{10,11... | collective-permute-start | bytes 1572872 | tf_op jit(solution)/shard_map/ppermute | solution.py:201
  39.1 4.5 %collective-permute-start = (bf16[32,256]{1,0:T(8,128)(2,1)S(1)}, bf16[32,256]{1,0:T(8,128)(2,1)S(1)}, u32[]{:S(2)}, u32[]{:S(2)}) collective-permute-start(bf16[32,256]{1,0:T(8,128)(2,1)S(1)} %shard_map.86), channel_id=1, source_target_pairs={{0,32},{2,34},{4,36},{6,38},{8,40},{10,42},{12,44},{14,46},{16,48}... | collective-permute-start | bytes 49160 | tf_op jit(solution)/shard_map/ppermute | solution.py:246
  55.7 4.7 %collective-permute-start.2 = (bf16[32,256]{1,0:T(8,128)(2,1)S(1)}, bf16[32,256]{1,0:T(8,128)(2,1)S(1)}, u32[]{:S(2)}, u32[]{:S(2)}) collective-permute-start(bf16[32,256]{1,0:T(8,128)(2,1)S(1)} %shard_map.89), channel_id=1, source_target_pairs={{0,32},{2,34},{4,36},{6,38},{8,40},{10,42},{12,44},{14,46},{16,48}... | collective-permute-start | bytes 49160 | tf_op jit(solution)/shard_map/ppermute | solution.py:246
  72.7 5.7 %collective-permute-start.3 = (bf16[32,256]{1,0:T(8,128)(2,1)S(1)}, bf16[32,256]{1,0:T(8,128)(2,1)S(1)}, u32[]{:S(2)}, u32[]{:S(2)}) collective-permute-start(bf16[32,256]{1,0:T(8,128)(2,1)S(1)} %shard_map.91), channel_id=1, source_target_pairs={{0,32},{2,34},{4,36},{6,38},{8,40},{10,42},{12,44},{14,46},{16,48}... | collective-permute-start | bytes 49160 | tf_op jit(solution)/shard_map/ppermute | solution.py:246
  80.5 13.0 %collective-permute-start.4 = (bf16[4,16,256]{2,1,0:T(8,128)(2,1)S(1)}, bf16[4,16,256]{2,1,0:T(8,128)(2,1)S(1)}, u32[]{:S(2)}, u32[]{:S(2)}) collective-permute-start(bf16[4,16,256]{2,1,0:T(8,128)(2,1)S(1)} %slice.76), channel_id=1, source_target_pairs={{1,0},{3,2},{5,4},{7,6},{9,8},{11,10},{13,12},{15,14},{17,16},{19,... | collective-permute-start | bytes 98312 | tf_op jit(solution)/shard_map/ppermute | solution.py:234
  89.9 12.4 %all-to-all-start.4 = ((bf16[16,32,256]{2,1,0:T(8,128)(2,1)}), bf16[16,32,256]{2,1,0:T(8,128)(2,1)S(1)}, u32[]{:S(2)}, u32[]{:S(2)}) async-start(bf16[16,32,256]{2,1,0:T(8,128)(2,1)} %get-tuple-element.22), calls=%async_computation.4 | async-start | bytes 524288 | tf_op jit(solution)/shard_map/all_to_all | solution.py:227
  103.0 3.7 %collective-permute-start.5 = (bf16[4,16,256]{2,1,0:T(8,128)(2,1)S(1)}, bf16[4,16,256]{2,1,0:T(8,128)(2,1)S(1)}, u32[]{:S(2)}, u32[]{:S(2)}) collective-permute-start(bf16[4,16,256]{2,1,0:T(8,128)(2,1)S(1)} %broadcast_select_fusion), channel_id=1, source_target_pairs={{0,1},{1,0},{2,3},{3,2},{4,5},{5,4},{6,7},{7,6},{8,9},{9,8},{10,11... | collective-permute-start | bytes 98312 | tf_op jit(solution)/shard_map/ppermute | solution.py:252

commit v3 on v1

v3 whole, which is shorter than its diff:
```python
import functools

import jax
import jax.numpy as jnp
from jax import lax
from jax.experimental import pallas as pl
from jax.experimental.pallas import tpu as pltpu
from jax.sharding import Mesh, PartitionSpec as P


SX, SY, SZ = 4, 8, 8
CELLS = SX * SY * SZ
TAPS = 27
OWN = 16
PAIR = 32
ROUNDS = 4
CHANNELS = 512
ROWS = TAPS * OWN
STEPS = (SY * SZ, SZ, 1)
EXTENT = (SX, SY, SZ)
VMEM_LIMIT = 16 * 1024 * 1024
LIGHT = pl.CostEstimate(flops=1, transcendentals=0, bytes_accessed=1)


def coordinates(rows):
    cell = lax.broadcasted_iota(jnp.int32, (rows, CELLS), 1)
    return (cell >> 6, (cell >> 3) & 7, cell & 7)


def moved(value, where, axis, step):
    if step == 0:
        return value
    rolled = pltpu.roll(value, (-step * STEPS[axis]) % CELLS, 1)
    place = where[axis]
    inside = place < EXTENT[axis] - 1 if step > 0 else place > 0
    return jnp.where(inside, rolled, 0.0)


def tap_total(taps, base, where):
    total = None
    for i in range(3):
        plane = None
        for j in range(3):
            line = None
            for l in range(3):
                start = base + OWN * (9 * i + 3 * j + l)
                term = moved(taps[start : start + OWN, :], where, 2, l - 1)
                line = term if line is None else line + term
            line = moved(line, where, 1, j - 1)
            plane = line if plane is None else plane + line
        plane = moved(plane, where, 0, i - 1)
        total = plane if total is None else total + plane
    return total


def spread_into(spread, base, value, where):
    for i in range(3):
        plane = moved(value, where, 0, 1 - i)
        for j in range(3):
            line = moved(plane, where, 1, 1 - j)
            for l in range(3):
                start = base + OWN * (9 * i + 3 * j + l)
                spread[start : start + OWN, :] = moved(line, where, 2, 1 - l).astype(jnp.bfloat16)


def slope_into(slope, filters, whole, taps, where):
    taps[...] = jnp.dot(filters[...], whole.reshape(CHANNELS, CELLS), preferred_element_type=jnp.float32)
    for c in range(2):
        pre = tap_total(taps, ROWS * c, where)
        logistic = 1.0 / (1.0 + jnp.exp(-pre))
        slope[OWN * c : OWN * (c + 1), :] = logistic * (1.0 + pre * (1.0 - logistic))


def silu_into(out, filters, whole, taps, where):
    taps[...] = jnp.dot(filters[...], whole.reshape(CHANNELS, CELLS), preferred_element_type=jnp.float32)
    for c in range(2):
        pre = tap_total(taps, ROWS * c, where)
        out[OWN * c : OWN * (c + 1), :] = (pre / (1.0 + jnp.exp(-pre))).astype(jnp.bfloat16)


def late_round(tails, r, whole):
    if r < 3:
        return tails[2 - r, :, 0:2]
    whole[:, 0] = tails[0, :, 2]
    whole[:, 1] = tails[1, :, 2]
    return whole[...]


def first_kernel(flags, near, filters, act, slope, taps):
    where = coordinates(OWN)

    @pl.when(flags[0] == 0)
    def _():
        silu_into(act, filters, near[:, 0:2], taps, where)
        slope[...] = jnp.zeros_like(slope)

    @pl.when(flags[0] != 0)
    def _():
        act[...] = jnp.zeros_like(act)
        slope_into(slope, filters, near[:, 0:2], taps, where)


def slope_kernel(flags, filters, tails, second, third, fourth, taps, whole):
    @pl.when(flags[0] == 0)
    def _():
        for slope in (second, third, fourth):
            slope[...] = jnp.zeros_like(slope)

    @pl.when(flags[0] != 0)
    def _():
        where = coordinates(OWN)
        for r, slope in enumerate((second, third, fourth)):
            slope_into(slope, filters, late_round(tails, r + 1, whole), taps, where)


def sum_into(out, arrived):
    total = arrived[0].astype(jnp.float32)
    for p in range(1, arrived.shape[0]):
        total = total + arrived[p].astype(jnp.float32)
    out[...] = total.astype(jnp.bfloat16)


def finish_kernel(flags, arrived, filters, out, taps):
    @pl.when(flags[0] == 0)
    def _():
        silu_into(out, filters, arrived[...], taps, coordinates(OWN))

    @pl.when(flags[0] != 0)
    def _():
        sum_into(out, arrived)


def sum_kernel(flags, arrived, out):
    @pl.when(flags[0] == 0)
    def _():
        out[...] = jnp.zeros_like(out)

    @pl.when(flags[0] != 0)
    def _():
        sum_into(out, arrived)


def pack_kernel(flags, arrived, filters, *refs):
    (*outs, grad), dpres, (act, parcel, taps) = refs[:4], refs[4:8], refs[8:]

    @pl.when(flags[0] == 0)
    def _():
        silu_into(act, filters, arrived[...], taps, coordinates(OWN))
        for r, pair in enumerate((*outs, act)):
            parcel[r] = pair[OWN:, :]
        for r in range(ROUNDS - 1):
            parcel[ROUNDS + r] = jnp.zeros((OWN, CELLS), jnp.bfloat16)

    @pl.when(flags[0] != 0)
    def _():
        act[...] = jnp.zeros_like(act)
        for r, pair in enumerate((*dpres, *outs[1:], grad)):
            parcel[r] = pair[:OWN, :]


def last_kernel(flags, arrived, parcels, second, third, fourth, grads):
    for r, pair in enumerate((second, third, fourth)):
        odd = pair[OWN:, :].astype(jnp.float32)
        even = parcels[1, ROUNDS + r].astype(jnp.float32)
        grads[r] = jnp.where(flags[0] == 0, even, odd).astype(jnp.bfloat16)
    total = arrived[1].astype(jnp.float32)
    for d in range(3, arrived.shape[0], 2):
        total = total + arrived[d].astype(jnp.float32)
    grads[ROUNDS - 1] = total.astype(jnp.bfloat16)


def start_kernel(edge_slot, last, flags, received, outside, slope, filters, sent, dpre, spread):
    take = flags[edge_slot] != 0
    value = jnp.where(take, outside[...].astype(jnp.float32), received[...].astype(jnp.float32))

    @pl.when(flags[0] == 0)
    def _():
        copy = value.astype(jnp.bfloat16)
        dpre[...] = copy
        if last:
            sent[...] = jnp.zeros_like(sent)
        else:
            for p in range(sent.shape[0]):
                sent[p] = copy

    @pl.when(flags[0] != 0)
    def _():
        where = coordinates(OWN)
        rounded = (value * slope[...]).astype(jnp.bfloat16)
        dpre[...] = rounded
        wide = rounded.astype(jnp.float32)
        for c in range(2):
            spread_into(spread, ROWS * c, wide[OWN * c : OWN * (c + 1), :], where)
        part = lax.dot_general(
            filters[...], spread[...], (((0,), (0,)), ((), ())), preferred_element_type=jnp.float32
        )
        sent[...] = part.astype(jnp.bfloat16).reshape(sent.shape)


def filter_kernel(flags, heads, tails, parcels, *refs):
    acts_pair, dpres, (out, acts, spread, whole) = refs[:4], refs[4:8], refs[8:]
    where = coordinates(OWN)
    even_core = flags[0] == 0
    for r in range(ROUNDS):
        own = acts_pair[r][:OWN, :].astype(jnp.float32)
        acts[r] = jnp.where(even_core, own, parcels[0, r].astype(jnp.float32)).astype(jnp.bfloat16)
        own = dpres[r][OWN:, :].astype(jnp.float32)
        spread_into(spread, 0, jnp.where(even_core, parcels[1, r].astype(jnp.float32), own), where)
        term = lax.dot_general(
            spread[...],
            (late_round(tails, r, whole) if r else heads[1]).reshape(CHANNELS, CELLS),
            (((1,), (1,)), ((), ())),
            preferred_element_type=jnp.float32,
        )
        if r == 0:
            out[...] = term
        else:
            out[...] += term


def local_call(kernel, outs, kinds, scratch, cost=None):
    spaces = {"s": pltpu.SMEM, "v": pltpu.VMEM}
    specs = [pl.BlockSpec(memory_space=spaces[kind]) for kind in kinds]
    result = jax.tree.map(lambda _: pl.BlockSpec(memory_space=pltpu.VMEM), outs)
    return pl.pallas_call(
        kernel,
        out_shape=outs,
        in_specs=specs,
        out_specs=result,
        scratch_shapes=scratch,
        compiler_params=pltpu.CompilerParams(vmem_limit_bytes=VMEM_LIMIT),
        cost_estimate=cost,
    )


def shape(dims, dtype=jnp.bfloat16):
    return jax.ShapeDtypeStruct(dims, dtype)


def body(sections, inputs, front, back, saved, weights, cotangent):
    chips = CHANNELS // PAIR
    section = lax.axis_index("section")
    core = lax.axis_index("core")
    forward = core == 0
    at_edge = jnp.where(forward, section == 0, section == sections - 1)
    from_outside = jnp.where(forward, section == 0, True)
    flags = jnp.stack([core, from_outside.astype(jnp.int32), at_edge.astype(jnp.int32)]).astype(jnp.int32)
    ahead, behind = [], []
    for s in range(sections - 1):
        for p in range(chips):
            here = (s * chips + p) * 2
            ahead.append((here, here + 2 * chips))
            behind.append((here + 1 + 2 * chips, here + 1))
    hops = [ahead, ahead + behind, ahead + behind, behind]

    known = lax.all_gather(
        jnp.concatenate([jnp.where(section == 0, inputs[:1], front), saved[0]]), "core", axis=1, tiled=True
    )
    block = jnp.where(
        forward,
        jnp.concatenate([known[0], known[3], known[4, :OWN]]),
        jnp.concatenate([known[1], known[2], known[4, OWN:]]),
    ).reshape(5, OWN, CELLS)
    near = lax.all_to_all(jnp.broadcast_to(block[None], (chips,) + block.shape), "chip", 0, 0)

    filters = lax.all_gather(
        jnp.transpose(weights[0], (1, 0, 2)).reshape(ROWS, CHANNELS), "core", axis=0, tiled=True
    )
    ends = jnp.concatenate(
        [inputs[1:], jnp.where(section == sections - 1, cotangent[:1], back), cotangent[1:]]
    )
    ends = lax.all_gather(ends, "core", axis=1, tiled=True)
    outside = jnp.where(forward, jnp.concatenate([ends[:3], ends[2:3]]), ends[3:])

    taps_scratch = pltpu.VMEM((2 * ROWS, CELLS), jnp.float32)
    spread_scratch = pltpu.VMEM((2 * ROWS, CELLS), jnp.bfloat16)
    whole_scratch = pltpu.VMEM((chips, 2, OWN, CELLS), jnp.bfloat16)
    mine, slope_shape = shape((PAIR, CELLS)), shape((PAIR, CELLS), jnp.float32)

    act, slope = local_call(first_kernel, (mine, slope_shape), "svv", [taps_scratch])(flags, near, filters)
    slopes = [slope]
    outs, dpres = [act], []
    for step in range(ROUNDS):
        last = step + 1 == ROUNDS
        received = lax.ppermute(outs[step], ("section", "chip", "core"), hops[step])
        sent_shape = shape((2 * chips, OWN, CELLS) if last else (chips, PAIR, CELLS))
        sent, dpre = local_call(
            functools.partial(start_kernel, 1 if step == 0 else 2, last),
            (sent_shape, mine),
            "svvvv",
            [spread_scratch],
        )(flags, received, outside[step], slopes[step], filters)
        dpres.append(dpre)
        if last:
            break
        if step == 0:
            sent, near = lax.optimization_barrier((sent, near))
        arrived = lax.all_to_all(sent, "chip", 0, 0)
        if step == 0:
            tails = lax.all_gather(near[:, 2:], "core", axis=0)
            heads = lax.all_gather(near[:, :2], "core", axis=0)
            rest = local_call(slope_kernel, (slope_shape,) * 3, "svv", [taps_scratch, whole_scratch], LIGHT)(
                flags, filters, tails
            )
            arrived, heads, *rest = lax.optimization_barrier((arrived, heads, *rest))
            slopes.extend(rest)
        if step + 2 < ROUNDS:
            out = local_call(finish_kernel, mine, "svv", [taps_scratch])(flags, arrived, filters)
        else:
            out = local_call(sum_kernel, mine, "sv", [])(flags, arrived)
        outs.append(out)

    sent, arrived = lax.optimization_barrier((sent, arrived))
    partials = lax.all_to_all(sent, ("chip", "core"), 0, 0)
    act, parcel = local_call(
        pack_kernel, (mine, shape((2 * ROUNDS - 1, OWN, CELLS))), "svv" + "v" * 8, [taps_scratch], LIGHT
    )(flags, arrived, filters, *outs, *dpres)
    parcels = lax.all_gather(parcel, "core", axis=0)
    filter_grad, acts = local_call(
        filter_kernel,
        (shape((ROWS, CHANNELS), jnp.float32), shape((ROUNDS, OWN, CELLS))),
        "svvv" + "v" * 8,
        [pltpu.VMEM((ROWS, CELLS), jnp.bfloat16), whole_scratch],
        LIGHT,
    )(flags, heads, tails, parcels, *outs[:3], act, *dpres)
    partials, filter_grad = lax.optimization_barrier((partials, filter_grad))
    grads = local_call(last_kernel, shape((ROUNDS, OWN, CELLS)), "svvvvv", [])(
        flags, partials, parcels, *outs[1:]
    )
    filter_grad = jnp.transpose(filter_grad.reshape(TAPS, OWN, CHANNELS), (1, 0, 2))
    return acts[None], grads[None], filter_grad[None]


def solution(mesh):
    sections = mesh.shape["section"]
    fine = Mesh(mesh.devices.reshape(sections, -1, 2), ("section", "chip", "core"))
    chan = ("chip", "core")
    return jax.shard_map(
        lambda *arrays: body(sections, *arrays),
        mesh=fine,
        in_specs=(
            P(None, chan, None),
            P("section", chan, None),
            P("section", chan, None),
            P("section", None, chan, None),
            P("section", chan, None, None),
            P(None, chan, None),
        ),
        out_specs=(
            P("section", None, chan, None),
            P("section", None, chan, None),
            P("section", chan, None, None),
        ),
        check_vma=False,
    )
```

time: 117 us -> 107 us (0.915)
  the two profiles are of different devices: /device:TPU:385 before, /device:TPU:97 now
where the time goes in v3:
time: 107 us
  blocking collectives  45 us (42%)
  waiting for transfers between devices  21.4 us (20%)
  starting transfers between devices  20.5 us (19%)
  Pallas kernels  16.4 us (15%)
  local copies, waits for them, and re-layouts  1.63 us (2%)
    all_to_all x2, blocking collectives, body(): arrived = lax.all_to_all(sent, 'chip', 0, 0)  24.9 us
    ppermute x4, waiting for transfers between devices, body(): received = lax.ppermute(outs[step], ('section', 'chip', 'core'), hops[step])  11.9 us
    all_gather x1, blocking collectives, body(): tails = lax.all_gather(near[:, 2:], 'core', axis=0)  8.66 us
    pallas_call x4, Pallas kernels, body(): local_call(functools.partial(start_kernel, 1 if step == 0 else 2, last),...  7.13 us
    all_to_all x1, starting transfers between devices, body(): lax.all_to_all(jnp.broadcast_to(block[None], (chips,) + block.shape), 'ch...  6.9 us
    ppermute x4, starting transfers between devices, body(): received = lax.ppermute(outs[step], ('section', 'chip', 'core'), hops[step])  6.42 us
    all_to_all x1, waiting for transfers between devices, body(): lax.all_to_all(jnp.broadcast_to(block[None], (chips,) + block.shape), 'ch...  6.42 us
    all_to_all x1, starting transfers between devices, body(): partials = lax.all_to_all(sent, ('chip', 'core'), 0, 0)  3.65 us
  transfers between devices with their start and end apart: 7, of which 5 were waited for; matrix products, arithmetic and copies ran while one was open for 0% of the time, Pallas kernels for 5%

profile of v3, /device:TPU:97, one launch (start us, length us, event | category | flops | bytes accessed | tf_op | source)
XLA Modules:
  0.0 106.7 jit_solution(11172267100513864573)
XLA Ops:
  0.6 0.0 copy-start.4
  0.6 0.7 slice_select_fusion.2
  1.4 0.0 copy-done.4
  1.4 2.2 %all_gather.27 = bf16[5,32,256]{2,1,0:T(8,128)(2,1)S(1)} all-gather(bf16[5,16,256]{2,1,0:T(8,128)(2,1)S(1)} %pad_maximum_fusion.1), channel_id=1, replica_groups=mesh['section'=16,'chip'=16,'core'=2] {'core'}, dimensions={1}, use_global_device_ids=true | all-gather | bytes 122880 | tf_op jit(solution)/shard_map/all_gather | solution.py:256
  3.6 0.9 broadcast_in_dim.14
  4.5 6.9 %all-to-all-start = ((bf16[16,5,16,256]{3,2,1,0:T(8,128)(2,1)}), bf16[16,5,16,256]{3,2,1,0:T(8,128)(2,1)S(1)}, u32[]{:S(2)}, u32[]{:S(2)}) async-start(bf16[16,5,16,256]{3,2,1,0:T(8,128)(2,1)} %broadcast_in_dim.14), calls=%async_computation | async-start | bytes 1310720 | tf_op jit(solution)/shard_map/all_to_all | solution.py:264
  11.4 0.0 copy-start.2
  11.4 0.0 copy-done.3
  11.4 0.0 copy-done.5
  11.5 0.0 slice-done.1
  11.5 0.0 slice-done.2
  11.5 2.3 %all_gather.29 = bf16[7,32,256]{2,1,0:T(8,128)(2,1)S(1)} all-gather(bf16[7,16,256]{2,1,0:T(8,128)(2,1)S(1)} %pad_maximum_fusion), channel_id=1, replica_groups=mesh['section'=16,'chip'=16,'core'=2] {'core'}, dimensions={1}, use_global_device_ids=true | all-gather | bytes 172032 | tf_op jit(solution)/shard_map/all_gather | solution.py:272
  13.8 0.6 copy-done
  14.5 0.1 pad_add_fusion.flags
  14.5 0.0 copy-done.2
  14.5 2.6 %all_gather.28.filters = bf16[864,512]{1,0:T(8,128)(2,1)S(1)} all-gather(bf16[432,512]{1,0:T(8,128)(2,1)S(1)} %bitcast.45), channel_id=1, replica_groups=mesh['section'=16,'chip'=16,'core'=2] {'core'}, dimensions={0}, use_global_device_ids=true | all-gather | bytes 1327104 | tf_op jit(solution)/shard_map/all_gather | solution.py:266
  17.1 0.0 copy-done.1
  17.1 0.0 slice-done
  17.1 6.4 %all-to-all-done.near = bf16[16,5,16,256]{3,2,1,0:T(8,128)(2,1)S(1)} async-done(((bf16[16,5,16,256]{3,2,1,0:T(8,128)(2,1)}), bf16[16,5,16,256]{3,2,1,0:T(8,128)(2,1)S(1)}, u32[]{:S(2)}, u32[]{:S(2)}) %all-to-all-start) | async-done | bytes 655392 | tf_op jit(solution)/shard_map/all_to_all | solution.py:264
  23.5 1.2 %shard_map.85 = (bf16[32,256]{1,0:T(8,128)(2,1)S(1)}, f32[32,256]{1,0:T(8,128)S(1)}) custom-call(s32[3]{0:T(128)S(1)} %pad_add_fusion.flags, bf16[16,5,16,256]{3,2,1,0:T(8,128)(2,1)S(1)} %all-to-all-done.near, bf16[864,512]{1,0:T(8,128)(2,1)S(1)} %all_gather.28.filters), custom_call_target="tpu_custom_call" | custom-call | tf_op jit(solution)/shard_map/pallas_call | solution.py:280
  24.7 0.7 collective-permute-start
  25.4 0.0 collective-permute-done.received
  25.4 2.1 %shard_map.86 = (bf16[16,32,256]{2,1,0:T(8,128)(2,1)}, bf16[32,256]{1,0:T(8,128)(2,1)S(1)}) custom-call(s32[3]{0:T(128)S(1)} %pad_add_fusion.flags, bf16[32,256]{1,0:T(8,128)(2,1)S(1)} %collective-permute-done.received, bf16[32,256]{1,0:T(8,128)(2,1)S(1)} %get-tuple-element.68.outside, f32[32,256]{1,0:T(8,128)S(1)} %get-tuple-element.32.slope, ...), custom_call_target="tpu_custom_call" | custom-call | tf_op jit(solution)/shard_map/pallas_call | solution.py:287
  27.5 3.5 %all-to-all-start.1 = ((bf16[16,32,256]{2,1,0:T(8,128)(2,1)}), bf16[16,32,256]{2,1,0:T(8,128)(2,1)S(1)}, u32[]{:S(2)}, u32[]{:S(2)}) async-start(bf16[16,32,256]{2,1,0:T(8,128)(2,1)} %get-tuple-element.34), calls=%async_computation.1 | async-start | bytes 524288 | tf_op jit(solution)/shard_map/all_to_all | solution.py:298
  31.1 8.7 %all-gather.1 = bf16[32,3,16,256]{3,2,1,0:T(8,128)(2,1)S(1)} all-gather(bf16[16,3,16,256]{3,2,1,0:T(8,128)(2,1)S(1)} %slice.72), channel_id=3, replica_groups=mesh['section'=16,'chip'=16,'core'=2] {'core'}, dimensions={0}, use_global_device_ids=true | all-gather | bytes 1179648 | tf_op jit(solution)/shard_map/all_gather | solution.py:300
  39.8 1.8 %shard_map.87 = (f32[32,256]{1,0:T(8,128)S(1)}, f32[32,256]{1,0:T(8,128)S(1)}, f32[32,256]{1,0:T(8,128)S(1)}) custom-call(s32[3]{0:T(128)S(1)} %pad_add_fusion.flags, bf16[864,512]{1,0:T(8,128)(2,1)S(1)} %all_gather.28.filters, bf16[2,16,3,16,256]{4,3,2,1,0:T(8,128)(2,1)S(1)} %bitcast.40), custom_call_target="tpu_custom_call" | custom-call | flops 1 | bytes 1 | tf_op jit(solution)/shard_map/pallas_call | solution.py:302
  41.6 2.2 %all-gather = bf16[32,2,16,256]{3,2,1,0:T(8,128)(2,1)S(1)} all-gather(bf16[16,2,16,256]{3,2,1,0:T(8,128)(2,1)S(1)} %slice.71), channel_id=2, replica_groups=mesh['section'=16,'chip'=16,'core'=2] {'core'}, dimensions={0}, use_global_device_ids=true | all-gather | bytes 786432 | tf_op jit(solution)/shard_map/all_gather | solution.py:301
  43.8 0.0 all-to-all-done.1.arrived
  43.8 0.6 shard_map.88.refs_1_.second
  44.4 1.9 %collective-permute-start.1 = (bf16[32,256]{1,0:T(8,128)(2,1)S(1)}, bf16[32,256]{1,0:T(8,128)(2,1)S(1)}, u32[]{:S(2)}, u32[]{:S(2)}) collective-permute-start(bf16[32,256]{1,0:T(8,128)(2,1)S(1)} %shard_map.88.refs_1_.second), channel_id=1, source_target_pairs={{0,32},{2,34},{4,36},{6,38},{8,40},{10,42},{12,44},{14,46},{16,48}... | collective-permute-start | bytes 49160 | tf_op jit(solution)/shard_map/ppermute | solution.py:285
  46.3 4.3 %collective-permute-done.1.received = bf16[32,256]{1,0:T(8,128)(2,1)S(1)} collective-permute-done((bf16[32,256]{1,0:T(8,128)(2,1)S(1)}, bf16[32,256]{1,0:T(8,128)(2,1)S(1)}, u32[]{:S(2)}, u32[]{:S(2)}) %collective-permute-start.1) | collective-permute-done | bytes 16416 | tf_op jit(solution)/shard_map/ppermute | solution.py:285
  50.6 1.4 %shard_map.89 = (bf16[16,32,256]{2,1,0:T(8,128)(2,1)S(1)}, bf16[32,256]{1,0:T(8,128)(2,1)S(1)}) custom-call(s32[3]{0:T(128)S(1)} %pad_add_fusion.flags, bf16[32,256]{1,0:T(8,128)(2,1)S(1)} %collective-permute-done.1.received, bf16[32,256]{1,0:T(8,128)(2,1)S(1)} %get-tuple-element.67.outside, f32[32,256]{1,0:T(8,128)S(1)} %get-tuple-element.41.slope, ...), custom_call_target="tpu_custom_call" | custom-call | tf_op jit(solution)/shard_map/pallas_call | solution.py:287
  52.1 14.7 %all_to_all.25.arrived = bf16[16,32,256]{2,1,0:T(8,128)(2,1)S(1)} all-to-all(bf16[16,32,256]{2,1,0:T(8,128)(2,1)S(1)} %get-tuple-element.42), channel_id=1, replica_groups=mesh['section'=16,'chip'=16,'core'=2] {'chip'}, dimensions={0} | all-to-all | bytes 524288 | tf_op jit(solution)/shard_map/all_to_all | solution.py:298
  66.8 0.6 shard_map.90.refs_2_.third
  67.4 1.9 %collective-permute-start.2 = (bf16[32,256]{1,0:T(8,128)(2,1)S(1)}, bf16[32,256]{1,0:T(8,128)(2,1)S(1)}, u32[]{:S(2)}, u32[]{:S(2)}) collective-permute-start(bf16[32,256]{1,0:T(8,128)(2,1)S(1)} %shard_map.90.refs_2_.third), channel_id=1, source_target_pairs={{0,32},{2,34},{4,36},{6,38},{8,40},{10,42},{12,44},{14,46},{16,48}... | collective-permute-start | bytes 49160 | tf_op jit(solution)/shard_map/ppermute | solution.py:285
  69.3 3.8 %collective-permute-done.2.received = bf16[32,256]{1,0:T(8,128)(2,1)S(1)} collective-permute-done((bf16[32,256]{1,0:T(8,128)(2,1)S(1)}, bf16[32,256]{1,0:T(8,128)(2,1)S(1)}, u32[]{:S(2)}, u32[]{:S(2)}) %collective-permute-start.2) | collective-permute-done | bytes 16416 | tf_op jit(solution)/shard_map/ppermute | solution.py:285
  73.1 1.4 %shard_map.91 = (bf16[16,32,256]{2,1,0:T(8,128)(2,1)S(1)}, bf16[32,256]{1,0:T(8,128)(2,1)S(1)}) custom-call(s32[3]{0:T(128)S(1)} %pad_add_fusion.flags, bf16[32,256]{1,0:T(8,128)(2,1)S(1)} %collective-permute-done.2.received, bf16[32,256]{1,0:T(8,128)(2,1)S(1)} %get-tuple-element.66.outside, f32[32,256]{1,0:T(8,128)S(1)} %get-tuple-element.43.slope, ...), custom_call_target="tpu_custom_call" | custom-call | tf_op jit(solution)/shard_map/pallas_call | solution.py:287
  74.5 10.2 %all_to_all.26.arrived = bf16[16,32,256]{2,1,0:T(8,128)(2,1)S(1)} all-to-all(bf16[16,32,256]{2,1,0:T(8,128)(2,1)S(1)} %get-tuple-element.44), channel_id=1, replica_groups=mesh['section'=16,'chip'=16,'core'=2] {'chip'}, dimensions={0} | all-to-all | bytes 524288 | tf_op jit(solution)/shard_map/all_to_all | solution.py:298
  84.7 0.6 shard_map.92.refs_3_.fourth
  85.3 1.9 %collective-permute-start.3 = (bf16[32,256]{1,0:T(8,128)(2,1)S(1)}, bf16[32,256]{1,0:T(8,128)(2,1)S(1)}, u32[]{:S(2)}, u32[]{:S(2)}) collective-permute-start(bf16[32,256]{1,0:T(8,128)(2,1)S(1)} %shard_map.92.refs_3_.fourth), channel_id=1, source_target_pairs={{33,1},{35,3},{37,5},{39,7},{41,9},{43,11},{45,13},{47,15},{49,17}... | collective-permute-start | bytes 49160 | tf_op jit(solution)/shard_map/ppermute | solution.py:285
  87.2 3.8 %collective-permute-done.3.received = bf16[32,256]{1,0:T(8,128)(2,1)S(1)} collective-permute-done((bf16[32,256]{1,0:T(8,128)(2,1)S(1)}, bf16[32,256]{1,0:T(8,128)(2,1)S(1)}, u32[]{:S(2)}, u32[]{:S(2)}) %collective-permute-start.3) | collective-permute-done | bytes 16416 | tf_op jit(solution)/shard_map/ppermute | solution.py:285
  91.0 2.1 %shard_map.93 = (bf16[32,16,256]{2,1,0:T(8,128)(2,1)}, bf16[32,256]{1,0:T(8,128)(2,1)S(1)}) custom-call(s32[3]{0:T(128)S(1)} %pad_add_fusion.flags, bf16[32,256]{1,0:T(8,128)(2,1)S(1)} %collective-permute-done.3.received, bf16[32,256]{1,0:T(8,128)(2,1)S(1)} %get-tuple-element.65.outside, f32[32,256]{1,0:T(8,128)S(1)} %get-tuple-element.45.slope, ...), custom_call_target="tpu_custom_call" | custom-call | tf_op jit(solution)/shard_map/pallas_call | solution.py:287
  93.1 3.7 %all-to-all-start.4 = ((bf16[32,16,256]{2,1,0:T(8,128)(2,1)}), bf16[32,16,256]{2,1,0:T(8,128)(2,1)S(1)}, u32[]{:S(2)}, u32[]{:S(2)}) async-start(bf16[32,16,256]{2,1,0:T(8,128)(2,1)} %get-tuple-element.55), calls=%async_computation.4 | async-start | bytes 524288 | tf_op jit(solution)/shard_map/all_to_all | solution.py:314
  96.7 0.6 shard_map.94
  97.3 2.3 %all-gather.2 = bf16[14,16,256]{2,1,0:T(8,128)(2,1)S(1)} all-gather(bf16[7,16,256]{2,1,0:T(8,128)(2,1)S(1)} %get-tuple-element.52), channel_id=4, replica_groups=mesh['section'=16,'chip'=16,'core'=2] {'core'}, dimensions={0}, use_global_device_ids=true | all-gather | bytes 172032 | tf_op jit(solution)/shard_map/all_gather | solution.py:318
  99.6 2.8 %shard_map.95 = (f32[432,512]{1,0:T(8,128)}, bf16[4,16,256]{2,1,0:T(8,128)(2,1)}) custom-call(s32[3]{0:T(128)S(1)} %pad_add_fusion.flags, bf16[2,16,2,16,256]{4,3,2,1,0:T(8,128)(2,1)S(1)} %bitcast.42, bf16[2,16,3,16,256]{4,3,2,1,0:T(8,128)(2,1)S(1)} %bitcast.41, bf16[2,7,16,256]{3,2,1,0:T(8,128)(2,1)S(1)} %bitcast.43, ...), custom_call_target="tpu_custom_call" | custom-call | flops 1 | bytes 1 | tf_op jit(solution)/shard_map/pallas_call | solution.py:319
  102.4 3.2 %all-to-all-done.4.arrived = bf16[32,16,256]{2,1,0:T(8,128)(2,1)S(1)} async-done(((bf16[32,16,256]{2,1,0:T(8,128)(2,1)}), bf16[32,16,256]{2,1,0:T(8,128)(2,1)S(1)}, u32[]{:S(2)}, u32[]{:S(2)}) %all-to-all-start.4) | async-done | bytes 262176 | tf_op jit(solution)/shard_map/all_to_all | solution.py:314
  105.5 1.2 %shard_map.96 = bf16[4,16,256]{2,1,0:T(8,128)(2,1)} custom-call(s32[3]{0:T(128)S(1)} %pad_add_fusion.flags, bf16[32,16,256]{2,1,0:T(8,128)(2,1)S(1)} %all-to-all-done.4.arrived, bf16[2,7,16,256]{3,2,1,0:T(8,128)(2,1)S(1)} %bitcast.44, bf16[32,256]{1,0:T(8,128)(2,1)S(1)} %shard_map.88.refs_1_.second, bf16[32,256]{1,0:T(8,128)(2,1)S(1)} %shard_map.90.refs_2_.third, ...), custom_call_target="tpu_custom_call" | custom-call | tf_op jit(solution)/shard_map/pallas_call | solution.py:327
  (18 shorter events, 0.1 us)
Async XLA Ops:
  0.6 0.8 copy-start.4
  4.5 6.9 %copy-start.3 = (bf16[4,16,256]{2,1,0:T(8,128)(2,1)S(1)}, bf16[4,16,256]{2,1,0:T(8,128)(2,1)}, u32[]{:S(2)}) copy-start(bf16[4,16,256]{2,1,0:T(8,128)(2,1)} %param.11) | copy-start | bytes 98308
  4.5 6.9 %copy-start.5 = (bf16[1,16,256]{2,1,0:T(8,128)(2,1)S(1)}, bf16[1,16,256]{2,1,0:T(8,128)(2,1)}, u32[]{:S(2)}) copy-start(bf16[1,16,256]{2,1,0:T(8,128)(2,1)} %param.8) | copy-start | bytes 24580
  4.5 7.0 %slice-start.1 = ((bf16[4,16,256]{2,1,0:T(8,128)(2,1)}), bf16[3,16,256]{2,1,0:T(8,128)(2,1)S(1)}, s32[]{:S(2)}) async-start(bf16[4,16,256]{2,1,0:T(8,128)(2,1)} %param.6), calls=%async_computation.6 | async-start | bytes 49152 | tf_op jit(solution)/shard_map/slice | solution.py:270
  4.5 7.0 %slice-start.2 = ((bf16[4,16,256]{2,1,0:T(8,128)(2,1)}), bf16[3,16,256]{2,1,0:T(8,128)(2,1)S(1)}, s32[]{:S(2)}) async-start(bf16[4,16,256]{2,1,0:T(8,128)(2,1)} %param.11), calls=%async_computation.7 | async-start | bytes 49152 | tf_op jit(solution)/shard_map/slice | solution.py:270
  4.5 19.0 %all-to-all-start = ((bf16[16,5,16,256]{3,2,1,0:T(8,128)(2,1)}), bf16[16,5,16,256]{3,2,1,0:T(8,128)(2,1)S(1)}, u32[]{:S(2)}, u32[]{:S(2)}) async-start(bf16[16,5,16,256]{3,2,1,0:T(8,128)(2,1)} %broadcast_in_dim.14), calls=%async_computation | async-start | bytes 1310720 | tf_op jit(solution)/shard_map/all_to_all | solution.py:264
  11.4 3.1 %copy-start.2 = (bf16[1,16,27,512]{3,1,2,0:T(8,128)(2,1)S(1)}, bf16[1,16,27,512]{3,1,2,0:T(8,128)(2,1)}, u32[]{:S(2)}) copy-start(bf16[1,16,27,512]{3,1,2,0:T(8,128)(2,1)} %param.10) | copy-start | bytes 1327108
  13.8 0.6 copy-start
  14.5 2.6 %copy-start.1 = (bf16[7,32,256]{2,1,0:T(8,128)(2,1)S(1)}, bf16[7,32,256]{2,1,0:T(8,128)(2,1)}, u32[]{:S(2)}) copy-start(bf16[7,32,256]{2,1,0:T(8,128)(2,1)} %copy-done) | copy-start | bytes 344068
  14.5 2.6 %slice-start = ((bf16[7,32,256]{2,1,0:T(8,128)(2,1)}), bf16[3,32,256]{2,1,0:T(8,128)(2,1)S(1)}, s32[]{:S(2)}) async-start(bf16[7,32,256]{2,1,0:T(8,128)(2,1)} %copy-done), calls=%async_computation.5 | async-start | bytes 98304 | tf_op jit(solution)/shard_map/slice | solution.py:273
  24.7 0.7 collective-permute-start
  27.5 16.2 %all-to-all-start.1 = ((bf16[16,32,256]{2,1,0:T(8,128)(2,1)}), bf16[16,32,256]{2,1,0:T(8,128)(2,1)S(1)}, u32[]{:S(2)}, u32[]{:S(2)}) async-start(bf16[16,32,256]{2,1,0:T(8,128)(2,1)} %get-tuple-element.34), calls=%async_computation.1 | async-start | bytes 524288 | tf_op jit(solution)/shard_map/all_to_all | solution.py:298
  44.4 6.3 %collective-permute-start.1 = (bf16[32,256]{1,0:T(8,128)(2,1)S(1)}, bf16[32,256]{1,0:T(8,128)(2,1)S(1)}, u32[]{:S(2)}, u32[]{:S(2)}) collective-permute-start(bf16[32,256]{1,0:T(8,128)(2,1)S(1)} %shard_map.88.refs_1_.second), channel_id=1, source_target_pairs={{0,32},{2,34},{4,36},{6,38},{8,40},{10,42},{12,44},{14,46},{16,48}... | collective-permute-start | bytes 49160 | tf_op jit(solution)/shard_map/ppermute | solution.py:285
  67.4 5.7 %collective-permute-start.2 = (bf16[32,256]{1,0:T(8,128)(2,1)S(1)}, bf16[32,256]{1,0:T(8,128)(2,1)S(1)}, u32[]{:S(2)}, u32[]{:S(2)}) collective-permute-start(bf16[32,256]{1,0:T(8,128)(2,1)S(1)} %shard_map.90.refs_2_.third), channel_id=1, source_target_pairs={{0,32},{2,34},{4,36},{6,38},{8,40},{10,42},{12,44},{14,46},{16,48}... | collective-permute-start | bytes 49160 | tf_op jit(solution)/shard_map/ppermute | solution.py:285
  85.3 5.7 %collective-permute-start.3 = (bf16[32,256]{1,0:T(8,128)(2,1)S(1)}, bf16[32,256]{1,0:T(8,128)(2,1)S(1)}, u32[]{:S(2)}, u32[]{:S(2)}) collective-permute-start(bf16[32,256]{1,0:T(8,128)(2,1)S(1)} %shard_map.92.refs_3_.fourth), channel_id=1, source_target_pairs={{33,1},{35,3},{37,5},{39,7},{41,9},{43,11},{45,13},{47,15},{49,17}... | collective-permute-start | bytes 49160 | tf_op jit(solution)/shard_map/ppermute | solution.py:285
  93.1 12.4 %all-to-all-start.4 = ((bf16[32,16,256]{2,1,0:T(8,128)(2,1)}), bf16[32,16,256]{2,1,0:T(8,128)(2,1)S(1)}, u32[]{:S(2)}, u32[]{:S(2)}) async-start(bf16[32,16,256]{2,1,0:T(8,128)(2,1)} %get-tuple-element.55), calls=%async_computation.4 | async-start | bytes 524288 | tf_op jit(solution)/shard_map/all_to_all | solution.py:314

commit v4 on v3

--- a/solution.py
+++ b/solution.py
@@ -78,39 +78,39 @@
         out[OWN * c : OWN * (c + 1), :] = (pre / (1.0 + jnp.exp(-pre))).astype(jnp.bfloat16)
 
 
-def late_round(tails, r, whole):
-    if r < 3:
-        return tails[2 - r, :, 0:2]
-    whole[:, 0] = tails[0, :, 2]
-    whole[:, 1] = tails[1, :, 2]
+def joined(even, odd, whole):
+    whole[:, 0] = even[:, 4]
+    whole[:, 1] = odd[:, 4]
     return whole[...]
 
 
-def first_kernel(flags, near, filters, act, slope, taps):
+def first_kernel(flags, near, filters, act, first, second, taps):
     where = coordinates(OWN)
 
     @pl.when(flags[0] == 0)
     def _():
         silu_into(act, filters, near[:, 0:2], taps, where)
-        slope[...] = jnp.zeros_like(slope)
+        for slope in (first, second):
+            slope[...] = jnp.zeros_like(slope)
 
     @pl.when(flags[0] != 0)
     def _():
         act[...] = jnp.zeros_like(act)
-        slope_into(slope, filters, near[:, 0:2], taps, where)
-
-
-def slope_kernel(flags, filters, tails, second, third, fourth, taps, whole):
-    @pl.when(flags[0] == 0)
-    def _():
-        for slope in (second, third, fourth):
+        slope_into(first, filters, near[:, 0:2], taps, where)
+        slope_into(second, filters, near[:, 2:4], taps, where)
+
+
+def slope_kernel(flags, filters, near, far, third, fourth, taps, whole):
+    @pl.when(flags[0] == 0)
+    def _():
+        for slope in (third, fourth):
             slope[...] = jnp.zeros_like(slope)
 
     @pl.when(flags[0] != 0)
     def _():
         where = coordinates(OWN)
-        for r, slope in enumerate((second, third, fourth)):
-            slope_into(slope, filters, late_round(tails, r + 1, whole), taps, where)
+        slope_into(third, filters, far[:, 2:4], taps, where)
+        slope_into(fourth, filters, joined(far, near, whole), taps, where)
 
 
 def sum_into(out, arrived):
@@ -130,31 +130,19 @@
         sum_into(out, arrived)
 
 
-def sum_kernel(flags, arrived, out):
-    @pl.when(flags[0] == 0)
-    def _():
-        out[...] = jnp.zeros_like(out)
-
-    @pl.when(flags[0] != 0)
-    def _():
-        sum_into(out, arrived)
-
-
-def pack_kernel(flags, arrived, filters, *refs):
-    (*outs, grad), dpres, (act, parcel, taps) = refs[:4], refs[4:8], refs[8:]
-
-    @pl.when(flags[0] == 0)
-    def _():
-        silu_into(act, filters, arrived[...], taps, coordinates(OWN))
-        for r, pair in enumerate((*outs, act)):
+def pack_kernel(flags, *refs):
+    outs, dpres, parcel = refs[:4], refs[4:8], refs[8]
+
+    @pl.when(flags[0] == 0)
+    def _():
+        for r, pair in enumerate(outs):
             parcel[r] = pair[OWN:, :]
         for r in range(ROUNDS - 1):
             parcel[ROUNDS + r] = jnp.zeros((OWN, CELLS), jnp.bfloat16)
 
     @pl.when(flags[0] != 0)
     def _():
-        act[...] = jnp.zeros_like(act)
-        for r, pair in enumerate((*dpres, *outs[1:], grad)):
+        for r, pair in enumerate((*dpres, *outs[1:])):
             parcel[r] = pair[:OWN, :]
 
 
@@ -197,25 +185,38 @@
         sent[...] = part.astype(jnp.bfloat16).reshape(sent.shape)
 
 
-def filter_kernel(flags, heads, tails, parcels, *refs):
+def filter_kernel(flags, near, far, parcels, *refs):
     acts_pair, dpres, (out, acts, spread, whole) = refs[:4], refs[4:8], refs[8:]
-    where = coordinates(OWN)
-    even_core = flags[0] == 0
-    for r in range(ROUNDS):
-        own = acts_pair[r][:OWN, :].astype(jnp.float32)
-        acts[r] = jnp.where(even_core, own, parcels[0, r].astype(jnp.float32)).astype(jnp.bfloat16)
-        own = dpres[r][OWN:, :].astype(jnp.float32)
-        spread_into(spread, 0, jnp.where(even_core, parcels[1, r].astype(jnp.float32), own), where)
-        term = lax.dot_general(
-            spread[...],
-            (late_round(tails, r, whole) if r else heads[1]).reshape(CHANNELS, CELLS),
-            (((1,), (1,)), ((), ())),
-            preferred_element_type=jnp.float32,
+
+    def total(even, odd, act_of, dpre_of):
+        where = coordinates(OWN)
+        stored = (
+            lambda: odd[:, 0:2],
+            lambda: odd[:, 2:4],
+            lambda: even[:, 2:4],
+            lambda: joined(even, odd, whole),
         )
-        if r == 0:
-            out[...] = term
-        else:
-            out[...] += term
+        for r in range(ROUNDS):
+            acts[r] = act_of(r)
+            spread_into(spread, 0, dpre_of(r).astype(jnp.float32), where)
+            term = lax.dot_general(
+                spread[...],
+                stored[r]().reshape(CHANNELS, CELLS),
+                (((1,), (1,)), ((), ())),
+                preferred_element_type=jnp.float32,
+            )
+            if r == 0:
+                out[...] = term
+            else:
+                out[...] += term
+
+    @pl.when(flags[0] == 0)
+    def _():
+        total(near, far, lambda r: acts_pair[r][:OWN, :], lambda r: parcels[1, r])
+
+    @pl.when(flags[0] != 0)
+    def _():
+        total(far, near, lambda r: parcels[0, r], lambda r: dpres[r][OWN:, :])
 
 
 def local_call(kernel, outs, kinds, scratch, cost=None):
@@ -277,12 +278,23 @@
     whole_scratch = pltpu.VMEM((chips, 2, OWN, CELLS), jnp.bfloat16)
     mine, slope_shape = shape((PAIR, CELLS)), shape((PAIR, CELLS), jnp.float32)
 
-    act, slope = local_call(first_kernel, (mine, slope_shape), "svv", [taps_scratch])(flags, near, filters)
-    slopes = [slope]
+    act, *slopes = local_call(first_kernel, (mine, slope_shape, slope_shape), "svv", [taps_scratch])(
+        flags, near, filters
+    )
+    after = lax.optimization_barrier
     outs, dpres = [act], []
     for step in range(ROUNDS):
         last = step + 1 == ROUNDS
+        outs[step], near, filters = after((outs[step], near, filters))
         received = lax.ppermute(outs[step], ("section", "chip", "core"), hops[step])
+        if step == 0:
+            far = lax.ppermute(near, "core", [(0, 1), (1, 0)])
+        elif step == 2:
+            rest = local_call(slope_kernel, (slope_shape,) * 2, "svvv", [taps_scratch, whole_scratch], LIGHT)(
+                flags, filters, near, far
+            )
+            received, *rest = after((received, *rest))
+            slopes.extend(rest)
         sent_shape = shape((2 * chips, OWN, CELLS) if last else (chips, PAIR, CELLS))
         sent, dpre = local_call(
             functools.partial(start_kernel, 1 if step == 0 else 2, last),
@@ -293,28 +305,14 @@
         dpres.append(dpre)
         if last:
             break
-        if step == 0:
-            sent, near = lax.optimization_barrier((sent, near))
         arrived = lax.all_to_all(sent, "chip", 0, 0)
-        if step == 0:
-            tails = lax.all_gather(near[:, 2:], "core", axis=0)
-            heads = lax.all_gather(near[:, :2], "core", axis=0)
-            rest = local_call(slope_kernel, (slope_shape,) * 3, "svv", [taps_scratch, whole_scratch], LIGHT)(
-                flags, filters, tails
-            )
-            arrived, heads, *rest = lax.optimization_barrier((arrived, heads, *rest))
-            slopes.extend(rest)
-        if step + 2 < ROUNDS:
-            out = local_call(finish_kernel, mine, "svv", [taps_scratch])(flags, arrived, filters)
-        else:
-            out = local_call(sum_kernel, mine, "sv", [])(flags, arrived)
-        outs.append(out)
-
-    sent, arrived = lax.optimization_barrier((sent, arrived))
+        outs.append(local_call(finish_kernel, mine, "svv", [taps_scratch])(flags, arrived, filters))
+
+    sent, *dpres = after((sent, *dpres))
     partials = lax.all_to_all(sent, ("chip", "core"), 0, 0)
-    act, parcel = local_call(
-        pack_kernel, (mine, shape((2 * ROUNDS - 1, OWN, CELLS))), "svv" + "v" * 8, [taps_scratch], LIGHT
-    )(flags, arrived, filters, *outs, *dpres)
+    parcel = local_call(pack_kernel, shape((2 * ROUNDS - 1, OWN, CELLS)), "s" + "v" * 8, [], LIGHT)(
+        flags, *outs, *dpres
+    )
     parcels = lax.all_gather(parcel, "core", axis=0)
     filter_grad, acts = local_call(
         filter_kernel,
@@ -322,7 +320,7 @@
         "svvv" + "v" * 8,
         [pltpu.VMEM((ROWS, CELLS), jnp.bfloat16), whole_scratch],
         LIGHT,
-    )(flags, heads, tails, parcels, *outs[:3], act, *dpres)
+    )(flags, near, far, parcels, *outs, *dpres)
     partials, filter_grad = lax.optimization_barrier((partials, filter_grad))
     grads = local_call(last_kernel, shape((ROUNDS, OWN, CELLS)), "svvvvv", [])(
         flags, partials, parcels, *outs[1:]

time: 107 us -> 106 us (level)
  starting transfers between devices: 20.5 us -> 24.6 us
  blocking collectives: 45 us -> 41.7 us
  waiting for transfers between devices: 21.4 us -> 19.6 us
    all_gather x2 -> x0, blocking collectives: 10.8 us -> none  [the longest x1 8.66 us: body(): tails = lax.all_gather(near[:, 2:], 'core', axis=0)]
    all_to_all x2 -> x3, blocking collectives: 24.9 us -> 32.8 us  [body(): arrived = lax.all_to_all(sent, 'chip', 0, 0)]
    ppermute x0 -> x1, starting transfers between devices: none -> 7.66 us  [body(): far = lax.ppermute(near, 'core', [(0, 1), (1, 0)])]
    all_to_all x1 -> x0, starting transfers between devices: 3.53 us -> none  [body(): arrived = lax.all_to_all(sent, 'chip', 0, 0)]
    ppermute x4, waiting for transfers between devices: 11.9 us -> 9.73 us  [body(): received = lax.ppermute(outs[step], ('section', 'chip', 'core'), hops[step])]
    pallas_call x4 -> x3, Pallas kernels: 4.09 us -> 3.66 us  [the longest x1 1.55 us: body(): local_call(slope_kernel, (slope_shape,) * 2, 'svvv', [taps_scratch, whole...]
  transfers between devices with their start and end apart: 7 -> 7, of which waited for: 5 -> 5; matrix products, arithmetic and copies ran while one was open for 0% -> 0% of each run, Pallas kernels for 5% -> 8%
where the time goes in v4:
time: 106 us; the launch traced here: 105 us
  blocking collectives  41.7 us (39%)
  starting transfers between devices  24.6 us (23%)
  waiting for transfers between devices  19.6 us (18%)
  Pallas kernels  15.8 us (15%)
  local copies, waits for them, and re-layouts  1.59 us (2%)
    all_to_all x3, blocking collectives, body(): arrived = lax.all_to_all(sent, 'chip', 0, 0)  32.8 us
    ppermute x4, waiting for transfers between devices, body(): received = lax.ppermute(outs[step], ('section', 'chip', 'core'), hops[step])  9.73 us
    ppermute x1, starting transfers between devices, body(): far = lax.ppermute(near, 'core', [(0, 1), (1, 0)])  7.66 us
    all_to_all x1, starting transfers between devices, body(): lax.all_to_all(jnp.broadcast_to(block[None], (chips,) + block.shape), 'ch...  6.9 us
    pallas_call x4, Pallas kernels, body(): local_call(functools.partial(start_kernel, 1 if step == 0 else 2, last),...  6.43 us
    ppermute x4, starting transfers between devices, body(): received = lax.ppermute(outs[step], ('section', 'chip', 'core'), hops[step])  6.42 us
    all_to_all x1, waiting for transfers between devices, body(): lax.all_to_all(jnp.broadcast_to(block[None], (chips,) + block.shape), 'ch...  6.41 us
    all_to_all x1, starting transfers between devices, body(): partials = lax.all_to_all(sent, ('chip', 'core'), 0, 0)  3.65 us
  transfers between devices with their start and end apart: 7, of which 5 were waited for; matrix products, arithmetic and copies ran while one was open for 0% of the time, Pallas kernels for 8%

profile of v4, /device:TPU:97, one launch (start us, length us, event | category | flops | bytes accessed | tf_op | source)
XLA Modules:
  0.0 105.1 jit_solution(11225014151500394684)
XLA Ops:
  0.6 0.0 copy-start.4
  0.6 0.7 slice_select_fusion.2
  1.4 0.0 copy-done.4
  1.4 2.2 %all_gather.15 = bf16[5,32,256]{2,1,0:T(8,128)(2,1)S(1)} all-gather(bf16[5,16,256]{2,1,0:T(8,128)(2,1)S(1)} %pad_maximum_fusion.1), channel_id=1, replica_groups=mesh['section'=16,'chip'=16,'core'=2] {'core'}, dimensions={1}, use_global_device_ids=true | all-gather | bytes 122880 | tf_op jit(solution)/shard_map/all_gather | solution.py:257
  3.6 0.9 broadcast_in_dim.14
  4.5 0.0 copy-start.3
  4.5 6.9 %all-to-all-start = ((bf16[16,5,16,256]{3,2,1,0:T(8,128)(2,1)}), bf16[16,5,16,256]{3,2,1,0:T(8,128)(2,1)S(1)}, u32[]{:S(2)}, u32[]{:S(2)}) async-start(bf16[16,5,16,256]{3,2,1,0:T(8,128)(2,1)} %broadcast_in_dim.14), calls=%async_computation | async-start | bytes 1310720 | tf_op jit(solution)/shard_map/all_to_all | solution.py:265
  11.4 0.0 copy-start.2
  11.4 0.0 copy-done.3
  11.4 0.0 copy-done.5
  11.5 0.0 slice-done.1
  11.5 0.0 slice-done.2
  11.5 2.3 %all_gather.17 = bf16[7,32,256]{2,1,0:T(8,128)(2,1)S(1)} all-gather(bf16[7,16,256]{2,1,0:T(8,128)(2,1)S(1)} %pad_maximum_fusion), channel_id=1, replica_groups=mesh['section'=16,'chip'=16,'core'=2] {'core'}, dimensions={1}, use_global_device_ids=true | all-gather | bytes 172032 | tf_op jit(solution)/shard_map/all_gather | solution.py:273
  13.8 0.6 copy-done
  14.5 0.1 pad_add_fusion.flags
  14.5 0.0 copy-done.2
  14.5 2.6 %all_gather.16.filters = bf16[864,512]{1,0:T(8,128)(2,1)S(1)} all-gather(bf16[432,512]{1,0:T(8,128)(2,1)S(1)} %bitcast.40), channel_id=1, replica_groups=mesh['section'=16,'chip'=16,'core'=2] {'core'}, dimensions={0}, use_global_device_ids=true | all-gather | bytes 1327104 | tf_op jit(solution)/shard_map/all_gather | solution.py:267
  17.1 0.0 copy-done.1
  17.1 0.0 slice-done
  17.1 6.4 %all-to-all-done.near = bf16[16,5,16,256]{3,2,1,0:T(8,128)(2,1)S(1)} async-done(((bf16[16,5,16,256]{3,2,1,0:T(8,128)(2,1)}), bf16[16,5,16,256]{3,2,1,0:T(8,128)(2,1)S(1)}, u32[]{:S(2)}, u32[]{:S(2)}) %all-to-all-start) | async-done | bytes 655392 | tf_op jit(solution)/shard_map/all_to_all | solution.py:265
  23.5 1.5 %shard_map.85 = (bf16[32,256]{1,0:T(8,128)(2,1)S(1)}, f32[32,256]{1,0:T(8,128)S(1)}, f32[32,256]{1,0:T(8,128)S(1)}) custom-call(s32[3]{0:T(128)S(1)} %pad_add_fusion.flags, bf16[16,5,16,256]{3,2,1,0:T(8,128)(2,1)S(1)} %all-to-all-done.near, bf16[864,512]{1,0:T(8,128)(2,1)S(1)} %all_gather.16.filters), custom_call_target="tpu_custom_call" | custom-call | tf_op jit(solution)/shard_map/pallas_call | solution.py:281
  25.1 0.7 collective-permute-start
  25.8 7.7 %collective-permute-start.3 = (bf16[16,5,16,256]{3,2,1,0:T(8,128)(2,1)S(1)}, bf16[16,5,16,256]{3,2,1,0:T(8,128)(2,1)S(1)}, u32[]{:S(2)}, u32[]{:S(2)}) collective-permute-start(bf16[16,5,16,256]{3,2,1,0:T(8,128)(2,1)S(1)} %all-to-all-done.near), channel_id=1, source_target_pairs={{0,1},{1,0},{2,3},{3,2},{4,5},{5,4},{6,7},{7,6},{8,9},{9,8},{10,11... | collective-permute-start | bytes 1966088 | tf_op jit(solution)/shard_map/ppermute | solution.py:291
  33.4 0.0 collective-permute-done.received
  33.5 1.4 %shard_map.86 = (bf16[16,32,256]{2,1,0:T(8,128)(2,1)S(1)}, bf16[32,256]{1,0:T(8,128)(2,1)S(1)}) custom-call(s32[3]{0:T(128)S(1)} %pad_add_fusion.flags, bf16[32,256]{1,0:T(8,128)(2,1)S(1)} %collective-permute-done.received, bf16[32,256]{1,0:T(8,128)(2,1)S(1)} %get-tuple-element.86.outside, f32[32,256]{1,0:T(8,128)S(1)} %get-tuple-element.42.slope, ...), custom_call_target="tpu_custom_call" | custom-call | tf_op jit(solution)/shard_map/pallas_call | solution.py:299
  34.9 11.4 %all_to_all.25.arrived = bf16[16,32,256]{2,1,0:T(8,128)(2,1)S(1)} all-to-all(bf16[16,32,256]{2,1,0:T(8,128)(2,1)S(1)} %get-tuple-element.44), channel_id=1, replica_groups=mesh['section'=16,'chip'=16,'core'=2] {'chip'}, dimensions={0} | all-to-all | bytes 524288 | tf_op jit(solution)/shard_map/all_to_all | solution.py:308
  46.3 0.6 shard_map.87.refs_1_.second
  46.9 1.9 %collective-permute-start.1 = (bf16[32,256]{1,0:T(8,128)(2,1)S(1)}, bf16[32,256]{1,0:T(8,128)(2,1)S(1)}, u32[]{:S(2)}, u32[]{:S(2)}) collective-permute-start(bf16[32,256]{1,0:T(8,128)(2,1)S(1)} %shard_map.87.refs_1_.second), channel_id=1, source_target_pairs={{0,32},{2,34},{4,36},{6,38},{8,40},{10,42},{12,44},{14,46},{16,48}... | collective-permute-start | bytes 49160 | tf_op jit(solution)/shard_map/ppermute | solution.py:289
  48.9 3.8 %collective-permute-done.1.received = bf16[32,256]{1,0:T(8,128)(2,1)S(1)} collective-permute-done((bf16[32,256]{1,0:T(8,128)(2,1)S(1)}, bf16[32,256]{1,0:T(8,128)(2,1)S(1)}, u32[]{:S(2)}, u32[]{:S(2)}) %collective-permute-start.1) | collective-permute-done | bytes 16416 | tf_op jit(solution)/shard_map/ppermute | solution.py:289
  52.6 1.4 %shard_map.88 = (bf16[16,32,256]{2,1,0:T(8,128)(2,1)S(1)}, bf16[32,256]{1,0:T(8,128)(2,1)S(1)}) custom-call(s32[3]{0:T(128)S(1)} %pad_add_fusion.flags, bf16[32,256]{1,0:T(8,128)(2,1)S(1)} %collective-permute-done.1.received, bf16[32,256]{1,0:T(8,128)(2,1)S(1)} %get-tuple-element.85.outside, f32[32,256]{1,0:T(8,128)S(1)} %get-tuple-element.47.slope, ...), custom_call_target="tpu_custom_call" | custom-call | tf_op jit(solution)/shard_map/pallas_call | solution.py:299
  54.1 10.9 %all_to_all.26.arrived = bf16[16,32,256]{2,1,0:T(8,128)(2,1)S(1)} all-to-all(bf16[16,32,256]{2,1,0:T(8,128)(2,1)S(1)} %get-tuple-element.49), channel_id=1, replica_groups=mesh['section'=16,'chip'=16,'core'=2] {'chip'}, dimensions={0} | all-to-all | bytes 524288 | tf_op jit(solution)/shard_map/all_to_all | solution.py:308
  65.0 0.6 shard_map.89.refs_2_.third
  65.6 1.9 %collective-permute-start.2 = (bf16[32,256]{1,0:T(8,128)(2,1)S(1)}, bf16[32,256]{1,0:T(8,128)(2,1)S(1)}, u32[]{:S(2)}, u32[]{:S(2)}) collective-permute-start(bf16[32,256]{1,0:T(8,128)(2,1)S(1)} %shard_map.89.refs_2_.third), channel_id=1, source_target_pairs={{0,32},{2,34},{4,36},{6,38},{8,40},{10,42},{12,44},{14,46},{16,48}... | collective-permute-start | bytes 49160 | tf_op jit(solution)/shard_map/ppermute | solution.py:289
  67.5 0.0 collective-permute-done.3.far
  67.5 1.5 %shard_map.90 = (f32[32,256]{1,0:T(8,128)S(1)}, f32[32,256]{1,0:T(8,128)S(1)}) custom-call(s32[3]{0:T(128)S(1)} %pad_add_fusion.flags, bf16[864,512]{1,0:T(8,128)(2,1)S(1)} %all_gather.16.filters, bf16[16,5,16,256]{3,2,1,0:T(8,128)(2,1)S(1)} %all-to-all-done.near, bf16[16,5,16,256]{3,2,1,0:T(8,128)(2,1)S(1)} %collective-permute-done.3.far), custom_call_target="tpu_custom_call" | custom-call | flops 1 | bytes 1 | tf_op jit(solution)/shard_map/pallas_call | solution.py:293
  69.1 2.2 %collective-permute-done.2.received = bf16[32,256]{1,0:T(8,128)(2,1)S(1)} collective-permute-done((bf16[32,256]{1,0:T(8,128)(2,1)S(1)}, bf16[32,256]{1,0:T(8,128)(2,1)S(1)}, u32[]{:S(2)}, u32[]{:S(2)}) %collective-permute-start.2) | collective-permute-done | bytes 16416 | tf_op jit(solution)/shard_map/ppermute | solution.py:289
  71.3 1.4 %shard_map.91 = (bf16[16,32,256]{2,1,0:T(8,128)(2,1)S(1)}, bf16[32,256]{1,0:T(8,128)(2,1)S(1)}) custom-call(s32[3]{0:T(128)S(1)} %pad_add_fusion.flags, bf16[32,256]{1,0:T(8,128)(2,1)S(1)} %collective-permute-done.2.received, bf16[32,256]{1,0:T(8,128)(2,1)S(1)} %get-tuple-element.84.outside, f32[32,256]{1,0:T(8,128)S(1)} %get-tuple-element.57.slope, ...), custom_call_target="tpu_custom_call" | custom-call | tf_op jit(solution)/shard_map/pallas_call | solution.py:299
  72.7 10.4 %all_to_all.27.arrived = bf16[16,32,256]{2,1,0:T(8,128)(2,1)S(1)} all-to-all(bf16[16,32,256]{2,1,0:T(8,128)(2,1)S(1)} %get-tuple-element.58), channel_id=1, replica_groups=mesh['section'=16,'chip'=16,'core'=2] {'chip'}, dimensions={0} | all-to-all | bytes 524288 | tf_op jit(solution)/shard_map/all_to_all | solution.py:308
  83.1 0.6 shard_map.92.refs_3_.fourth
  83.7 1.9 %collective-permute-start.4 = (bf16[32,256]{1,0:T(8,128)(2,1)S(1)}, bf16[32,256]{1,0:T(8,128)(2,1)S(1)}, u32[]{:S(2)}, u32[]{:S(2)}) collective-permute-start(bf16[32,256]{1,0:T(8,128)(2,1)S(1)} %shard_map.92.refs_3_.fourth), channel_id=1, source_target_pairs={{33,1},{35,3},{37,5},{39,7},{41,9},{43,11},{45,13},{47,15},{49,17}... | collective-permute-start | bytes 49160 | tf_op jit(solution)/shard_map/ppermute | solution.py:289
  85.7 3.8 %collective-permute-done.4.received = bf16[32,256]{1,0:T(8,128)(2,1)S(1)} collective-permute-done((bf16[32,256]{1,0:T(8,128)(2,1)S(1)}, bf16[32,256]{1,0:T(8,128)(2,1)S(1)}, u32[]{:S(2)}, u32[]{:S(2)}) %collective-permute-start.4) | collective-permute-done | bytes 16416 | tf_op jit(solution)/shard_map/ppermute | solution.py:289
  89.4 2.1 %shard_map.93 = (bf16[32,16,256]{2,1,0:T(8,128)(2,1)}, bf16[32,256]{1,0:T(8,128)(2,1)S(1)}) custom-call(s32[3]{0:T(128)S(1)} %pad_add_fusion.flags, bf16[32,256]{1,0:T(8,128)(2,1)S(1)} %collective-permute-done.4.received, bf16[32,256]{1,0:T(8,128)(2,1)S(1)} %get-tuple-element.83.outside, f32[32,256]{1,0:T(8,128)S(1)} %get-tuple-element.61.slope, ...), custom_call_target="tpu_custom_call" | custom-call | tf_op jit(solution)/shard_map/pallas_call | solution.py:299
  91.6 3.7 %all-to-all-start.4 = ((bf16[32,16,256]{2,1,0:T(8,128)(2,1)}), bf16[32,16,256]{2,1,0:T(8,128)(2,1)S(1)}, u32[]{:S(2)}, u32[]{:S(2)}) async-start(bf16[32,16,256]{2,1,0:T(8,128)(2,1)} %get-tuple-element.73), calls=%async_computation.4 | async-start | bytes 524288 | tf_op jit(solution)/shard_map/all_to_all | solution.py:312
  95.2 0.6 shard_map.94
  95.8 1.9 %all-gather = bf16[14,16,256]{2,1,0:T(8,128)(2,1)S(1)} all-gather(bf16[7,16,256]{2,1,0:T(8,128)(2,1)S(1)} %shard_map.94), channel_id=2, replica_groups=mesh['section'=16,'chip'=16,'core'=2] {'core'}, dimensions={0}, use_global_device_ids=true | all-gather | bytes 172032 | tf_op jit(solution)/shard_map/all_gather | solution.py:316
  97.7 2.7 %shard_map.95 = (f32[432,512]{1,0:T(8,128)}, bf16[4,16,256]{2,1,0:T(8,128)(2,1)}) custom-call(s32[3]{0:T(128)S(1)} %pad_add_fusion.flags, bf16[16,5,16,256]{3,2,1,0:T(8,128)(2,1)S(1)} %all-to-all-done.near, bf16[16,5,16,256]{3,2,1,0:T(8,128)(2,1)S(1)} %collective-permute-done.3.far, bf16[2,7,16,256]{3,2,1,0:T(8,128)(2,1)S(1)} %bitcast.38, ...), custom_call_target="tpu_custom_call" | custom-call | flops 1 | bytes 1 | tf_op jit(solution)/shard_map/pallas_call | solution.py:317
  100.4 3.5 %all-to-all-done.4.arrived = bf16[32,16,256]{2,1,0:T(8,128)(2,1)S(1)} async-done(((bf16[32,16,256]{2,1,0:T(8,128)(2,1)}), bf16[32,16,256]{2,1,0:T(8,128)(2,1)S(1)}, u32[]{:S(2)}, u32[]{:S(2)}) %all-to-all-start.4) | async-done | bytes 262176 | tf_op jit(solution)/shard_map/all_to_all | solution.py:312
  103.9 1.2 %shard_map.96 = bf16[4,16,256]{2,1,0:T(8,128)(2,1)} custom-call(s32[3]{0:T(128)S(1)} %pad_add_fusion.flags, bf16[32,16,256]{2,1,0:T(8,128)(2,1)S(1)} %all-to-all-done.4.arrived, bf16[2,7,16,256]{3,2,1,0:T(8,128)(2,1)S(1)} %bitcast.39, bf16[32,256]{1,0:T(8,128)(2,1)S(1)} %shard_map.87.refs_1_.second, bf16[32,256]{1,0:T(8,128)(2,1)S(1)} %shard_map.89.refs_2_.third, ...), custom_call_target="tpu_custom_call" | custom-call | tf_op jit(solution)/shard_map/pallas_call | solution.py:325
  (15 shorter events, 0.1 us)
Async XLA Ops:
  0.6 0.8 copy-start.4
  4.5 6.9 %copy-start.3 = (bf16[4,16,256]{2,1,0:T(8,128)(2,1)S(1)}, bf16[4,16,256]{2,1,0:T(8,128)(2,1)}, u32[]{:S(2)}) copy-start(bf16[4,16,256]{2,1,0:T(8,128)(2,1)} %param.11) | copy-start | bytes 98308
  4.5 6.9 %copy-start.5 = (bf16[1,16,256]{2,1,0:T(8,128)(2,1)S(1)}, bf16[1,16,256]{2,1,0:T(8,128)(2,1)}, u32[]{:S(2)}) copy-start(bf16[1,16,256]{2,1,0:T(8,128)(2,1)} %param.8) | copy-start | bytes 24580
  4.5 7.0 %slice-start.1 = ((bf16[4,16,256]{2,1,0:T(8,128)(2,1)}), bf16[3,16,256]{2,1,0:T(8,128)(2,1)S(1)}, s32[]{:S(2)}) async-start(bf16[4,16,256]{2,1,0:T(8,128)(2,1)} %param.6), calls=%async_computation.6 | async-start | bytes 49152 | tf_op jit(solution)/shard_map/slice | solution.py:271
  4.5 7.0 %slice-start.2 = ((bf16[4,16,256]{2,1,0:T(8,128)(2,1)}), bf16[3,16,256]{2,1,0:T(8,128)(2,1)S(1)}, s32[]{:S(2)}) async-start(bf16[4,16,256]{2,1,0:T(8,128)(2,1)} %param.11), calls=%async_computation.7 | async-start | bytes 49152 | tf_op jit(solution)/shard_map/slice | solution.py:271
  4.5 19.0 %all-to-all-start = ((bf16[16,5,16,256]{3,2,1,0:T(8,128)(2,1)}), bf16[16,5,16,256]{3,2,1,0:T(8,128)(2,1)S(1)}, u32[]{:S(2)}, u32[]{:S(2)}) async-start(bf16[16,5,16,256]{3,2,1,0:T(8,128)(2,1)} %broadcast_in_dim.14), calls=%async_computation | async-start | bytes 1310720 | tf_op jit(solution)/shard_map/all_to_all | solution.py:265
  11.4 3.1 %copy-start.2 = (bf16[1,16,27,512]{3,1,2,0:T(8,128)(2,1)S(1)}, bf16[1,16,27,512]{3,1,2,0:T(8,128)(2,1)}, u32[]{:S(2)}) copy-start(bf16[1,16,27,512]{3,1,2,0:T(8,128)(2,1)} %param.10) | copy-start | bytes 1327108
  13.8 0.6 copy-start
  14.5 2.6 %copy-start.1 = (bf16[7,32,256]{2,1,0:T(8,128)(2,1)S(1)}, bf16[7,32,256]{2,1,0:T(8,128)(2,1)}, u32[]{:S(2)}) copy-start(bf16[7,32,256]{2,1,0:T(8,128)(2,1)} %copy-done) | copy-start | bytes 344068
  14.5 2.6 %slice-start = ((bf16[7,32,256]{2,1,0:T(8,128)(2,1)}), bf16[3,32,256]{2,1,0:T(8,128)(2,1)S(1)}, s32[]{:S(2)}) async-start(bf16[7,32,256]{2,1,0:T(8,128)(2,1)} %copy-done), calls=%async_computation.5 | async-start | bytes 98304 | tf_op jit(solution)/shard_map/slice | solution.py:274
  25.1 8.4 %collective-permute-start = (bf16[32,256]{1,0:T(8,128)(2,1)S(1)}, bf16[32,256]{1,0:T(8,128)(2,1)S(1)}, u32[]{:S(2)}, u32[]{:S(2)}) collective-permute-start(bf16[32,256]{1,0:T(8,128)(2,1)S(1)} %get-tuple-element.41.refs_0_), channel_id=1, source_target_pairs={{0,32},{2,34},{4,36},{6,38},{8,40},{10,42},{12,44},{14,46},{16,48}... | collective-permute-start | bytes 49160 | tf_op jit(solution)/shard_map/ppermute | solution.py:289
  25.8 41.8 %collective-permute-start.3 = (bf16[16,5,16,256]{3,2,1,0:T(8,128)(2,1)S(1)}, bf16[16,5,16,256]{3,2,1,0:T(8,128)(2,1)S(1)}, u32[]{:S(2)}, u32[]{:S(2)}) collective-permute-start(bf16[16,5,16,256]{3,2,1,0:T(8,128)(2,1)S(1)} %all-to-all-done.near), channel_id=1, source_target_pairs={{0,1},{1,0},{2,3},{3,2},{4,5},{5,4},{6,7},{7,6},{8,9},{9,8},{10,11... | collective-permute-start | bytes 1966088 | tf_op jit(solution)/shard_map/ppermute | solution.py:291
  46.9 5.7 %collective-permute-start.1 = (bf16[32,256]{1,0:T(8,128)(2,1)S(1)}, bf16[32,256]{1,0:T(8,128)(2,1)S(1)}, u32[]{:S(2)}, u32[]{:S(2)}) collective-permute-start(bf16[32,256]{1,0:T(8,128)(2,1)S(1)} %shard_map.87.refs_1_.second), channel_id=1, source_target_pairs={{0,32},{2,34},{4,36},{6,38},{8,40},{10,42},{12,44},{14,46},{16,48}... | collective-permute-start | bytes 49160 | tf_op jit(solution)/shard_map/ppermute | solution.py:289
  65.6 5.7 %collective-permute-start.2 = (bf16[32,256]{1,0:T(8,128)(2,1)S(1)}, bf16[32,256]{1,0:T(8,128)(2,1)S(1)}, u32[]{:S(2)}, u32[]{:S(2)}) collective-permute-start(bf16[32,256]{1,0:T(8,128)(2,1)S(1)} %shard_map.89.refs_2_.third), channel_id=1, source_target_pairs={{0,32},{2,34},{4,36},{6,38},{8,40},{10,42},{12,44},{14,46},{16,48}... | collective-permute-start | bytes 49160 | tf_op jit(solution)/shard_map/ppermute | solution.py:289
  83.7 5.7 %collective-permute-start.4 = (bf16[32,256]{1,0:T(8,128)(2,1)S(1)}, bf16[32,256]{1,0:T(8,128)(2,1)S(1)}, u32[]{:S(2)}, u32[]{:S(2)}) collective-permute-start(bf16[32,256]{1,0:T(8,128)(2,1)S(1)} %shard_map.92.refs_3_.fourth), channel_id=1, source_target_pairs={{33,1},{35,3},{37,5},{39,7},{41,9},{43,11},{45,13},{47,15},{49,17}... | collective-permute-start | bytes 49160 | tf_op jit(solution)/shard_map/ppermute | solution.py:289
  91.6 12.3 %all-to-all-start.4 = ((bf16[32,16,256]{2,1,0:T(8,128)(2,1)}), bf16[32,16,256]{2,1,0:T(8,128)(2,1)S(1)}, u32[]{:S(2)}, u32[]{:S(2)}) async-start(bf16[32,16,256]{2,1,0:T(8,128)(2,1)} %get-tuple-element.73), calls=%async_computation.4 | async-start | bytes 524288 | tf_op jit(solution)/shard_map/all_to_all | solution.py:312

commit v5 on v4

--- a/solution.py
+++ b/solution.py
@@ -84,29 +84,29 @@
     return whole[...]
 
 
-def first_kernel(flags, near, filters, act, first, second, taps):
+def first_kernel(near, filters, act, first, second, taps):
     where = coordinates(OWN)
 
-    @pl.when(flags[0] == 0)
+    @pl.when(lax.axis_index("core") == 0)
     def _():
         silu_into(act, filters, near[:, 0:2], taps, where)
         for slope in (first, second):
             slope[...] = jnp.zeros_like(slope)
 
-    @pl.when(flags[0] != 0)
+    @pl.when(lax.axis_index("core") != 0)
     def _():
         act[...] = jnp.zeros_like(act)
         slope_into(first, filters, near[:, 0:2], taps, where)
         slope_into(second, filters, near[:, 2:4], taps, where)
 
 
-def slope_kernel(flags, filters, near, far, third, fourth, taps, whole):
-    @pl.when(flags[0] == 0)
+def slope_kernel(filters, near, far, third, fourth, taps, whole):
+    @pl.when(lax.axis_index("core") == 0)
     def _():
         for slope in (third, fourth):
             slope[...] = jnp.zeros_like(slope)
 
-    @pl.when(flags[0] != 0)
+    @pl.when(lax.axis_index("core") != 0)
     def _():
         where = coordinates(OWN)
         slope_into(third, filters, far[:, 2:4], taps, where)
@@ -120,48 +120,52 @@
     out[...] = total.astype(jnp.bfloat16)
 
 
-def finish_kernel(flags, arrived, filters, out, taps):
-    @pl.when(flags[0] == 0)
+def finish_kernel(arrived, filters, out, taps):
+    @pl.when(lax.axis_index("core") == 0)
     def _():
         silu_into(out, filters, arrived[...], taps, coordinates(OWN))
 
-    @pl.when(flags[0] != 0)
+    @pl.when(lax.axis_index("core") != 0)
     def _():
         sum_into(out, arrived)
 
 
-def pack_kernel(flags, *refs):
+def pack_kernel(*refs):
     outs, dpres, parcel = refs[:4], refs[4:8], refs[8]
 
-    @pl.when(flags[0] == 0)
+    @pl.when(lax.axis_index("core") == 0)
     def _():
         for r, pair in enumerate(outs):
             parcel[r] = pair[OWN:, :]
         for r in range(ROUNDS - 1):
             parcel[ROUNDS + r] = jnp.zeros((OWN, CELLS), jnp.bfloat16)
 
-    @pl.when(flags[0] != 0)
+    @pl.when(lax.axis_index("core") != 0)
     def _():
         for r, pair in enumerate((*dpres, *outs[1:])):
             parcel[r] = pair[:OWN, :]
 
 
-def last_kernel(flags, arrived, parcels, second, third, fourth, grads):
+def last_kernel(arrived, parcels, second, third, fourth, grads):
     for r, pair in enumerate((second, third, fourth)):
         odd = pair[OWN:, :].astype(jnp.float32)
         even = parcels[1, ROUNDS + r].astype(jnp.float32)
-        grads[r] = jnp.where(flags[0] == 0, even, odd).astype(jnp.bfloat16)
+        grads[r] = jnp.where(lax.axis_index("core") == 0, even, odd).astype(jnp.bfloat16)
     total = arrived[1].astype(jnp.float32)
     for d in range(3, arrived.shape[0], 2):
         total = total + arrived[d].astype(jnp.float32)
     grads[ROUNDS - 1] = total.astype(jnp.bfloat16)
 
 
-def start_kernel(edge_slot, last, flags, received, outside, slope, filters, sent, dpre, spread):
-    take = flags[edge_slot] != 0
+def start_kernel(step, received, outside, slope, filters, sent, dpre, spread):
+    last = step + 1 == ROUNDS
+    section = lax.axis_index("section")
+    edge = section == lax.axis_size("section") - 1
+    backward_edge = True if step == 0 else edge
+    take = jnp.where(lax.axis_index("core") == 0, section == 0, backward_edge)
     value = jnp.where(take, outside[...].astype(jnp.float32), received[...].astype(jnp.float32))
 
-    @pl.when(flags[0] == 0)
+    @pl.when(lax.axis_index("core") == 0)
     def _():
         copy = value.astype(jnp.bfloat16)
         dpre[...] = copy
@@ -171,7 +175,7 @@
             for p in range(sent.shape[0]):
                 sent[p] = copy
 
-    @pl.when(flags[0] != 0)
+    @pl.when(lax.axis_index("core") != 0)
     def _():
         where = coordinates(OWN)
         rounded = (value * slope[...]).astype(jnp.bfloat16)
@@ -185,7 +189,7 @@
         sent[...] = part.astype(jnp.bfloat16).reshape(sent.shape)
 
 
-def filter_kernel(flags, near, far, parcels, *refs):
+def filter_kernel(near, far, parcels, *refs):
     acts_pair, dpres, (out, acts, spread, whole) = refs[:4], refs[4:8], refs[8:]
 
     def total(even, odd, act_of, dpre_of):
@@ -210,18 +214,17 @@
             else:
                 out[...] += term
 
-    @pl.when(flags[0] == 0)
+    @pl.when(lax.axis_index("core") == 0)
     def _():
         total(near, far, lambda r: acts_pair[r][:OWN, :], lambda r: parcels[1, r])
 
-    @pl.when(flags[0] != 0)
+    @pl.when(lax.axis_index("core") != 0)
     def _():
         total(far, near, lambda r: parcels[0, r], lambda r: dpres[r][OWN:, :])
 
 
-def local_call(kernel, outs, kinds, scratch, cost=None):
-    spaces = {"s": pltpu.SMEM, "v": pltpu.VMEM}
-    specs = [pl.BlockSpec(memory_space=spaces[kind]) for kind in kinds]
+def local_call(kernel, outs, count, scratch, cost=None):
+    specs = [pl.BlockSpec(memory_space=pltpu.VMEM)] * count
     result = jax.tree.map(lambda _: pl.BlockSpec(memory_space=pltpu.VMEM), outs)
     return pl.pallas_call(
         kernel,
@@ -243,9 +246,6 @@
     section = lax.axis_index("section")
     core = lax.axis_index("core")
     forward = core == 0
-    at_edge = jnp.where(forward, section == 0, section == sections - 1)
-    from_outside = jnp.where(forward, section == 0, True)
-    flags = jnp.stack([core, from_outside.astype(jnp.int32), at_edge.astype(jnp.int32)]).astype(jnp.int32)
     ahead, behind = [], []
     for s in range(sections - 1):
         for p in range(chips):
@@ -278,8 +278,8 @@
     whole_scratch = pltpu.VMEM((chips, 2, OWN, CELLS), jnp.bfloat16)
     mine, slope_shape = shape((PAIR, CELLS)), shape((PAIR, CELLS), jnp.float32)
 
-    act, *slopes = local_call(first_kernel, (mine, slope_shape, slope_shape), "svv", [taps_scratch])(
-        flags, near, filters
+    act, *slopes = local_call(first_kernel, (mine, slope_shape, slope_shape), 2, [taps_scratch])(
+        near, filters
     )
     after = lax.optimization_barrier
     outs, dpres = [act], []
@@ -290,40 +290,40 @@
         if step == 0:
             far = lax.ppermute(near, "core", [(0, 1), (1, 0)])
         elif step == 2:
-            rest = local_call(slope_kernel, (slope_shape,) * 2, "svvv", [taps_scratch, whole_scratch], LIGHT)(
-                flags, filters, near, far
+            rest = local_call(slope_kernel, (slope_shape,) * 2, 3, [taps_scratch, whole_scratch], LIGHT)(
+                filters, near, far
             )
             received, *rest = after((received, *rest))
             slopes.extend(rest)
         sent_shape = shape((2 * chips, OWN, CELLS) if last else (chips, PAIR, CELLS))
         sent, dpre = local_call(
-            functools.partial(start_kernel, 1 if step == 0 else 2, last),
+            functools.partial(start_kernel, step),
             (sent_shape, mine),
-            "svvvv",
+            4,
             [spread_scratch],
-        )(flags, received, outside[step], slopes[step], filters)
+        )(received, outside[step], slopes[step], filters)
         dpres.append(dpre)
         if last:
             break
         arrived = lax.all_to_all(sent, "chip", 0, 0)
-        outs.append(local_call(finish_kernel, mine, "svv", [taps_scratch])(flags, arrived, filters))
+        outs.append(local_call(finish_kernel, mine, 2, [taps_scratch])(arrived, filters))
 
     sent, *dpres = after((sent, *dpres))
     partials = lax.all_to_all(sent, ("chip", "core"), 0, 0)
-    parcel = local_call(pack_kernel, shape((2 * ROUNDS - 1, OWN, CELLS)), "s" + "v" * 8, [], LIGHT)(
-        flags, *outs, *dpres
+    parcel = local_call(pack_kernel, shape((2 * ROUNDS - 1, OWN, CELLS)), 8, [], LIGHT)(
+        *outs, *dpres
     )
     parcels = lax.all_gather(parcel, "core", axis=0)
     filter_grad, acts = local_call(
         filter_kernel,
         (shape((ROWS, CHANNELS), jnp.float32), shape((ROUNDS, OWN, CELLS))),
-        "svvv" + "v" * 8,
+        11,
         [pltpu.VMEM((ROWS, CELLS), jnp.bfloat16), whole_scratch],
         LIGHT,
-    )(flags, near, far, parcels, *outs, *dpres)
+    )(near, far, parcels, *outs, *dpres)
     partials, filter_grad = lax.optimization_barrier((partials, filter_grad))
-    grads = local_call(last_kernel, shape((ROUNDS, OWN, CELLS)), "svvvvv", [])(
-        flags, partials, parcels, *outs[1:]
+    grads = local_call(last_kernel, shape((ROUNDS, OWN, CELLS)), 5, [])(
+        partials, parcels, *outs[1:]
     )
     filter_grad = jnp.transpose(filter_grad.reshape(TAPS, OWN, CHANNELS), (1, 0, 2))
     return acts[None], grads[None], filter_grad[None]

time: 106 us -> 101 us (0.953)
  Pallas kernels: 15.8 us -> 9.25 us
  waiting for transfers between devices: 19.6 us -> 21.3 us
    pallas_call x11, Pallas kernels: 13 us -> 7.05 us  [the longest x4 4.25 us: body(): local_call(functools.partial(start_kernel, step), (sent_shape, mine), 4,...]
    all_to_all x1, waiting for transfers between devices: 3.46 us -> 4.57 us  [body(): partials = lax.all_to_all(sent, ('chip', 'core'), 0, 0)]
  transfers between devices with their start and end apart: 7 -> 7, of which waited for: 5 -> 5; matrix products, arithmetic and copies ran while one was open for 0% -> 0% of each run, Pallas kernels for 8% -> 5%
where the time goes in v5:
time: 101 us; the launch traced here: 100 us
  blocking collectives  41.7 us (41%)
  starting transfers between devices  24.6 us (24%)
  waiting for transfers between devices  21.3 us (21%)
  Pallas kernels  9.25 us (9%)
  local copies, waits for them, and re-layouts  1.59 us (2%)
    all_to_all x3, blocking collectives, body(): arrived = lax.all_to_all(sent, 'chip', 0, 0)  32.8 us
    ppermute x4, waiting for transfers between devices, body(): received = lax.ppermute(outs[step], ('section', 'chip', 'core'), hops[step])  10.3 us
    ppermute x1, starting transfers between devices, body(): far = lax.ppermute(near, 'core', [(0, 1), (1, 0)])  7.66 us
    all_to_all x1, starting transfers between devices, body(): lax.all_to_all(jnp.broadcast_to(block[None], (chips,) + block.shape), 'ch...  6.9 us
    all_to_all x1, waiting for transfers between devices, body(): lax.all_to_all(jnp.broadcast_to(block[None], (chips,) + block.shape), 'ch...  6.5 us
    ppermute x4, starting transfers between devices, body(): received = lax.ppermute(outs[step], ('section', 'chip', 'core'), hops[step])  6.42 us
    all_to_all x1, waiting for transfers between devices, body(): partials = lax.all_to_all(sent, ('chip', 'core'), 0, 0)  4.57 us
    pallas_call x4, Pallas kernels, body(): local_call(functools.partial(start_kernel, step), (sent_shape, mine), 4,...  4.25 us
  transfers between devices with their start and end apart: 7, of which 5 were waited for; matrix products, arithmetic and copies ran while one was open for 0% of the time, Pallas kernels for 5%

profile of v5, /device:TPU:97, one launch (start us, length us, event | category | flops | bytes accessed | tf_op | source)
XLA Modules:
  0.0 100.1 jit_solution(284297883773322905)
XLA Ops:
  0.6 0.0 copy-start.4
  0.6 0.7 slice_select_fusion.2
  1.4 0.0 copy-done.4
  1.4 2.2 %all_gather.15 = bf16[5,32,256]{2,1,0:T(8,128)(2,1)S(1)} all-gather(bf16[5,16,256]{2,1,0:T(8,128)(2,1)S(1)} %pad_maximum_fusion.1), channel_id=1, replica_groups=mesh['section'=16,'chip'=16,'core'=2] {'core'}, dimensions={1}, use_global_device_ids=true | all-gather | bytes 122880 | tf_op jit(solution)/shard_map/all_gather | solution.py:257
  3.6 0.9 broadcast_in_dim.14
  4.5 0.0 copy-start.3
  4.5 0.0 copy-start.5
  4.5 0.0 slice-start.1
  4.5 0.0 slice-start.2
  4.5 6.9 %all-to-all-start = ((bf16[16,5,16,256]{3,2,1,0:T(8,128)(2,1)}), bf16[16,5,16,256]{3,2,1,0:T(8,128)(2,1)S(1)}, u32[]{:S(2)}, u32[]{:S(2)}) async-start(bf16[16,5,16,256]{3,2,1,0:T(8,128)(2,1)} %broadcast_in_dim.14), calls=%async_computation | async-start | bytes 1310720 | tf_op jit(solution)/shard_map/all_to_all | solution.py:265
  11.4 0.0 copy-start.2
  11.4 0.0 copy-done.3
  11.4 0.0 copy-done.5
  11.5 0.0 slice-done.1
  11.5 0.0 slice-done.2
  11.5 2.3 %all_gather.17 = bf16[7,32,256]{2,1,0:T(8,128)(2,1)S(1)} all-gather(bf16[7,16,256]{2,1,0:T(8,128)(2,1)S(1)} %pad_maximum_fusion), channel_id=1, replica_groups=mesh['section'=16,'chip'=16,'core'=2] {'core'}, dimensions={1}, use_global_device_ids=true | all-gather | bytes 172032 | tf_op jit(solution)/shard_map/all_gather | solution.py:273
  13.8 0.0 copy-start
  13.8 0.6 copy-done
  14.4 0.0 copy-done.2
  14.5 0.0 copy-start.1
  14.5 2.6 %all_gather.16.filters = bf16[864,512]{1,0:T(8,128)(2,1)S(1)} all-gather(bf16[432,512]{1,0:T(8,128)(2,1)S(1)} %bitcast.37), channel_id=1, replica_groups=mesh['section'=16,'chip'=16,'core'=2] {'core'}, dimensions={0}, use_global_device_ids=true | all-gather | bytes 1327104 | tf_op jit(solution)/shard_map/all_gather | solution.py:267
  17.0 0.0 copy-done.1
  17.0 0.0 slice-done
  17.0 6.5 %all-to-all-done.near = bf16[16,5,16,256]{3,2,1,0:T(8,128)(2,1)S(1)} async-done(((bf16[16,5,16,256]{3,2,1,0:T(8,128)(2,1)}), bf16[16,5,16,256]{3,2,1,0:T(8,128)(2,1)S(1)}, u32[]{:S(2)}, u32[]{:S(2)}) %all-to-all-start) | async-done | bytes 655392 | tf_op jit(solution)/shard_map/all_to_all | solution.py:265
  23.5 1.0 shard_map.85
  24.5 0.7 collective-permute-start
  25.2 7.7 %collective-permute-start.3 = (bf16[16,5,16,256]{3,2,1,0:T(8,128)(2,1)S(1)}, bf16[16,5,16,256]{3,2,1,0:T(8,128)(2,1)S(1)}, u32[]{:S(2)}, u32[]{:S(2)}) collective-permute-start(bf16[16,5,16,256]{3,2,1,0:T(8,128)(2,1)S(1)} %all-to-all-done.near), channel_id=1, source_target_pairs={{0,1},{1,0},{2,3},{3,2},{4,5},{5,4},{6,7},{7,6},{8,9},{9,8},{10,11... | collective-permute-start | bytes 1966088 | tf_op jit(solution)/shard_map/ppermute | solution.py:291
  32.9 0.0 collective-permute-done.received
  32.9 0.9 shard_map.86
  33.8 11.5 %all_to_all.25.arrived = bf16[16,32,256]{2,1,0:T(8,128)(2,1)S(1)} all-to-all(bf16[16,32,256]{2,1,0:T(8,128)(2,1)S(1)} %get-tuple-element.44), channel_id=1, replica_groups=mesh['section'=16,'chip'=16,'core'=2] {'chip'}, dimensions={0} | all-to-all | bytes 524288 | tf_op jit(solution)/shard_map/all_to_all | solution.py:308
  45.3 1.9 %collective-permute-start.1 = (bf16[32,256]{1,0:T(8,128)(2,1)S(1)}, bf16[32,256]{1,0:T(8,128)(2,1)S(1)}, u32[]{:S(2)}, u32[]{:S(2)}) collective-permute-start(bf16[32,256]{1,0:T(8,128)(2,1)S(1)} %shard_map.87.refs_1_.second), channel_id=1, source_target_pairs={{0,32},{2,34},{4,36},{6,38},{8,40},{10,42},{12,44},{14,46},{16,48}... | collective-permute-start | bytes 49160 | tf_op jit(solution)/shard_map/ppermute | solution.py:289
  47.2 3.8 %collective-permute-done.1.received = bf16[32,256]{1,0:T(8,128)(2,1)S(1)} collective-permute-done((bf16[32,256]{1,0:T(8,128)(2,1)S(1)}, bf16[32,256]{1,0:T(8,128)(2,1)S(1)}, u32[]{:S(2)}, u32[]{:S(2)}) %collective-permute-start.1) | collective-permute-done | bytes 16416 | tf_op jit(solution)/shard_map/ppermute | solution.py:289
  51.0 0.9 shard_map.88
  51.9 10.9 %all_to_all.26.arrived = bf16[16,32,256]{2,1,0:T(8,128)(2,1)S(1)} all-to-all(bf16[16,32,256]{2,1,0:T(8,128)(2,1)S(1)} %get-tuple-element.49), channel_id=1, replica_groups=mesh['section'=16,'chip'=16,'core'=2] {'chip'}, dimensions={0} | all-to-all | bytes 524288 | tf_op jit(solution)/shard_map/all_to_all | solution.py:308
  62.9 1.9 %collective-permute-start.2 = (bf16[32,256]{1,0:T(8,128)(2,1)S(1)}, bf16[32,256]{1,0:T(8,128)(2,1)S(1)}, u32[]{:S(2)}, u32[]{:S(2)}) collective-permute-start(bf16[32,256]{1,0:T(8,128)(2,1)S(1)} %shard_map.89.refs_2_.third), channel_id=1, source_target_pairs={{0,32},{2,34},{4,36},{6,38},{8,40},{10,42},{12,44},{14,46},{16,48}... | collective-permute-start | bytes 49160 | tf_op jit(solution)/shard_map/ppermute | solution.py:289
  64.8 0.0 collective-permute-done.3.far
  64.8 1.0 %shard_map.90 = (f32[32,256]{1,0:T(8,128)S(1)}, f32[32,256]{1,0:T(8,128)S(1)}) custom-call(bf16[864,512]{1,0:T(8,128)(2,1)S(1)} %all_gather.16.filters, bf16[16,5,16,256]{3,2,1,0:T(8,128)(2,1)S(1)} %all-to-all-done.near, bf16[16,5,16,256]{3,2,1,0:T(8,128)(2,1)S(1)} %collective-permute-done.3.far), custom_call_target="tpu_custom_call" | custom-call | flops 1 | bytes 1 | tf_op jit(solution)/shard_map/pallas_call | solution.py:293
  65.8 2.7 %collective-permute-done.2.received = bf16[32,256]{1,0:T(8,128)(2,1)S(1)} collective-permute-done((bf16[32,256]{1,0:T(8,128)(2,1)S(1)}, bf16[32,256]{1,0:T(8,128)(2,1)S(1)}, u32[]{:S(2)}, u32[]{:S(2)}) %collective-permute-start.2) | collective-permute-done | bytes 16416 | tf_op jit(solution)/shard_map/ppermute | solution.py:289
  68.6 0.9 shard_map.91
  69.4 10.4 %all_to_all.27.arrived = bf16[16,32,256]{2,1,0:T(8,128)(2,1)S(1)} all-to-all(bf16[16,32,256]{2,1,0:T(8,128)(2,1)S(1)} %get-tuple-element.58), channel_id=1, replica_groups=mesh['section'=16,'chip'=16,'core'=2] {'chip'}, dimensions={0} | all-to-all | bytes 524288 | tf_op jit(solution)/shard_map/all_to_all | solution.py:308
  79.9 1.9 %collective-permute-start.4 = (bf16[32,256]{1,0:T(8,128)(2,1)S(1)}, bf16[32,256]{1,0:T(8,128)(2,1)S(1)}, u32[]{:S(2)}, u32[]{:S(2)}) collective-permute-start(bf16[32,256]{1,0:T(8,128)(2,1)S(1)} %shard_map.92.refs_3_.fourth), channel_id=1, source_target_pairs={{33,1},{35,3},{37,5},{39,7},{41,9},{43,11},{45,13},{47,15},{49,17}... | collective-permute-start | bytes 49160 | tf_op jit(solution)/shard_map/ppermute | solution.py:289
  81.8 3.8 %collective-permute-done.4.received = bf16[32,256]{1,0:T(8,128)(2,1)S(1)} collective-permute-done((bf16[32,256]{1,0:T(8,128)(2,1)S(1)}, bf16[32,256]{1,0:T(8,128)(2,1)S(1)}, u32[]{:S(2)}, u32[]{:S(2)}) %collective-permute-start.4) | collective-permute-done | bytes 16416 | tf_op jit(solution)/shard_map/ppermute | solution.py:289
  85.6 1.6 %shard_map.93 = (bf16[32,16,256]{2,1,0:T(8,128)(2,1)}, bf16[32,256]{1,0:T(8,128)(2,1)S(1)}) custom-call(bf16[32,256]{1,0:T(8,128)(2,1)S(1)} %collective-permute-done.4.received, bf16[32,256]{1,0:T(8,128)(2,1)S(1)} %get-tuple-element.83.outside, f32[32,256]{1,0:T(8,128)S(1)} %get-tuple-element.61.slope, bf16[864,512]{1,0:T(8,128)(2,1)S(1)} %all_gather.16.filters), custom_call_target="tpu_custom_call" | custom-call | tf_op jit(solution)/shard_map/pallas_call | solution.py:299
  87.1 3.7 %all-to-all-start.4 = ((bf16[32,16,256]{2,1,0:T(8,128)(2,1)}), bf16[32,16,256]{2,1,0:T(8,128)(2,1)S(1)}, u32[]{:S(2)}, u32[]{:S(2)}) async-start(bf16[32,16,256]{2,1,0:T(8,128)(2,1)} %get-tuple-element.73), calls=%async_computation.4 | async-start | bytes 524288 | tf_op jit(solution)/shard_map/all_to_all | solution.py:312
  90.8 1.9 %all-gather = bf16[14,16,256]{2,1,0:T(8,128)(2,1)S(1)} all-gather(bf16[7,16,256]{2,1,0:T(8,128)(2,1)S(1)} %shard_map.94), channel_id=2, replica_groups=mesh['section'=16,'chip'=16,'core'=2] {'core'}, dimensions={0}, use_global_device_ids=true | all-gather | bytes 172032 | tf_op jit(solution)/shard_map/all_gather | solution.py:316
  92.7 2.2 %shard_map.95 = (f32[432,512]{1,0:T(8,128)}, bf16[4,16,256]{2,1,0:T(8,128)(2,1)}) custom-call(bf16[16,5,16,256]{3,2,1,0:T(8,128)(2,1)S(1)} %all-to-all-done.near, bf16[16,5,16,256]{3,2,1,0:T(8,128)(2,1)S(1)} %collective-permute-done.3.far, bf16[2,7,16,256]{3,2,1,0:T(8,128)(2,1)S(1)} %bitcast.35, bf16[32,256]{1,0:T(8,128)(2,1)S(1)} %get-tuple-element.41.refs_0_, ...), custom_call_target="tpu_custom_call" | custom-call | flops 1 | bytes 1 | tf_op jit(solution)/shard_map/pallas_call | solution.py:317
  94.9 4.6 %all-to-all-done.4.arrived = bf16[32,16,256]{2,1,0:T(8,128)(2,1)S(1)} async-done(((bf16[32,16,256]{2,1,0:T(8,128)(2,1)}), bf16[32,16,256]{2,1,0:T(8,128)(2,1)S(1)}, u32[]{:S(2)}, u32[]{:S(2)}) %all-to-all-start.4) | async-done | bytes 262176 | tf_op jit(solution)/shard_map/all_to_all | solution.py:312
  99.5 0.6 shard_map.96
  (14 shorter events, 0.2 us)
Async XLA Ops:
  0.6 0.8 copy-start.4
  4.5 6.9 %copy-start.3 = (bf16[4,16,256]{2,1,0:T(8,128)(2,1)S(1)}, bf16[4,16,256]{2,1,0:T(8,128)(2,1)}, u32[]{:S(2)}) copy-start(bf16[4,16,256]{2,1,0:T(8,128)(2,1)} %param.11) | copy-start | bytes 98308
  4.5 6.9 %copy-start.5 = (bf16[1,16,256]{2,1,0:T(8,128)(2,1)S(1)}, bf16[1,16,256]{2,1,0:T(8,128)(2,1)}, u32[]{:S(2)}) copy-start(bf16[1,16,256]{2,1,0:T(8,128)(2,1)} %param.8) | copy-start | bytes 24580
  4.5 7.0 %slice-start.1 = ((bf16[4,16,256]{2,1,0:T(8,128)(2,1)}), bf16[3,16,256]{2,1,0:T(8,128)(2,1)S(1)}, s32[]{:S(2)}) async-start(bf16[4,16,256]{2,1,0:T(8,128)(2,1)} %param.6), calls=%async_computation.6 | async-start | bytes 49152 | tf_op jit(solution)/shard_map/slice | solution.py:271
  4.5 7.0 %slice-start.2 = ((bf16[4,16,256]{2,1,0:T(8,128)(2,1)}), bf16[3,16,256]{2,1,0:T(8,128)(2,1)S(1)}, s32[]{:S(2)}) async-start(bf16[4,16,256]{2,1,0:T(8,128)(2,1)} %param.11), calls=%async_computation.7 | async-start | bytes 49152 | tf_op jit(solution)/shard_map/slice | solution.py:271
  4.5 19.0 %all-to-all-start = ((bf16[16,5,16,256]{3,2,1,0:T(8,128)(2,1)}), bf16[16,5,16,256]{3,2,1,0:T(8,128)(2,1)S(1)}, u32[]{:S(2)}, u32[]{:S(2)}) async-start(bf16[16,5,16,256]{3,2,1,0:T(8,128)(2,1)} %broadcast_in_dim.14), calls=%async_computation | async-start | bytes 1310720 | tf_op jit(solution)/shard_map/all_to_all | solution.py:265
  11.4 3.0 %copy-start.2 = (bf16[1,16,27,512]{3,1,2,0:T(8,128)(2,1)S(1)}, bf16[1,16,27,512]{3,1,2,0:T(8,128)(2,1)}, u32[]{:S(2)}) copy-start(bf16[1,16,27,512]{3,1,2,0:T(8,128)(2,1)} %param.10) | copy-start | bytes 1327108
  13.8 0.6 copy-start
  14.5 2.6 %copy-start.1 = (bf16[7,32,256]{2,1,0:T(8,128)(2,1)S(1)}, bf16[7,32,256]{2,1,0:T(8,128)(2,1)}, u32[]{:S(2)}) copy-start(bf16[7,32,256]{2,1,0:T(8,128)(2,1)} %copy-done) | copy-start | bytes 344068
  14.5 2.6 %slice-start = ((bf16[7,32,256]{2,1,0:T(8,128)(2,1)}), bf16[3,32,256]{2,1,0:T(8,128)(2,1)S(1)}, s32[]{:S(2)}) async-start(bf16[7,32,256]{2,1,0:T(8,128)(2,1)} %copy-done), calls=%async_computation.5 | async-start | bytes 98304 | tf_op jit(solution)/shard_map/slice | solution.py:274
  24.5 8.4 %collective-permute-start = (bf16[32,256]{1,0:T(8,128)(2,1)S(1)}, bf16[32,256]{1,0:T(8,128)(2,1)S(1)}, u32[]{:S(2)}, u32[]{:S(2)}) collective-permute-start(bf16[32,256]{1,0:T(8,128)(2,1)S(1)} %get-tuple-element.41.refs_0_), channel_id=1, source_target_pairs={{0,32},{2,34},{4,36},{6,38},{8,40},{10,42},{12,44},{14,46},{16,48}... | collective-permute-start | bytes 49160 | tf_op jit(solution)/shard_map/ppermute | solution.py:289
  25.2 39.6 %collective-permute-start.3 = (bf16[16,5,16,256]{3,2,1,0:T(8,128)(2,1)S(1)}, bf16[16,5,16,256]{3,2,1,0:T(8,128)(2,1)S(1)}, u32[]{:S(2)}, u32[]{:S(2)}) collective-permute-start(bf16[16,5,16,256]{3,2,1,0:T(8,128)(2,1)S(1)} %all-to-all-done.near), channel_id=1, source_target_pairs={{0,1},{1,0},{2,3},{3,2},{4,5},{5,4},{6,7},{7,6},{8,9},{9,8},{10,11... | collective-permute-start | bytes 1966088 | tf_op jit(solution)/shard_map/ppermute | solution.py:291
  45.3 5.7 %collective-permute-start.1 = (bf16[32,256]{1,0:T(8,128)(2,1)S(1)}, bf16[32,256]{1,0:T(8,128)(2,1)S(1)}, u32[]{:S(2)}, u32[]{:S(2)}) collective-permute-start(bf16[32,256]{1,0:T(8,128)(2,1)S(1)} %shard_map.87.refs_1_.second), channel_id=1, source_target_pairs={{0,32},{2,34},{4,36},{6,38},{8,40},{10,42},{12,44},{14,46},{16,48}... | collective-permute-start | bytes 49160 | tf_op jit(solution)/shard_map/ppermute | solution.py:289
  62.9 5.7 %collective-permute-start.2 = (bf16[32,256]{1,0:T(8,128)(2,1)S(1)}, bf16[32,256]{1,0:T(8,128)(2,1)S(1)}, u32[]{:S(2)}, u32[]{:S(2)}) collective-permute-start(bf16[32,256]{1,0:T(8,128)(2,1)S(1)} %shard_map.89.refs_2_.third), channel_id=1, source_target_pairs={{0,32},{2,34},{4,36},{6,38},{8,40},{10,42},{12,44},{14,46},{16,48}... | collective-permute-start | bytes 49160 | tf_op jit(solution)/shard_map/ppermute | solution.py:289
  79.9 5.7 %collective-permute-start.4 = (bf16[32,256]{1,0:T(8,128)(2,1)S(1)}, bf16[32,256]{1,0:T(8,128)(2,1)S(1)}, u32[]{:S(2)}, u32[]{:S(2)}) collective-permute-start(bf16[32,256]{1,0:T(8,128)(2,1)S(1)} %shard_map.92.refs_3_.fourth), channel_id=1, source_target_pairs={{33,1},{35,3},{37,5},{39,7},{41,9},{43,11},{45,13},{47,15},{49,17}... | collective-permute-start | bytes 49160 | tf_op jit(solution)/shard_map/ppermute | solution.py:289
  87.1 12.4 %all-to-all-start.4 = ((bf16[32,16,256]{2,1,0:T(8,128)(2,1)}), bf16[32,16,256]{2,1,0:T(8,128)(2,1)S(1)}, u32[]{:S(2)}, u32[]{:S(2)}) async-start(bf16[32,16,256]{2,1,0:T(8,128)(2,1)} %get-tuple-element.73), calls=%async_computation.4 | async-start | bytes 524288 | tf_op jit(solution)/shard_map/all_to_all | solution.py:312

commit v6 on v5

--- a/solution.py
+++ b/solution.py
@@ -189,7 +189,7 @@
         sent[...] = part.astype(jnp.bfloat16).reshape(sent.shape)
 
 
-def filter_kernel(near, far, parcels, *refs):
+def filter_kernel(near, far, back_far, parcels, *refs):
     acts_pair, dpres, (out, acts, spread, whole) = refs[:4], refs[4:8], refs[8:]
 
     def total(even, odd, act_of, dpre_of):
@@ -216,7 +216,7 @@
 
     @pl.when(lax.axis_index("core") == 0)
     def _():
-        total(near, far, lambda r: acts_pair[r][:OWN, :], lambda r: parcels[1, r])
+        total(near, back_far, lambda r: acts_pair[r][:OWN, :], lambda r: parcels[1, r])
 
     @pl.when(lax.axis_index("core") != 0)
     def _():
@@ -288,7 +288,7 @@
         outs[step], near, filters = after((outs[step], near, filters))
         received = lax.ppermute(outs[step], ("section", "chip", "core"), hops[step])
         if step == 0:
-            far = lax.ppermute(near, "core", [(0, 1), (1, 0)])
+            far = lax.ppermute(near, "core", [(0, 1)])
         elif step == 2:
             rest = local_call(slope_kernel, (slope_shape,) * 2, 3, [taps_scratch, whole_scratch], LIGHT)(
                 filters, near, far
@@ -308,7 +308,8 @@
         arrived = lax.all_to_all(sent, "chip", 0, 0)
         outs.append(local_call(finish_kernel, mine, 2, [taps_scratch])(arrived, filters))
 
-    sent, *dpres = after((sent, *dpres))
+    sent, near, *dpres = after((sent, near, *dpres))
+    back_far = lax.ppermute(near, "core", [(1, 0)])
     partials = lax.all_to_all(sent, ("chip", "core"), 0, 0)
     parcel = local_call(pack_kernel, shape((2 * ROUNDS - 1, OWN, CELLS)), 8, [], LIGHT)(
         *outs, *dpres
@@ -317,10 +318,10 @@
     filter_grad, acts = local_call(
         filter_kernel,
         (shape((ROWS, CHANNELS), jnp.float32), shape((ROUNDS, OWN, CELLS))),
-        11,
+        12,
         [pltpu.VMEM((ROWS, CELLS), jnp.bfloat16), whole_scratch],
         LIGHT,
-    )(near, far, parcels, *outs, *dpres)
+    )(near, far, back_far, parcels, *outs, *dpres)
     partials, filter_grad = lax.optimization_barrier((partials, filter_grad))
     grads = local_call(last_kernel, shape((ROUNDS, OWN, CELLS)), 5, [])(
         partials, parcels, *outs[1:]

time: 101 us -> 100 us (0.990)
  the two profiles are of different devices: /device:TPU:97 before, /device:TPU:385 now
where the time goes in v6:
time: 100 us; the launch traced here: 99.3 us
  blocking collectives  40 us (40%)
  starting transfers between devices  34.1 us (34%)
  waiting for transfers between devices  12.7 us (13%)
  Pallas kernels  9.26 us (9%)
  local copies, waits for them, and re-layouts  1.59 us (2%)
    all_to_all x3, blocking collectives, body(): arrived = lax.all_to_all(sent, 'chip', 0, 0)  31.1 us
    ppermute x4, starting transfers between devices, body(): received = lax.ppermute(outs[step], ('section', 'chip', 'core'), hops[step])  13.9 us
    ppermute x1, starting transfers between devices, body(): back_far = lax.ppermute(near, 'core', [(1, 0)])  8.35 us
    all_to_all x1, starting transfers between devices, body(): lax.all_to_all(jnp.broadcast_to(block[None], (chips,) + block.shape), 'ch...  6.9 us
    all_to_all x1, waiting for transfers between devices, body(): lax.all_to_all(jnp.broadcast_to(block[None], (chips,) + block.shape), 'ch...  6.5 us
    all_to_all x1, waiting for transfers between devices, body(): partials = lax.all_to_all(sent, ('chip', 'core'), 0, 0)  4.38 us
    pallas_call x4, Pallas kernels, body(): local_call(functools.partial(start_kernel, step), (sent_shape, mine), 4,...  4.26 us
    all_to_all x1, starting transfers between devices, body(): partials = lax.all_to_all(sent, ('chip', 'core'), 0, 0)  3.66 us
  transfers between devices with their start and end apart: 8, of which 4 were waited for; matrix products, arithmetic and copies ran while one was open for 0% of the time, Pallas kernels for 5%

profile of v6, /device:TPU:385, one launch (start us, length us, event | category | flops | bytes accessed | tf_op | source)
XLA Modules:
  0.0 99.3 jit_solution(2548322791405324566)
XLA Ops:
  0.6 0.0 copy-start.4
  0.6 0.7 slice_select_fusion.2
  1.4 0.0 copy-done.4
  1.4 2.2 %all_gather.15 = bf16[5,32,256]{2,1,0:T(8,128)(2,1)S(1)} all-gather(bf16[5,16,256]{2,1,0:T(8,128)(2,1)S(1)} %pad_maximum_fusion.1), channel_id=1, replica_groups=mesh['section'=16,'chip'=16,'core'=2] {'core'}, dimensions={1}, use_global_device_ids=true | all-gather | bytes 122880 | tf_op jit(solution)/shard_map/all_gather | solution.py:257
  3.6 0.9 broadcast_in_dim.14
  4.5 0.0 copy-start.3
  4.5 0.0 copy-start.5
  4.5 0.0 slice-start.1
  4.5 0.0 slice-start.2
  4.5 6.9 %all-to-all-start = ((bf16[16,5,16,256]{3,2,1,0:T(8,128)(2,1)}), bf16[16,5,16,256]{3,2,1,0:T(8,128)(2,1)S(1)}, u32[]{:S(2)}, u32[]{:S(2)}) async-start(bf16[16,5,16,256]{3,2,1,0:T(8,128)(2,1)} %broadcast_in_dim.14), calls=%async_computation | async-start | bytes 1310720 | tf_op jit(solution)/shard_map/all_to_all | solution.py:265
  11.4 0.0 copy-start.2
  11.4 0.0 copy-done.3
  11.4 0.0 copy-done.5
  11.5 0.0 slice-done.1
  11.5 0.0 slice-done.2
  11.5 2.3 %all_gather.17 = bf16[7,32,256]{2,1,0:T(8,128)(2,1)S(1)} all-gather(bf16[7,16,256]{2,1,0:T(8,128)(2,1)S(1)} %pad_maximum_fusion), channel_id=1, replica_groups=mesh['section'=16,'chip'=16,'core'=2] {'core'}, dimensions={1}, use_global_device_ids=true | all-gather | bytes 172032 | tf_op jit(solution)/shard_map/all_gather | solution.py:273
  13.8 0.6 copy-done
  14.4 0.0 copy-done.2
  14.5 2.6 %all_gather.16.filters = bf16[864,512]{1,0:T(8,128)(2,1)S(1)} all-gather(bf16[432,512]{1,0:T(8,128)(2,1)S(1)} %bitcast.37), channel_id=1, replica_groups=mesh['section'=16,'chip'=16,'core'=2] {'core'}, dimensions={0}, use_global_device_ids=true | all-gather | bytes 1327104 | tf_op jit(solution)/shard_map/all_gather | solution.py:267
  17.0 0.0 copy-done.1
  17.0 0.0 slice-done
  17.0 6.5 %all-to-all-done.near = bf16[16,5,16,256]{3,2,1,0:T(8,128)(2,1)S(1)} async-done(((bf16[16,5,16,256]{3,2,1,0:T(8,128)(2,1)}), bf16[16,5,16,256]{3,2,1,0:T(8,128)(2,1)S(1)}, u32[]{:S(2)}, u32[]{:S(2)}) %all-to-all-start) | async-done | bytes 655392 | tf_op jit(solution)/shard_map/all_to_all | solution.py:265
  23.5 1.0 %shard_map.85 = (bf16[32,256]{1,0:T(8,128)(2,1)S(1)}, f32[32,256]{1,0:T(8,128)S(1)}, f32[32,256]{1,0:T(8,128)S(1)}) custom-call(bf16[16,5,16,256]{3,2,1,0:T(8,128)(2,1)S(1)} %all-to-all-done.near, bf16[864,512]{1,0:T(8,128)(2,1)S(1)} %all_gather.16.filters), custom_call_target="tpu_custom_call" | custom-call | tf_op jit(solution)/shard_map/pallas_call | solution.py:281
  24.5 0.7 collective-permute-start
  25.2 1.3 %collective-permute-start.3 = (bf16[16,5,16,256]{3,2,1,0:T(8,128)(2,1)S(1)}, bf16[16,5,16,256]{3,2,1,0:T(8,128)(2,1)S(1)}, u32[]{:S(2)}, u32[]{:S(2)}) collective-permute-start(bf16[16,5,16,256]{3,2,1,0:T(8,128)(2,1)S(1)} %all-to-all-done.near), channel_id=1, source_target_pairs={{0,1},{2,3},{4,5},{6,7},{8,9},{10,11},{12,13},{14,15},{16,17},{18,... | collective-permute-start | bytes 1966088 | tf_op jit(solution)/shard_map/ppermute | solution.py:291
  26.5 0.0 collective-permute-done.received
  26.5 0.9 shard_map.86
  27.4 10.8 %all_to_all.25.arrived = bf16[16,32,256]{2,1,0:T(8,128)(2,1)S(1)} all-to-all(bf16[16,32,256]{2,1,0:T(8,128)(2,1)S(1)} %get-tuple-element.45), channel_id=1, replica_groups=mesh['section'=16,'chip'=16,'core'=2] {'chip'}, dimensions={0} | all-to-all | bytes 524288 | tf_op jit(solution)/shard_map/all_to_all | solution.py:308
  38.2 3.8 %collective-permute-start.1 = (bf16[32,256]{1,0:T(8,128)(2,1)S(1)}, bf16[32,256]{1,0:T(8,128)(2,1)S(1)}, u32[]{:S(2)}, u32[]{:S(2)}) collective-permute-start(bf16[32,256]{1,0:T(8,128)(2,1)S(1)} %shard_map.87.refs_1_.second), channel_id=1, source_target_pairs={{0,32},{2,34},{4,36},{6,38},{8,40},{10,42},{12,44},{14,46},{16,48}... | collective-permute-start | bytes 49160 | tf_op jit(solution)/shard_map/ppermute | solution.py:289
  42.1 0.9 collective-permute-done.1.received
  43.0 0.9 shard_map.88
  43.9 10.2 %all_to_all.26.arrived = bf16[16,32,256]{2,1,0:T(8,128)(2,1)S(1)} all-to-all(bf16[16,32,256]{2,1,0:T(8,128)(2,1)S(1)} %get-tuple-element.50), channel_id=1, replica_groups=mesh['section'=16,'chip'=16,'core'=2] {'chip'}, dimensions={0} | all-to-all | bytes 524288 | tf_op jit(solution)/shard_map/all_to_all | solution.py:308
  54.1 4.8 %collective-permute-start.2 = (bf16[32,256]{1,0:T(8,128)(2,1)S(1)}, bf16[32,256]{1,0:T(8,128)(2,1)S(1)}, u32[]{:S(2)}, u32[]{:S(2)}) collective-permute-start(bf16[32,256]{1,0:T(8,128)(2,1)S(1)} %shard_map.89.refs_2_.third), channel_id=1, source_target_pairs={{0,32},{2,34},{4,36},{6,38},{8,40},{10,42},{12,44},{14,46},{16,48}... | collective-permute-start | bytes 49160 | tf_op jit(solution)/shard_map/ppermute | solution.py:289
  58.9 0.0 collective-permute-done.3.far
  58.9 1.0 %shard_map.90 = (f32[32,256]{1,0:T(8,128)S(1)}, f32[32,256]{1,0:T(8,128)S(1)}) custom-call(bf16[864,512]{1,0:T(8,128)(2,1)S(1)} %all_gather.16.filters, bf16[16,5,16,256]{3,2,1,0:T(8,128)(2,1)S(1)} %all-to-all-done.near, bf16[16,5,16,256]{3,2,1,0:T(8,128)(2,1)S(1)} %collective-permute-done.3.far), custom_call_target="tpu_custom_call" | custom-call | flops 1 | bytes 1 | tf_op jit(solution)/shard_map/pallas_call | solution.py:293
  59.9 0.0 collective-permute-done.2.received
  59.9 0.9 shard_map.91
  60.8 10.2 %all_to_all.27.arrived = bf16[16,32,256]{2,1,0:T(8,128)(2,1)S(1)} all-to-all(bf16[16,32,256]{2,1,0:T(8,128)(2,1)S(1)} %get-tuple-element.59), channel_id=1, replica_groups=mesh['section'=16,'chip'=16,'core'=2] {'chip'}, dimensions={0} | all-to-all | bytes 524288 | tf_op jit(solution)/shard_map/all_to_all | solution.py:308
  71.0 4.6 %collective-permute-start.4 = (bf16[32,256]{1,0:T(8,128)(2,1)S(1)}, bf16[32,256]{1,0:T(8,128)(2,1)S(1)}, u32[]{:S(2)}, u32[]{:S(2)}) collective-permute-start(bf16[32,256]{1,0:T(8,128)(2,1)S(1)} %shard_map.92.refs_3_.fourth), channel_id=1, source_target_pairs={{33,1},{35,3},{37,5},{39,7},{41,9},{43,11},{45,13},{47,15},{49,17}... | collective-permute-start | bytes 49160 | tf_op jit(solution)/shard_map/ppermute | solution.py:289
  75.7 0.8 collective-permute-done.4.received
  76.5 1.6 %shard_map.93 = (bf16[32,16,256]{2,1,0:T(8,128)(2,1)}, bf16[32,256]{1,0:T(8,128)(2,1)S(1)}) custom-call(bf16[32,256]{1,0:T(8,128)(2,1)S(1)} %collective-permute-done.4.received, bf16[32,256]{1,0:T(8,128)(2,1)S(1)} %get-tuple-element.85.outside, f32[32,256]{1,0:T(8,128)S(1)} %get-tuple-element.61.slope, bf16[864,512]{1,0:T(8,128)(2,1)S(1)} %all_gather.16.filters), custom_call_target="tpu_custom_call" | custom-call | tf_op jit(solution)/shard_map/pallas_call | solution.py:299
  78.1 8.4 %collective-permute-start.5 = (bf16[16,5,16,256]{3,2,1,0:T(8,128)(2,1)S(1)}, bf16[16,5,16,256]{3,2,1,0:T(8,128)(2,1)S(1)}, u32[]{:S(2)}, u32[]{:S(2)}) collective-permute-start(bf16[16,5,16,256]{3,2,1,0:T(8,128)(2,1)S(1)} %all-to-all-done.near), channel_id=1, source_target_pairs={{1,0},{3,2},{5,4},{7,6},{9,8},{11,10},{13,12},{15,14},{17,16},{19,... | collective-permute-start | bytes 1966088 | tf_op jit(solution)/shard_map/ppermute | solution.py:312
  86.5 3.7 %all-to-all-start.4 = ((bf16[32,16,256]{2,1,0:T(8,128)(2,1)}), bf16[32,16,256]{2,1,0:T(8,128)(2,1)S(1)}, u32[]{:S(2)}, u32[]{:S(2)}) async-start(bf16[32,16,256]{2,1,0:T(8,128)(2,1)} %get-tuple-element.75), calls=%async_computation.4 | async-start | bytes 524288 | tf_op jit(solution)/shard_map/all_to_all | solution.py:313
  90.2 1.9 %all-gather = bf16[14,16,256]{2,1,0:T(8,128)(2,1)S(1)} all-gather(bf16[7,16,256]{2,1,0:T(8,128)(2,1)S(1)} %shard_map.94), channel_id=2, replica_groups=mesh['section'=16,'chip'=16,'core'=2] {'core'}, dimensions={0}, use_global_device_ids=true | all-gather | bytes 172032 | tf_op jit(solution)/shard_map/all_gather | solution.py:317
  92.1 0.0 collective-permute-done.5.back_far
  92.1 2.2 %shard_map.95 = (f32[432,512]{1,0:T(8,128)}, bf16[4,16,256]{2,1,0:T(8,128)(2,1)}) custom-call(bf16[16,5,16,256]{3,2,1,0:T(8,128)(2,1)S(1)} %all-to-all-done.near, bf16[16,5,16,256]{3,2,1,0:T(8,128)(2,1)S(1)} %collective-permute-done.3.far, bf16[16,5,16,256]{3,2,1,0:T(8,128)(2,1)S(1)} %collective-permute-done.5.back_far, ...), custom_call_target="tpu_custom_call" | custom-call | flops 1 | bytes 1 | tf_op jit(solution)/shard_map/pallas_call | solution.py:318
  94.3 4.4 %all-to-all-done.4.arrived = bf16[32,16,256]{2,1,0:T(8,128)(2,1)S(1)} async-done(((bf16[32,16,256]{2,1,0:T(8,128)(2,1)}), bf16[32,16,256]{2,1,0:T(8,128)(2,1)S(1)}, u32[]{:S(2)}, u32[]{:S(2)}) %all-to-all-start.4) | async-done | bytes 262176 | tf_op jit(solution)/shard_map/all_to_all | solution.py:313
  98.7 0.6 shard_map.96
  (16 shorter events, 0.2 us)
Async XLA Ops:
  0.6 0.8 copy-start.4
  4.5 6.9 %copy-start.3 = (bf16[4,16,256]{2,1,0:T(8,128)(2,1)S(1)}, bf16[4,16,256]{2,1,0:T(8,128)(2,1)}, u32[]{:S(2)}) copy-start(bf16[4,16,256]{2,1,0:T(8,128)(2,1)} %param.11) | copy-start | bytes 98308
  4.5 6.9 %copy-start.5 = (bf16[1,16,256]{2,1,0:T(8,128)(2,1)S(1)}, bf16[1,16,256]{2,1,0:T(8,128)(2,1)}, u32[]{:S(2)}) copy-start(bf16[1,16,256]{2,1,0:T(8,128)(2,1)} %param.8) | copy-start | bytes 24580
  4.5 7.0 %slice-start.1 = ((bf16[4,16,256]{2,1,0:T(8,128)(2,1)}), bf16[3,16,256]{2,1,0:T(8,128)(2,1)S(1)}, s32[]{:S(2)}) async-start(bf16[4,16,256]{2,1,0:T(8,128)(2,1)} %param.6), calls=%async_computation.6 | async-start | bytes 49152 | tf_op jit(solution)/shard_map/slice | solution.py:271
  4.5 7.0 %slice-start.2 = ((bf16[4,16,256]{2,1,0:T(8,128)(2,1)}), bf16[3,16,256]{2,1,0:T(8,128)(2,1)S(1)}, s32[]{:S(2)}) async-start(bf16[4,16,256]{2,1,0:T(8,128)(2,1)} %param.11), calls=%async_computation.7 | async-start | bytes 49152 | tf_op jit(solution)/shard_map/slice | solution.py:271
  4.5 19.0 %all-to-all-start = ((bf16[16,5,16,256]{3,2,1,0:T(8,128)(2,1)}), bf16[16,5,16,256]{3,2,1,0:T(8,128)(2,1)S(1)}, u32[]{:S(2)}, u32[]{:S(2)}) async-start(bf16[16,5,16,256]{3,2,1,0:T(8,128)(2,1)} %broadcast_in_dim.14), calls=%async_computation | async-start | bytes 1310720 | tf_op jit(solution)/shard_map/all_to_all | solution.py:265
  11.4 3.0 %copy-start.2 = (bf16[1,16,27,512]{3,1,2,0:T(8,128)(2,1)S(1)}, bf16[1,16,27,512]{3,1,2,0:T(8,128)(2,1)}, u32[]{:S(2)}) copy-start(bf16[1,16,27,512]{3,1,2,0:T(8,128)(2,1)} %param.10) | copy-start | bytes 1327108
  13.8 0.6 copy-start
  14.5 2.6 %copy-start.1 = (bf16[7,32,256]{2,1,0:T(8,128)(2,1)S(1)}, bf16[7,32,256]{2,1,0:T(8,128)(2,1)}, u32[]{:S(2)}) copy-start(bf16[7,32,256]{2,1,0:T(8,128)(2,1)} %copy-done) | copy-start | bytes 344068
  14.5 2.6 %slice-start = ((bf16[7,32,256]{2,1,0:T(8,128)(2,1)}), bf16[3,32,256]{2,1,0:T(8,128)(2,1)S(1)}, s32[]{:S(2)}) async-start(bf16[7,32,256]{2,1,0:T(8,128)(2,1)} %copy-done), calls=%async_computation.5 | async-start | bytes 98304 | tf_op jit(solution)/shard_map/slice | solution.py:274
  24.5 2.0 %collective-permute-start = (bf16[32,256]{1,0:T(8,128)(2,1)S(1)}, bf16[32,256]{1,0:T(8,128)(2,1)S(1)}, u32[]{:S(2)}, u32[]{:S(2)}) collective-permute-start(bf16[32,256]{1,0:T(8,128)(2,1)S(1)} %get-tuple-element.42.refs_0_), channel_id=1, source_target_pairs={{0,32},{2,34},{4,36},{6,38},{8,40},{10,42},{12,44},{14,46},{16,48}... | collective-permute-start | bytes 49160 | tf_op jit(solution)/shard_map/ppermute | solution.py:289
  25.2 33.7 %collective-permute-start.3 = (bf16[16,5,16,256]{3,2,1,0:T(8,128)(2,1)S(1)}, bf16[16,5,16,256]{3,2,1,0:T(8,128)(2,1)S(1)}, u32[]{:S(2)}, u32[]{:S(2)}) collective-permute-start(bf16[16,5,16,256]{3,2,1,0:T(8,128)(2,1)S(1)} %all-to-all-done.near), channel_id=1, source_target_pairs={{0,1},{2,3},{4,5},{6,7},{8,9},{10,11},{12,13},{14,15},{16,17},{18,... | collective-permute-start | bytes 1966088 | tf_op jit(solution)/shard_map/ppermute | solution.py:291
  38.2 4.8 %collective-permute-start.1 = (bf16[32,256]{1,0:T(8,128)(2,1)S(1)}, bf16[32,256]{1,0:T(8,128)(2,1)S(1)}, u32[]{:S(2)}, u32[]{:S(2)}) collective-permute-start(bf16[32,256]{1,0:T(8,128)(2,1)S(1)} %shard_map.87.refs_1_.second), channel_id=1, source_target_pairs={{0,32},{2,34},{4,36},{6,38},{8,40},{10,42},{12,44},{14,46},{16,48}... | collective-permute-start | bytes 49160 | tf_op jit(solution)/shard_map/ppermute | solution.py:289
  54.1 5.8 %collective-permute-start.2 = (bf16[32,256]{1,0:T(8,128)(2,1)S(1)}, bf16[32,256]{1,0:T(8,128)(2,1)S(1)}, u32[]{:S(2)}, u32[]{:S(2)}) collective-permute-start(bf16[32,256]{1,0:T(8,128)(2,1)S(1)} %shard_map.89.refs_2_.third), channel_id=1, source_target_pairs={{0,32},{2,34},{4,36},{6,38},{8,40},{10,42},{12,44},{14,46},{16,48}... | collective-permute-start | bytes 49160 | tf_op jit(solution)/shard_map/ppermute | solution.py:289
  71.0 5.5 %collective-permute-start.4 = (bf16[32,256]{1,0:T(8,128)(2,1)S(1)}, bf16[32,256]{1,0:T(8,128)(2,1)S(1)}, u32[]{:S(2)}, u32[]{:S(2)}) collective-permute-start(bf16[32,256]{1,0:T(8,128)(2,1)S(1)} %shard_map.92.refs_3_.fourth), channel_id=1, source_target_pairs={{33,1},{35,3},{37,5},{39,7},{41,9},{43,11},{45,13},{47,15},{49,17}... | collective-permute-start | bytes 49160 | tf_op jit(solution)/shard_map/ppermute | solution.py:289
  78.1 14.0 %collective-permute-start.5 = (bf16[16,5,16,256]{3,2,1,0:T(8,128)(2,1)S(1)}, bf16[16,5,16,256]{3,2,1,0:T(8,128)(2,1)S(1)}, u32[]{:S(2)}, u32[]{:S(2)}) collective-permute-start(bf16[16,5,16,256]{3,2,1,0:T(8,128)(2,1)S(1)} %all-to-all-done.near), channel_id=1, source_target_pairs={{1,0},{3,2},{5,4},{7,6},{9,8},{11,10},{13,12},{15,14},{17,16},{19,... | collective-permute-start | bytes 1966088 | tf_op jit(solution)/shard_map/ppermute | solution.py:312
  86.5 12.2 %all-to-all-start.4 = ((bf16[32,16,256]{2,1,0:T(8,128)(2,1)}), bf16[32,16,256]{2,1,0:T(8,128)(2,1)S(1)}, u32[]{:S(2)}, u32[]{:S(2)}) async-start(bf16[32,16,256]{2,1,0:T(8,128)(2,1)} %get-tuple-element.75), calls=%async_computation.4 | async-start | bytes 524288 | tf_op jit(solution)/shard_map/all_to_all | solution.py:313

commit v7 on v6

--- a/solution.py
+++ b/solution.py
@@ -120,6 +120,13 @@
     out[...] = total.astype(jnp.bfloat16)
 
 
+def sum_into(out, arrived):
+    total = arrived[0].astype(jnp.float32)
+    for p in range(1, arrived.shape[0]):
+        total = total + arrived[p].astype(jnp.float32)
+    out[...] = total.astype(jnp.bfloat16)
+
+
 def finish_kernel(arrived, filters, out, taps):
     @pl.when(lax.axis_index("core") == 0)
     def _():
@@ -130,19 +137,31 @@
         sum_into(out, arrived)
 
 
-def pack_kernel(*refs):
-    outs, dpres, parcel = refs[:4], refs[4:8], refs[8]
-
-    @pl.when(lax.axis_index("core") == 0)
-    def _():
-        for r, pair in enumerate(outs):
+def sum_kernel(arrived, out):
+    @pl.when(lax.axis_index("core") == 0)
+    def _():
+        out[...] = jnp.zeros_like(out)
+
+    @pl.when(lax.axis_index("core") != 0)
+    def _():
+        sum_into(out, arrived)
+
+
+def pack_kernel(arrived, filters, *refs):
+    (*outs, grad), dpres, (act, parcel, taps) = refs[:4], refs[4:8], refs[8:]
+
+    @pl.when(lax.axis_index("core") == 0)
+    def _():
+        silu_into(act, filters, arrived[...], taps, coordinates(OWN))
+        for r, pair in enumerate((*outs, act)):
             parcel[r] = pair[OWN:, :]
         for r in range(ROUNDS - 1):
             parcel[ROUNDS + r] = jnp.zeros((OWN, CELLS), jnp.bfloat16)
 
     @pl.when(lax.axis_index("core") != 0)
     def _():
-        for r, pair in enumerate((*dpres, *outs[1:])):
+        act[...] = jnp.zeros_like(act)
+        for r, pair in enumerate((*dpres, *outs[1:], grad)):
             parcel[r] = pair[:OWN, :]
 
 
@@ -306,14 +325,17 @@
         if last:
             break
         arrived = lax.all_to_all(sent, "chip", 0, 0)
-        outs.append(local_call(finish_kernel, mine, 2, [taps_scratch])(arrived, filters))
-
-    sent, near, *dpres = after((sent, near, *dpres))
+        if step + 2 < ROUNDS:
+            outs.append(local_call(finish_kernel, mine, 2, [taps_scratch])(arrived, filters))
+        else:
+            outs.append(local_call(sum_kernel, mine, 1, [])(arrived))
+
+    sent, near, arrived, *dpres = after((sent, near, arrived, *dpres))
     back_far = lax.ppermute(near, "core", [(1, 0)])
     partials = lax.all_to_all(sent, ("chip", "core"), 0, 0)
-    parcel = local_call(pack_kernel, shape((2 * ROUNDS - 1, OWN, CELLS)), 8, [], LIGHT)(
-        *outs, *dpres
-    )
+    act, parcel = local_call(
+        pack_kernel, (mine, shape((2 * ROUNDS - 1, OWN, CELLS))), 10, [taps_scratch], LIGHT
+    )(arrived, filters, *outs, *dpres)
     parcels = lax.all_gather(parcel, "core", axis=0)
     filter_grad, acts = local_call(
         filter_kernel,
@@ -321,7 +343,7 @@
         12,
         [pltpu.VMEM((ROWS, CELLS), jnp.bfloat16), whole_scratch],
         LIGHT,
-    )(near, far, back_far, parcels, *outs, *dpres)
+    )(near, far, back_far, parcels, *outs[:3], act, *dpres)
     partials, filter_grad = lax.optimization_barrier((partials, filter_grad))
     grads = local_call(last_kernel, shape((ROUNDS, OWN, CELLS)), 5, [])(
         partials, parcels, *outs[1:]

time: 100 us -> 99.3 us (level)
  no operation moved by 1% of the time
where the time goes in v7:
time: 99.3 us; the launch traced here: 98.7 us
  blocking collectives  40.1 us (40%)
  starting transfers between devices  33.5 us (34%)
  waiting for transfers between devices  12.6 us (13%)
  Pallas kernels  8.56 us (9%)
  local copies, waits for them, and re-layouts  2.27 us (2%)
    all_to_all x3, blocking collectives, body(): arrived = lax.all_to_all(sent, 'chip', 0, 0)  31.1 us
    ppermute x4, starting transfers between devices, body(): received = lax.ppermute(outs[step], ('section', 'chip', 'core'), hops[step])  13.9 us
    ppermute x1, starting transfers between devices, body(): back_far = lax.ppermute(near, 'core', [(1, 0)])  7.73 us
    all_to_all x1, starting transfers between devices, body(): lax.all_to_all(jnp.broadcast_to(block[None], (chips,) + block.shape), 'ch...  6.9 us
    all_to_all x1, waiting for transfers between devices, body(): lax.all_to_all(jnp.broadcast_to(block[None], (chips,) + block.shape), 'ch...  6.5 us
    all_to_all x1, waiting for transfers between devices, body(): partials = lax.all_to_all(sent, ('chip', 'core'), 0, 0)  4.27 us
    all_to_all x1, starting transfers between devices, body(): partials = lax.all_to_all(sent, ('chip', 'core'), 0, 0)  3.66 us
    pallas_call x4, Pallas kernels, body(): local_call(functools.partial(start_kernel, step), (sent_shape, mine), 4,...  3.55 us
  transfers between devices with their start and end apart: 8, of which 4 were waited for; matrix products, arithmetic and copies ran while one was open for 0% of the time, Pallas kernels for 5%

profile of v7, /device:TPU:385, one launch (start us, length us, event | category | flops | bytes accessed | tf_op | source)
XLA Modules:
  0.0 98.7 jit_solution(16607319717452609432)
XLA Ops:
  0.6 0.0 copy-start.5
  0.6 0.7 slice_select_fusion.2
  1.4 0.0 copy-done.5
  1.4 2.2 %all_gather.15 = bf16[5,32,256]{2,1,0:T(8,128)(2,1)S(1)} all-gather(bf16[5,16,256]{2,1,0:T(8,128)(2,1)S(1)} %pad_maximum_fusion.1), channel_id=1, replica_groups=mesh['section'=16,'chip'=16,'core'=2] {'core'}, dimensions={1}, use_global_device_ids=true | all-gather | bytes 122880 | tf_op jit(solution)/shard_map/all_gather | solution.py:276
  3.6 0.9 broadcast_in_dim.14
  4.5 0.0 copy-start.4
  4.5 0.0 copy-start.6
  4.5 6.9 %all-to-all-start = ((bf16[16,5,16,256]{3,2,1,0:T(8,128)(2,1)}), bf16[16,5,16,256]{3,2,1,0:T(8,128)(2,1)S(1)}, u32[]{:S(2)}, u32[]{:S(2)}) async-start(bf16[16,5,16,256]{3,2,1,0:T(8,128)(2,1)} %broadcast_in_dim.14), calls=%async_computation | async-start | bytes 1310720 | tf_op jit(solution)/shard_map/all_to_all | solution.py:284
  11.4 0.0 copy-start.3
  11.4 0.0 copy-done.4
  11.4 0.0 copy-done.6
  11.5 0.0 slice-done.1
  11.5 0.0 slice-done.2
  11.5 2.3 %all_gather.17 = bf16[7,32,256]{2,1,0:T(8,128)(2,1)S(1)} all-gather(bf16[7,16,256]{2,1,0:T(8,128)(2,1)S(1)} %pad_maximum_fusion), channel_id=1, replica_groups=mesh['section'=16,'chip'=16,'core'=2] {'core'}, dimensions={1}, use_global_device_ids=true | all-gather | bytes 172032 | tf_op jit(solution)/shard_map/all_gather | solution.py:292
  13.8 0.6 copy-done.1
  14.5 0.0 copy-done.3
  14.5 2.6 %all_gather.16.filters = bf16[864,512]{1,0:T(8,128)(2,1)S(1)} all-gather(bf16[432,512]{1,0:T(8,128)(2,1)S(1)} %bitcast.37), channel_id=1, replica_groups=mesh['section'=16,'chip'=16,'core'=2] {'core'}, dimensions={0}, use_global_device_ids=true | all-gather | bytes 1327104 | tf_op jit(solution)/shard_map/all_gather | solution.py:286
  17.0 0.0 copy-done.2
  17.0 0.0 slice-done
  17.0 6.5 %all-to-all-done.near = bf16[16,5,16,256]{3,2,1,0:T(8,128)(2,1)S(1)} async-done(((bf16[16,5,16,256]{3,2,1,0:T(8,128)(2,1)}), bf16[16,5,16,256]{3,2,1,0:T(8,128)(2,1)S(1)}, u32[]{:S(2)}, u32[]{:S(2)}) %all-to-all-start) | async-done | bytes 655392 | tf_op jit(solution)/shard_map/all_to_all | solution.py:284
  23.5 1.0 %shard_map.85 = (bf16[32,256]{1,0:T(8,128)(2,1)S(1)}, f32[32,256]{1,0:T(8,128)S(1)}, f32[32,256]{1,0:T(8,128)S(1)}) custom-call(bf16[16,5,16,256]{3,2,1,0:T(8,128)(2,1)S(1)} %all-to-all-done.near, bf16[864,512]{1,0:T(8,128)(2,1)S(1)} %all_gather.16.filters), custom_call_target="tpu_custom_call" | custom-call | tf_op jit(solution)/shard_map/pallas_call | solution.py:300
  24.5 0.7 collective-permute-start
  25.2 1.3 %collective-permute-start.3 = (bf16[16,5,16,256]{3,2,1,0:T(8,128)(2,1)S(1)}, bf16[16,5,16,256]{3,2,1,0:T(8,128)(2,1)S(1)}, u32[]{:S(2)}, u32[]{:S(2)}) collective-permute-start(bf16[16,5,16,256]{3,2,1,0:T(8,128)(2,1)S(1)} %all-to-all-done.near), channel_id=1, source_target_pairs={{0,1},{2,3},{4,5},{6,7},{8,9},{10,11},{12,13},{14,15},{16,17},{18,... | collective-permute-start | bytes 1966088 | tf_op jit(solution)/shard_map/ppermute | solution.py:310
  26.5 0.0 collective-permute-done.received
  26.5 0.9 shard_map.86
  27.4 10.8 %all_to_all.25.arrived = bf16[16,32,256]{2,1,0:T(8,128)(2,1)S(1)} all-to-all(bf16[16,32,256]{2,1,0:T(8,128)(2,1)S(1)} %get-tuple-element.48), channel_id=1, replica_groups=mesh['section'=16,'chip'=16,'core'=2] {'chip'}, dimensions={0} | all-to-all | bytes 524288 | tf_op jit(solution)/shard_map/all_to_all | solution.py:327
  38.2 3.8 %collective-permute-start.1 = (bf16[32,256]{1,0:T(8,128)(2,1)S(1)}, bf16[32,256]{1,0:T(8,128)(2,1)S(1)}, u32[]{:S(2)}, u32[]{:S(2)}) collective-permute-start(bf16[32,256]{1,0:T(8,128)(2,1)S(1)} %shard_map.87.refs_1_.second), channel_id=1, source_target_pairs={{0,32},{2,34},{4,36},{6,38},{8,40},{10,42},{12,44},{14,46},{16,48}... | collective-permute-start | bytes 49160 | tf_op jit(solution)/shard_map/ppermute | solution.py:308
  42.1 0.9 collective-permute-done.1.received
  43.0 0.9 shard_map.88
  43.9 10.2 %all_to_all.26.arrived = bf16[16,32,256]{2,1,0:T(8,128)(2,1)S(1)} all-to-all(bf16[16,32,256]{2,1,0:T(8,128)(2,1)S(1)} %get-tuple-element.53), channel_id=1, replica_groups=mesh['section'=16,'chip'=16,'core'=2] {'chip'}, dimensions={0} | all-to-all | bytes 524288 | tf_op jit(solution)/shard_map/all_to_all | solution.py:327
  54.1 4.8 %collective-permute-start.2 = (bf16[32,256]{1,0:T(8,128)(2,1)S(1)}, bf16[32,256]{1,0:T(8,128)(2,1)S(1)}, u32[]{:S(2)}, u32[]{:S(2)}) collective-permute-start(bf16[32,256]{1,0:T(8,128)(2,1)S(1)} %shard_map.89.refs_2_.third), channel_id=1, source_target_pairs={{0,32},{2,34},{4,36},{6,38},{8,40},{10,42},{12,44},{14,46},{16,48}... | collective-permute-start | bytes 49160 | tf_op jit(solution)/shard_map/ppermute | solution.py:308
  58.9 0.0 collective-permute-done.3.far
  58.9 1.0 %shard_map.90 = (f32[32,256]{1,0:T(8,128)S(1)}, f32[32,256]{1,0:T(8,128)S(1)}) custom-call(bf16[864,512]{1,0:T(8,128)(2,1)S(1)} %all_gather.16.filters, bf16[16,5,16,256]{3,2,1,0:T(8,128)(2,1)S(1)} %all-to-all-done.near, bf16[16,5,16,256]{3,2,1,0:T(8,128)(2,1)S(1)} %collective-permute-done.3.far), custom_call_target="tpu_custom_call" | custom-call | flops 1 | bytes 1 | tf_op jit(solution)/shard_map/pallas_call | solution.py:312
  59.9 0.0 collective-permute-done.2.received
  59.9 0.9 shard_map.91
  60.8 10.2 %all_to_all.27.arrived = bf16[16,32,256]{2,1,0:T(8,128)(2,1)S(1)} all-to-all(bf16[16,32,256]{2,1,0:T(8,128)(2,1)S(1)} %get-tuple-element.62), channel_id=1, replica_groups=mesh['section'=16,'chip'=16,'core'=2] {'chip'}, dimensions={0} | all-to-all | bytes 524288 | tf_op jit(solution)/shard_map/all_to_all | solution.py:327
  71.0 4.6 %collective-permute-start.4 = (bf16[32,256]{1,0:T(8,128)(2,1)S(1)}, bf16[32,256]{1,0:T(8,128)(2,1)S(1)}, u32[]{:S(2)}, u32[]{:S(2)}) collective-permute-start(bf16[32,256]{1,0:T(8,128)(2,1)S(1)} %shard_map.92.refs_3_.fourth), channel_id=1, source_target_pairs={{33,1},{35,3},{37,5},{39,7},{41,9},{43,11},{45,13},{47,15},{49,17}... | collective-permute-start | bytes 49160 | tf_op jit(solution)/shard_map/ppermute | solution.py:308
  75.7 0.8 collective-permute-done.4.received
  76.5 0.9 shard_map.93
  77.4 0.0 copy-start
  77.4 0.7 copy-done
  78.1 7.7 %collective-permute-start.5 = (bf16[16,5,16,256]{3,2,1,0:T(8,128)(2,1)S(1)}, bf16[16,5,16,256]{3,2,1,0:T(8,128)(2,1)S(1)}, u32[]{:S(2)}, u32[]{:S(2)}) collective-permute-start(bf16[16,5,16,256]{3,2,1,0:T(8,128)(2,1)S(1)} %all-to-all-done.near), channel_id=1, source_target_pairs={{1,0},{3,2},{5,4},{7,6},{9,8},{11,10},{13,12},{15,14},{17,16},{19,... | collective-permute-start | bytes 1966088 | tf_op jit(solution)/shard_map/ppermute | solution.py:334
  85.8 3.7 %all-to-all-start.4 = ((bf16[32,16,256]{2,1,0:T(8,128)(2,1)}), bf16[32,16,256]{2,1,0:T(8,128)(2,1)S(1)}, u32[]{:S(2)}, u32[]{:S(2)}) async-start(bf16[32,16,256]{2,1,0:T(8,128)(2,1)} %copy-done), calls=%async_computation.4 | async-start | bytes 524288 | tf_op jit(solution)/shard_map/all_to_all | solution.py:335
  89.5 2.0 %all-gather = bf16[14,16,256]{2,1,0:T(8,128)(2,1)S(1)} all-gather(bf16[7,16,256]{2,1,0:T(8,128)(2,1)S(1)} %get-tuple-element.78), channel_id=2, replica_groups=mesh['section'=16,'chip'=16,'core'=2] {'core'}, dimensions={0}, use_global_device_ids=true | all-gather | bytes 172032 | tf_op jit(solution)/shard_map/all_gather | solution.py:339
  91.5 0.0 collective-permute-done.5.back_far
  91.5 2.2 %shard_map.95 = (f32[432,512]{1,0:T(8,128)}, bf16[4,16,256]{2,1,0:T(8,128)(2,1)}) custom-call(bf16[16,5,16,256]{3,2,1,0:T(8,128)(2,1)S(1)} %all-to-all-done.near, bf16[16,5,16,256]{3,2,1,0:T(8,128)(2,1)S(1)} %collective-permute-done.3.far, bf16[16,5,16,256]{3,2,1,0:T(8,128)(2,1)S(1)} %collective-permute-done.5.back_far, ...), custom_call_target="tpu_custom_call" | custom-call | flops 1 | bytes 1 | tf_op jit(solution)/shard_map/pallas_call | solution.py:340
  93.7 4.3 %all-to-all-done.4.arrived = bf16[32,16,256]{2,1,0:T(8,128)(2,1)S(1)} async-done(((bf16[32,16,256]{2,1,0:T(8,128)(2,1)}), bf16[32,16,256]{2,1,0:T(8,128)(2,1)S(1)}, u32[]{:S(2)}, u32[]{:S(2)}) %all-to-all-start.4) | async-done | bytes 262176 | tf_op jit(solution)/shard_map/all_to_all | solution.py:335
  98.0 0.6 shard_map.96
  (18 shorter events, 0.2 us)
Async XLA Ops:
  0.6 0.8 copy-start.5
  4.5 6.9 %copy-start.4 = (bf16[4,16,256]{2,1,0:T(8,128)(2,1)S(1)}, bf16[4,16,256]{2,1,0:T(8,128)(2,1)}, u32[]{:S(2)}) copy-start(bf16[4,16,256]{2,1,0:T(8,128)(2,1)} %param.11) | copy-start | bytes 98308
  4.5 6.9 %copy-start.6 = (bf16[1,16,256]{2,1,0:T(8,128)(2,1)S(1)}, bf16[1,16,256]{2,1,0:T(8,128)(2,1)}, u32[]{:S(2)}) copy-start(bf16[1,16,256]{2,1,0:T(8,128)(2,1)} %param.8) | copy-start | bytes 24580
  4.5 7.0 %slice-start.1 = ((bf16[4,16,256]{2,1,0:T(8,128)(2,1)}), bf16[3,16,256]{2,1,0:T(8,128)(2,1)S(1)}, s32[]{:S(2)}) async-start(bf16[4,16,256]{2,1,0:T(8,128)(2,1)} %param.6), calls=%async_computation.6 | async-start | bytes 49152 | tf_op jit(solution)/shard_map/slice | solution.py:290
  4.5 7.0 %slice-start.2 = ((bf16[4,16,256]{2,1,0:T(8,128)(2,1)}), bf16[3,16,256]{2,1,0:T(8,128)(2,1)S(1)}, s32[]{:S(2)}) async-start(bf16[4,16,256]{2,1,0:T(8,128)(2,1)} %param.11), calls=%async_computation.7 | async-start | bytes 49152 | tf_op jit(solution)/shard_map/slice | solution.py:290
  4.5 19.0 %all-to-all-start = ((bf16[16,5,16,256]{3,2,1,0:T(8,128)(2,1)}), bf16[16,5,16,256]{3,2,1,0:T(8,128)(2,1)S(1)}, u32[]{:S(2)}, u32[]{:S(2)}) async-start(bf16[16,5,16,256]{3,2,1,0:T(8,128)(2,1)} %broadcast_in_dim.14), calls=%async_computation | async-start | bytes 1310720 | tf_op jit(solution)/shard_map/all_to_all | solution.py:284
  11.4 3.1 %copy-start.3 = (bf16[1,16,27,512]{3,1,2,0:T(8,128)(2,1)S(1)}, bf16[1,16,27,512]{3,1,2,0:T(8,128)(2,1)}, u32[]{:S(2)}) copy-start(bf16[1,16,27,512]{3,1,2,0:T(8,128)(2,1)} %param.10) | copy-start | bytes 1327108
  13.8 0.7 copy-start.1
  14.5 2.6 %copy-start.2 = (bf16[7,32,256]{2,1,0:T(8,128)(2,1)S(1)}, bf16[7,32,256]{2,1,0:T(8,128)(2,1)}, u32[]{:S(2)}) copy-start(bf16[7,32,256]{2,1,0:T(8,128)(2,1)} %copy-done.1) | copy-start | bytes 344068
  14.5 2.6 %slice-start = ((bf16[7,32,256]{2,1,0:T(8,128)(2,1)}), bf16[3,32,256]{2,1,0:T(8,128)(2,1)S(1)}, s32[]{:S(2)}) async-start(bf16[7,32,256]{2,1,0:T(8,128)(2,1)} %copy-done.1), calls=%async_computation.5 | async-start | bytes 98304 | tf_op jit(solution)/shard_map/slice | solution.py:293
  24.5 2.0 %collective-permute-start = (bf16[32,256]{1,0:T(8,128)(2,1)S(1)}, bf16[32,256]{1,0:T(8,128)(2,1)S(1)}, u32[]{:S(2)}, u32[]{:S(2)}) collective-permute-start(bf16[32,256]{1,0:T(8,128)(2,1)S(1)} %get-tuple-element.45.refs_0_), channel_id=1, source_target_pairs={{0,32},{2,34},{4,36},{6,38},{8,40},{10,42},{12,44},{14,46},{16,48}... | collective-permute-start | bytes 49160 | tf_op jit(solution)/shard_map/ppermute | solution.py:308
  25.2 33.7 %collective-permute-start.3 = (bf16[16,5,16,256]{3,2,1,0:T(8,128)(2,1)S(1)}, bf16[16,5,16,256]{3,2,1,0:T(8,128)(2,1)S(1)}, u32[]{:S(2)}, u32[]{:S(2)}) collective-permute-start(bf16[16,5,16,256]{3,2,1,0:T(8,128)(2,1)S(1)} %all-to-all-done.near), channel_id=1, source_target_pairs={{0,1},{2,3},{4,5},{6,7},{8,9},{10,11},{12,13},{14,15},{16,17},{18,... | collective-permute-start | bytes 1966088 | tf_op jit(solution)/shard_map/ppermute | solution.py:310
  38.2 4.8 %collective-permute-start.1 = (bf16[32,256]{1,0:T(8,128)(2,1)S(1)}, bf16[32,256]{1,0:T(8,128)(2,1)S(1)}, u32[]{:S(2)}, u32[]{:S(2)}) collective-permute-start(bf16[32,256]{1,0:T(8,128)(2,1)S(1)} %shard_map.87.refs_1_.second), channel_id=1, source_target_pairs={{0,32},{2,34},{4,36},{6,38},{8,40},{10,42},{12,44},{14,46},{16,48}... | collective-permute-start | bytes 49160 | tf_op jit(solution)/shard_map/ppermute | solution.py:308
  54.1 5.8 %collective-permute-start.2 = (bf16[32,256]{1,0:T(8,128)(2,1)S(1)}, bf16[32,256]{1,0:T(8,128)(2,1)S(1)}, u32[]{:S(2)}, u32[]{:S(2)}) collective-permute-start(bf16[32,256]{1,0:T(8,128)(2,1)S(1)} %shard_map.89.refs_2_.third), channel_id=1, source_target_pairs={{0,32},{2,34},{4,36},{6,38},{8,40},{10,42},{12,44},{14,46},{16,48}... | collective-permute-start | bytes 49160 | tf_op jit(solution)/shard_map/ppermute | solution.py:308
  71.0 5.5 %collective-permute-start.4 = (bf16[32,256]{1,0:T(8,128)(2,1)S(1)}, bf16[32,256]{1,0:T(8,128)(2,1)S(1)}, u32[]{:S(2)}, u32[]{:S(2)}) collective-permute-start(bf16[32,256]{1,0:T(8,128)(2,1)S(1)} %shard_map.92.refs_3_.fourth), channel_id=1, source_target_pairs={{33,1},{35,3},{37,5},{39,7},{41,9},{43,11},{45,13},{47,15},{49,17}... | collective-permute-start | bytes 49160 | tf_op jit(solution)/shard_map/ppermute | solution.py:308
  77.4 0.7 copy-start
  78.1 13.4 %collective-permute-start.5 = (bf16[16,5,16,256]{3,2,1,0:T(8,128)(2,1)S(1)}, bf16[16,5,16,256]{3,2,1,0:T(8,128)(2,1)S(1)}, u32[]{:S(2)}, u32[]{:S(2)}) collective-permute-start(bf16[16,5,16,256]{3,2,1,0:T(8,128)(2,1)S(1)} %all-to-all-done.near), channel_id=1, source_target_pairs={{1,0},{3,2},{5,4},{7,6},{9,8},{11,10},{13,12},{15,14},{17,16},{19,... | collective-permute-start | bytes 1966088 | tf_op jit(solution)/shard_map/ppermute | solution.py:334
  85.8 12.2 %all-to-all-start.4 = ((bf16[32,16,256]{2,1,0:T(8,128)(2,1)}), bf16[32,16,256]{2,1,0:T(8,128)(2,1)S(1)}, u32[]{:S(2)}, u32[]{:S(2)}) async-start(bf16[32,16,256]{2,1,0:T(8,128)(2,1)} %copy-done), calls=%async_computation.4 | async-start | bytes 524288 | tf_op jit(solution)/shard_map/all_to_all | solution.py:335

commit v8 on v7

--- a/solution.py
+++ b/solution.py
@@ -90,8 +90,6 @@
     @pl.when(lax.axis_index("core") == 0)
     def _():
         silu_into(act, filters, near[:, 0:2], taps, where)
-        for slope in (first, second):
-            slope[...] = jnp.zeros_like(slope)
 
     @pl.when(lax.axis_index("core") != 0)
     def _():
@@ -101,11 +99,6 @@
 
 
 def slope_kernel(filters, near, far, third, fourth, taps, whole):
-    @pl.when(lax.axis_index("core") == 0)
-    def _():
-        for slope in (third, fourth):
-            slope[...] = jnp.zeros_like(slope)
-
     @pl.when(lax.axis_index("core") != 0)
     def _():
         where = coordinates(OWN)
@@ -138,10 +131,6 @@
 
 
 def sum_kernel(arrived, out):
-    @pl.when(lax.axis_index("core") == 0)
-    def _():
-        out[...] = jnp.zeros_like(out)
-
     @pl.when(lax.axis_index("core") != 0)
     def _():
         sum_into(out, arrived)
@@ -188,9 +177,7 @@
     def _():
         copy = value.astype(jnp.bfloat16)
         dpre[...] = copy
-        if last:
-            sent[...] = jnp.zeros_like(sent)
-        else:
+        if not last:
             for p in range(sent.shape[0]):
                 sent[p] = copy
 

time: 99.3 us -> 99.3 us (level)
  no operation moved by 1% of the time
where the time goes in v8:
time: 99.3 us; the launch traced here: 98.6 us
  blocking collectives  40.1 us (40%)
  starting transfers between devices  33.5 us (34%)
  waiting for transfers between devices  12.5 us (13%)
  Pallas kernels  8.56 us (9%)
  local copies, waits for them, and re-layouts  2.27 us (2%)
    all_to_all x3, blocking collectives, body(): arrived = lax.all_to_all(sent, 'chip', 0, 0)  31.1 us
    ppermute x4, starting transfers between devices, body(): received = lax.ppermute(outs[step], ('section', 'chip', 'core'), hops[step])  13.9 us
    ppermute x1, starting transfers between devices, body(): back_far = lax.ppermute(near, 'core', [(1, 0)])  7.71 us
    all_to_all x1, starting transfers between devices, body(): lax.all_to_all(jnp.broadcast_to(block[None], (chips,) + block.shape), 'ch...  6.9 us
    all_to_all x1, waiting for transfers between devices, body(): lax.all_to_all(jnp.broadcast_to(block[None], (chips,) + block.shape), 'ch...  6.5 us
    all_to_all x1, waiting for transfers between devices, body(): partials = lax.all_to_all(sent, ('chip', 'core'), 0, 0)  4.26 us
    all_to_all x1, starting transfers between devices, body(): partials = lax.all_to_all(sent, ('chip', 'core'), 0, 0)  3.66 us
    pallas_call x4, Pallas kernels, body(): local_call(functools.partial(start_kernel, step), (sent_shape, mine), 4,...  3.55 us
  transfers between devices with their start and end apart: 8, of which 4 were waited for; matrix products, arithmetic and copies ran while one was open for 0% of the time, Pallas kernels for 5%

profile of v8, /device:TPU:385, one launch (start us, length us, event | category | flops | bytes accessed | tf_op | source)
XLA Modules:
  0.0 98.6 jit_solution(1537241332688373329)
XLA Ops:
  0.6 0.0 copy-start.5
  0.6 0.7 slice_select_fusion.2
  1.4 0.0 copy-done.5
  1.4 2.2 %all_gather.15 = bf16[5,32,256]{2,1,0:T(8,128)(2,1)S(1)} all-gather(bf16[5,16,256]{2,1,0:T(8,128)(2,1)S(1)} %pad_maximum_fusion.1), channel_id=1, replica_groups=mesh['section'=16,'chip'=16,'core'=2] {'core'}, dimensions={1}, use_global_device_ids=true | all-gather | bytes 122880 | tf_op jit(solution)/shard_map/all_gather | solution.py:263
  3.6 0.9 broadcast_in_dim.14
  4.5 0.0 copy-start.4
  4.5 0.0 copy-start.6
  4.5 6.9 %all-to-all-start = ((bf16[16,5,16,256]{3,2,1,0:T(8,128)(2,1)}), bf16[16,5,16,256]{3,2,1,0:T(8,128)(2,1)S(1)}, u32[]{:S(2)}, u32[]{:S(2)}) async-start(bf16[16,5,16,256]{3,2,1,0:T(8,128)(2,1)} %broadcast_in_dim.14), calls=%async_computation | async-start | bytes 1310720 | tf_op jit(solution)/shard_map/all_to_all | solution.py:271
  11.4 0.0 copy-start.3
  11.4 0.0 copy-done.4
  11.4 0.0 copy-done.6
  11.5 0.0 slice-done.1
  11.5 0.0 slice-done.2
  11.5 2.3 %all_gather.17 = bf16[7,32,256]{2,1,0:T(8,128)(2,1)S(1)} all-gather(bf16[7,16,256]{2,1,0:T(8,128)(2,1)S(1)} %pad_maximum_fusion), channel_id=1, replica_groups=mesh['section'=16,'chip'=16,'core'=2] {'core'}, dimensions={1}, use_global_device_ids=true | all-gather | bytes 172032 | tf_op jit(solution)/shard_map/all_gather | solution.py:279
  13.8 0.6 copy-done.1
  14.5 0.0 copy-done.3
  14.5 2.6 %all_gather.16.filters = bf16[864,512]{1,0:T(8,128)(2,1)S(1)} all-gather(bf16[432,512]{1,0:T(8,128)(2,1)S(1)} %bitcast.37), channel_id=1, replica_groups=mesh['section'=16,'chip'=16,'core'=2] {'core'}, dimensions={0}, use_global_device_ids=true | all-gather | bytes 1327104 | tf_op jit(solution)/shard_map/all_gather | solution.py:273
  17.0 0.0 copy-done.2
  17.0 0.0 slice-done
  17.0 6.5 %all-to-all-done.near = bf16[16,5,16,256]{3,2,1,0:T(8,128)(2,1)S(1)} async-done(((bf16[16,5,16,256]{3,2,1,0:T(8,128)(2,1)}), bf16[16,5,16,256]{3,2,1,0:T(8,128)(2,1)S(1)}, u32[]{:S(2)}, u32[]{:S(2)}) %all-to-all-start) | async-done | bytes 655392 | tf_op jit(solution)/shard_map/all_to_all | solution.py:271
  23.5 1.0 %shard_map.85 = (bf16[32,256]{1,0:T(8,128)(2,1)S(1)}, f32[32,256]{1,0:T(8,128)S(1)}, f32[32,256]{1,0:T(8,128)S(1)}) custom-call(bf16[16,5,16,256]{3,2,1,0:T(8,128)(2,1)S(1)} %all-to-all-done.near, bf16[864,512]{1,0:T(8,128)(2,1)S(1)} %all_gather.16.filters), custom_call_target="tpu_custom_call" | custom-call | tf_op jit(solution)/shard_map/pallas_call | solution.py:287
  24.5 0.7 collective-permute-start
  25.2 1.3 %collective-permute-start.3 = (bf16[16,5,16,256]{3,2,1,0:T(8,128)(2,1)S(1)}, bf16[16,5,16,256]{3,2,1,0:T(8,128)(2,1)S(1)}, u32[]{:S(2)}, u32[]{:S(2)}) collective-permute-start(bf16[16,5,16,256]{3,2,1,0:T(8,128)(2,1)S(1)} %all-to-all-done.near), channel_id=1, source_target_pairs={{0,1},{2,3},{4,5},{6,7},{8,9},{10,11},{12,13},{14,15},{16,17},{18,... | collective-permute-start | bytes 1966088 | tf_op jit(solution)/shard_map/ppermute | solution.py:297
  26.5 0.0 collective-permute-done.received
  26.5 0.9 shard_map.86
  27.4 10.8 %all_to_all.25.arrived = bf16[16,32,256]{2,1,0:T(8,128)(2,1)S(1)} all-to-all(bf16[16,32,256]{2,1,0:T(8,128)(2,1)S(1)} %get-tuple-element.48), channel_id=1, replica_groups=mesh['section'=16,'chip'=16,'core'=2] {'chip'}, dimensions={0} | all-to-all | bytes 524288 | tf_op jit(solution)/shard_map/all_to_all | solution.py:314
  38.2 3.8 %collective-permute-start.1 = (bf16[32,256]{1,0:T(8,128)(2,1)S(1)}, bf16[32,256]{1,0:T(8,128)(2,1)S(1)}, u32[]{:S(2)}, u32[]{:S(2)}) collective-permute-start(bf16[32,256]{1,0:T(8,128)(2,1)S(1)} %shard_map.87.refs_1_.second), channel_id=1, source_target_pairs={{0,32},{2,34},{4,36},{6,38},{8,40},{10,42},{12,44},{14,46},{16,48}... | collective-permute-start | bytes 49160 | tf_op jit(solution)/shard_map/ppermute | solution.py:295
  42.1 0.9 collective-permute-done.1.received
  43.0 0.9 shard_map.88
  43.9 10.2 %all_to_all.26.arrived = bf16[16,32,256]{2,1,0:T(8,128)(2,1)S(1)} all-to-all(bf16[16,32,256]{2,1,0:T(8,128)(2,1)S(1)} %get-tuple-element.53), channel_id=1, replica_groups=mesh['section'=16,'chip'=16,'core'=2] {'chip'}, dimensions={0} | all-to-all | bytes 524288 | tf_op jit(solution)/shard_map/all_to_all | solution.py:314
  54.1 4.8 %collective-permute-start.2 = (bf16[32,256]{1,0:T(8,128)(2,1)S(1)}, bf16[32,256]{1,0:T(8,128)(2,1)S(1)}, u32[]{:S(2)}, u32[]{:S(2)}) collective-permute-start(bf16[32,256]{1,0:T(8,128)(2,1)S(1)} %shard_map.89.refs_2_.third), channel_id=1, source_target_pairs={{0,32},{2,34},{4,36},{6,38},{8,40},{10,42},{12,44},{14,46},{16,48}... | collective-permute-start | bytes 49160 | tf_op jit(solution)/shard_map/ppermute | solution.py:295
  58.9 0.0 collective-permute-done.3.far
  58.9 1.0 %shard_map.90 = (f32[32,256]{1,0:T(8,128)S(1)}, f32[32,256]{1,0:T(8,128)S(1)}) custom-call(bf16[864,512]{1,0:T(8,128)(2,1)S(1)} %all_gather.16.filters, bf16[16,5,16,256]{3,2,1,0:T(8,128)(2,1)S(1)} %all-to-all-done.near, bf16[16,5,16,256]{3,2,1,0:T(8,128)(2,1)S(1)} %collective-permute-done.3.far), custom_call_target="tpu_custom_call" | custom-call | flops 1 | bytes 1 | tf_op jit(solution)/shard_map/pallas_call | solution.py:299
  59.9 0.0 collective-permute-done.2.received
  59.9 0.9 shard_map.91
  60.8 10.2 %all_to_all.27.arrived = bf16[16,32,256]{2,1,0:T(8,128)(2,1)S(1)} all-to-all(bf16[16,32,256]{2,1,0:T(8,128)(2,1)S(1)} %get-tuple-element.62), channel_id=1, replica_groups=mesh['section'=16,'chip'=16,'core'=2] {'chip'}, dimensions={0} | all-to-all | bytes 524288 | tf_op jit(solution)/shard_map/all_to_all | solution.py:314
  71.0 4.6 %collective-permute-start.4 = (bf16[32,256]{1,0:T(8,128)(2,1)S(1)}, bf16[32,256]{1,0:T(8,128)(2,1)S(1)}, u32[]{:S(2)}, u32[]{:S(2)}) collective-permute-start(bf16[32,256]{1,0:T(8,128)(2,1)S(1)} %shard_map.92.refs_3_.fourth), channel_id=1, source_target_pairs={{33,1},{35,3},{37,5},{39,7},{41,9},{43,11},{45,13},{47,15},{49,17}... | collective-permute-start | bytes 49160 | tf_op jit(solution)/shard_map/ppermute | solution.py:295
  75.7 0.8 collective-permute-done.4.received
  76.5 0.9 shard_map.93
  77.4 0.0 copy-start
  77.4 0.7 copy-done
  78.1 7.7 %collective-permute-start.5 = (bf16[16,5,16,256]{3,2,1,0:T(8,128)(2,1)S(1)}, bf16[16,5,16,256]{3,2,1,0:T(8,128)(2,1)S(1)}, u32[]{:S(2)}, u32[]{:S(2)}) collective-permute-start(bf16[16,5,16,256]{3,2,1,0:T(8,128)(2,1)S(1)} %all-to-all-done.near), channel_id=1, source_target_pairs={{1,0},{3,2},{5,4},{7,6},{9,8},{11,10},{13,12},{15,14},{17,16},{19,... | collective-permute-start | bytes 1966088 | tf_op jit(solution)/shard_map/ppermute | solution.py:321
  85.8 3.7 %all-to-all-start.4 = ((bf16[32,16,256]{2,1,0:T(8,128)(2,1)}), bf16[32,16,256]{2,1,0:T(8,128)(2,1)S(1)}, u32[]{:S(2)}, u32[]{:S(2)}) async-start(bf16[32,16,256]{2,1,0:T(8,128)(2,1)} %copy-done), calls=%async_computation.4 | async-start | bytes 524288 | tf_op jit(solution)/shard_map/all_to_all | solution.py:322
  89.5 2.0 %all-gather = bf16[14,16,256]{2,1,0:T(8,128)(2,1)S(1)} all-gather(bf16[7,16,256]{2,1,0:T(8,128)(2,1)S(1)} %get-tuple-element.78), channel_id=2, replica_groups=mesh['section'=16,'chip'=16,'core'=2] {'core'}, dimensions={0}, use_global_device_ids=true | all-gather | bytes 172032 | tf_op jit(solution)/shard_map/all_gather | solution.py:326
  91.5 0.0 collective-permute-done.5.back_far
  91.5 2.2 %shard_map.95 = (f32[432,512]{1,0:T(8,128)}, bf16[4,16,256]{2,1,0:T(8,128)(2,1)}) custom-call(bf16[16,5,16,256]{3,2,1,0:T(8,128)(2,1)S(1)} %all-to-all-done.near, bf16[16,5,16,256]{3,2,1,0:T(8,128)(2,1)S(1)} %collective-permute-done.3.far, bf16[16,5,16,256]{3,2,1,0:T(8,128)(2,1)S(1)} %collective-permute-done.5.back_far, ...), custom_call_target="tpu_custom_call" | custom-call | flops 1 | bytes 1 | tf_op jit(solution)/shard_map/pallas_call | solution.py:327
  93.7 4.3 %all-to-all-done.4.arrived = bf16[32,16,256]{2,1,0:T(8,128)(2,1)S(1)} async-done(((bf16[32,16,256]{2,1,0:T(8,128)(2,1)}), bf16[32,16,256]{2,1,0:T(8,128)(2,1)S(1)}, u32[]{:S(2)}, u32[]{:S(2)}) %all-to-all-start.4) | async-done | bytes 262176 | tf_op jit(solution)/shard_map/all_to_all | solution.py:322
  98.0 0.6 shard_map.96
  (18 shorter events, 0.2 us)
Async XLA Ops:
  0.6 0.8 copy-start.5
  4.5 6.9 %copy-start.4 = (bf16[4,16,256]{2,1,0:T(8,128)(2,1)S(1)}, bf16[4,16,256]{2,1,0:T(8,128)(2,1)}, u32[]{:S(2)}) copy-start(bf16[4,16,256]{2,1,0:T(8,128)(2,1)} %param.11) | copy-start | bytes 98308
  4.5 6.9 %copy-start.6 = (bf16[1,16,256]{2,1,0:T(8,128)(2,1)S(1)}, bf16[1,16,256]{2,1,0:T(8,128)(2,1)}, u32[]{:S(2)}) copy-start(bf16[1,16,256]{2,1,0:T(8,128)(2,1)} %param.8) | copy-start | bytes 24580
  4.5 7.0 %slice-start.1 = ((bf16[4,16,256]{2,1,0:T(8,128)(2,1)}), bf16[3,16,256]{2,1,0:T(8,128)(2,1)S(1)}, s32[]{:S(2)}) async-start(bf16[4,16,256]{2,1,0:T(8,128)(2,1)} %param.6), calls=%async_computation.6 | async-start | bytes 49152 | tf_op jit(solution)/shard_map/slice | solution.py:277
  4.5 7.0 %slice-start.2 = ((bf16[4,16,256]{2,1,0:T(8,128)(2,1)}), bf16[3,16,256]{2,1,0:T(8,128)(2,1)S(1)}, s32[]{:S(2)}) async-start(bf16[4,16,256]{2,1,0:T(8,128)(2,1)} %param.11), calls=%async_computation.7 | async-start | bytes 49152 | tf_op jit(solution)/shard_map/slice | solution.py:277
  4.5 19.0 %all-to-all-start = ((bf16[16,5,16,256]{3,2,1,0:T(8,128)(2,1)}), bf16[16,5,16,256]{3,2,1,0:T(8,128)(2,1)S(1)}, u32[]{:S(2)}, u32[]{:S(2)}) async-start(bf16[16,5,16,256]{3,2,1,0:T(8,128)(2,1)} %broadcast_in_dim.14), calls=%async_computation | async-start | bytes 1310720 | tf_op jit(solution)/shard_map/all_to_all | solution.py:271
  11.4 3.1 %copy-start.3 = (bf16[1,16,27,512]{3,1,2,0:T(8,128)(2,1)S(1)}, bf16[1,16,27,512]{3,1,2,0:T(8,128)(2,1)}, u32[]{:S(2)}) copy-start(bf16[1,16,27,512]{3,1,2,0:T(8,128)(2,1)} %param.10) | copy-start | bytes 1327108
  13.8 0.7 copy-start.1
  14.5 2.6 %copy-start.2 = (bf16[7,32,256]{2,1,0:T(8,128)(2,1)S(1)}, bf16[7,32,256]{2,1,0:T(8,128)(2,1)}, u32[]{:S(2)}) copy-start(bf16[7,32,256]{2,1,0:T(8,128)(2,1)} %copy-done.1) | copy-start | bytes 344068
  14.5 2.6 %slice-start = ((bf16[7,32,256]{2,1,0:T(8,128)(2,1)}), bf16[3,32,256]{2,1,0:T(8,128)(2,1)S(1)}, s32[]{:S(2)}) async-start(bf16[7,32,256]{2,1,0:T(8,128)(2,1)} %copy-done.1), calls=%async_computation.5 | async-start | bytes 98304 | tf_op jit(solution)/shard_map/slice | solution.py:280
  24.5 2.0 %collective-permute-start = (bf16[32,256]{1,0:T(8,128)(2,1)S(1)}, bf16[32,256]{1,0:T(8,128)(2,1)S(1)}, u32[]{:S(2)}, u32[]{:S(2)}) collective-permute-start(bf16[32,256]{1,0:T(8,128)(2,1)S(1)} %get-tuple-element.45.refs_0_), channel_id=1, source_target_pairs={{0,32},{2,34},{4,36},{6,38},{8,40},{10,42},{12,44},{14,46},{16,48}... | collective-permute-start | bytes 49160 | tf_op jit(solution)/shard_map/ppermute | solution.py:295
  25.2 33.7 %collective-permute-start.3 = (bf16[16,5,16,256]{3,2,1,0:T(8,128)(2,1)S(1)}, bf16[16,5,16,256]{3,2,1,0:T(8,128)(2,1)S(1)}, u32[]{:S(2)}, u32[]{:S(2)}) collective-permute-start(bf16[16,5,16,256]{3,2,1,0:T(8,128)(2,1)S(1)} %all-to-all-done.near), channel_id=1, source_target_pairs={{0,1},{2,3},{4,5},{6,7},{8,9},{10,11},{12,13},{14,15},{16,17},{18,... | collective-permute-start | bytes 1966088 | tf_op jit(solution)/shard_map/ppermute | solution.py:297
  38.2 4.8 %collective-permute-start.1 = (bf16[32,256]{1,0:T(8,128)(2,1)S(1)}, bf16[32,256]{1,0:T(8,128)(2,1)S(1)}, u32[]{:S(2)}, u32[]{:S(2)}) collective-permute-start(bf16[32,256]{1,0:T(8,128)(2,1)S(1)} %shard_map.87.refs_1_.second), channel_id=1, source_target_pairs={{0,32},{2,34},{4,36},{6,38},{8,40},{10,42},{12,44},{14,46},{16,48}... | collective-permute-start | bytes 49160 | tf_op jit(solution)/shard_map/ppermute | solution.py:295
  54.1 5.8 %collective-permute-start.2 = (bf16[32,256]{1,0:T(8,128)(2,1)S(1)}, bf16[32,256]{1,0:T(8,128)(2,1)S(1)}, u32[]{:S(2)}, u32[]{:S(2)}) collective-permute-start(bf16[32,256]{1,0:T(8,128)(2,1)S(1)} %shard_map.89.refs_2_.third), channel_id=1, source_target_pairs={{0,32},{2,34},{4,36},{6,38},{8,40},{10,42},{12,44},{14,46},{16,48}... | collective-permute-start | bytes 49160 | tf_op jit(solution)/shard_map/ppermute | solution.py:295
  71.0 5.5 %collective-permute-start.4 = (bf16[32,256]{1,0:T(8,128)(2,1)S(1)}, bf16[32,256]{1,0:T(8,128)(2,1)S(1)}, u32[]{:S(2)}, u32[]{:S(2)}) collective-permute-start(bf16[32,256]{1,0:T(8,128)(2,1)S(1)} %shard_map.92.refs_3_.fourth), channel_id=1, source_target_pairs={{33,1},{35,3},{37,5},{39,7},{41,9},{43,11},{45,13},{47,15},{49,17}... | collective-permute-start | bytes 49160 | tf_op jit(solution)/shard_map/ppermute | solution.py:295
  77.4 0.7 copy-start
  78.1 13.4 %collective-permute-start.5 = (bf16[16,5,16,256]{3,2,1,0:T(8,128)(2,1)S(1)}, bf16[16,5,16,256]{3,2,1,0:T(8,128)(2,1)S(1)}, u32[]{:S(2)}, u32[]{:S(2)}) collective-permute-start(bf16[16,5,16,256]{3,2,1,0:T(8,128)(2,1)S(1)} %all-to-all-done.near), channel_id=1, source_target_pairs={{1,0},{3,2},{5,4},{7,6},{9,8},{11,10},{13,12},{15,14},{17,16},{19,... | collective-permute-start | bytes 1966088 | tf_op jit(solution)/shard_map/ppermute | solution.py:321
  85.8 12.2 %all-to-all-start.4 = ((bf16[32,16,256]{2,1,0:T(8,128)(2,1)}), bf16[32,16,256]{2,1,0:T(8,128)(2,1)S(1)}, u32[]{:S(2)}, u32[]{:S(2)}) async-start(bf16[32,16,256]{2,1,0:T(8,128)(2,1)} %copy-done), calls=%async_computation.4 | async-start | bytes 524288 | tf_op jit(solution)/shard_map/all_to_all | solution.py:322

commit v9 on v8

--- a/solution.py
+++ b/solution.py
@@ -93,7 +93,6 @@
 
     @pl.when(lax.axis_index("core") != 0)
     def _():
-        act[...] = jnp.zeros_like(act)
         slope_into(first, filters, near[:, 0:2], taps, where)
         slope_into(second, filters, near[:, 2:4], taps, where)
 
@@ -149,7 +148,6 @@
 
     @pl.when(lax.axis_index("core") != 0)
     def _():
-        act[...] = jnp.zeros_like(act)
         for r, pair in enumerate((*dpres, *outs[1:], grad)):
             parcel[r] = pair[:OWN, :]
 
@@ -176,7 +174,6 @@
     @pl.when(lax.axis_index("core") == 0)
     def _():
         copy = value.astype(jnp.bfloat16)
-        dpre[...] = copy
         if not last:
             for p in range(sent.shape[0]):
                 sent[p] = copy

time: 99.3 us -> 99.3 us (level)
  no operation moved by 1% of the time
where the time goes in v9:
time: 99.3 us; the launch traced here: 98.6 us
  blocking collectives  40.1 us (40%)
  starting transfers between devices  33.4 us (34%)
  waiting for transfers between devices  12.5 us (13%)
  Pallas kernels  8.56 us (9%)
  local copies, waits for them, and re-layouts  2.27 us (2%)
    all_to_all x3, blocking collectives, body(): arrived = lax.all_to_all(sent, 'chip', 0, 0)  31.1 us
    ppermute x4, starting transfers between devices, body(): received = lax.ppermute(outs[step], ('section', 'chip', 'core'), hops[step])  13.9 us
    ppermute x1, starting transfers between devices, body(): back_far = lax.ppermute(near, 'core', [(1, 0)])  7.69 us
    all_to_all x1, starting transfers between devices, body(): lax.all_to_all(jnp.broadcast_to(block[None], (chips,) + block.shape), 'ch...  6.9 us
    all_to_all x1, waiting for transfers between devices, body(): lax.all_to_all(jnp.broadcast_to(block[None], (chips,) + block.shape), 'ch...  6.5 us
    all_to_all x1, waiting for transfers between devices, body(): partials = lax.all_to_all(sent, ('chip', 'core'), 0, 0)  4.27 us
    all_to_all x1, starting transfers between devices, body(): partials = lax.all_to_all(sent, ('chip', 'core'), 0, 0)  3.66 us
    pallas_call x4, Pallas kernels, body(): local_call(functools.partial(start_kernel, step), (sent_shape, mine), 4,...  3.55 us
  transfers between devices with their start and end apart: 8, of which 4 were waited for; matrix products, arithmetic and copies ran while one was open for 0% of the time, Pallas kernels for 5%

profile of v9, /device:TPU:385, one launch (start us, length us, event | category | flops | bytes accessed | tf_op | source)
XLA Modules:
  0.0 98.6 jit_solution(16054538050991416443)
XLA Ops:
  0.6 0.0 copy-start.5
  0.6 0.7 slice_select_fusion.2
  1.4 0.0 copy-done.5
  1.4 2.2 %all_gather.15 = bf16[5,32,256]{2,1,0:T(8,128)(2,1)S(1)} all-gather(bf16[5,16,256]{2,1,0:T(8,128)(2,1)S(1)} %pad_maximum_fusion.1), channel_id=1, replica_groups=mesh['section'=16,'chip'=16,'core'=2] {'core'}, dimensions={1}, use_global_device_ids=true | all-gather | bytes 122880 | tf_op jit(solution)/shard_map/all_gather | solution.py:260
  3.6 0.9 broadcast_in_dim.14
  4.5 0.0 copy-start.4
  4.5 0.0 copy-start.6
  4.5 6.9 %all-to-all-start = ((bf16[16,5,16,256]{3,2,1,0:T(8,128)(2,1)}), bf16[16,5,16,256]{3,2,1,0:T(8,128)(2,1)S(1)}, u32[]{:S(2)}, u32[]{:S(2)}) async-start(bf16[16,5,16,256]{3,2,1,0:T(8,128)(2,1)} %broadcast_in_dim.14), calls=%async_computation | async-start | bytes 1310720 | tf_op jit(solution)/shard_map/all_to_all | solution.py:268
  11.4 0.0 copy-start.3
  11.4 0.0 copy-done.4
  11.4 0.0 copy-done.6
  11.5 0.0 slice-done.1
  11.5 0.0 slice-done.2
  11.5 2.3 %all_gather.17 = bf16[7,32,256]{2,1,0:T(8,128)(2,1)S(1)} all-gather(bf16[7,16,256]{2,1,0:T(8,128)(2,1)S(1)} %pad_maximum_fusion), channel_id=1, replica_groups=mesh['section'=16,'chip'=16,'core'=2] {'core'}, dimensions={1}, use_global_device_ids=true | all-gather | bytes 172032 | tf_op jit(solution)/shard_map/all_gather | solution.py:276
  13.8 0.6 copy-done.1
  14.5 0.0 copy-done.3
  14.5 2.6 %all_gather.16.filters = bf16[864,512]{1,0:T(8,128)(2,1)S(1)} all-gather(bf16[432,512]{1,0:T(8,128)(2,1)S(1)} %bitcast.37), channel_id=1, replica_groups=mesh['section'=16,'chip'=16,'core'=2] {'core'}, dimensions={0}, use_global_device_ids=true | all-gather | bytes 1327104 | tf_op jit(solution)/shard_map/all_gather | solution.py:270
  17.0 0.0 copy-done.2
  17.0 0.0 slice-done
  17.0 6.5 %all-to-all-done.near = bf16[16,5,16,256]{3,2,1,0:T(8,128)(2,1)S(1)} async-done(((bf16[16,5,16,256]{3,2,1,0:T(8,128)(2,1)}), bf16[16,5,16,256]{3,2,1,0:T(8,128)(2,1)S(1)}, u32[]{:S(2)}, u32[]{:S(2)}) %all-to-all-start) | async-done | bytes 655392 | tf_op jit(solution)/shard_map/all_to_all | solution.py:268
  23.5 1.0 %shard_map.85 = (bf16[32,256]{1,0:T(8,128)(2,1)S(1)}, f32[32,256]{1,0:T(8,128)S(1)}, f32[32,256]{1,0:T(8,128)S(1)}) custom-call(bf16[16,5,16,256]{3,2,1,0:T(8,128)(2,1)S(1)} %all-to-all-done.near, bf16[864,512]{1,0:T(8,128)(2,1)S(1)} %all_gather.16.filters), custom_call_target="tpu_custom_call" | custom-call | tf_op jit(solution)/shard_map/pallas_call | solution.py:284
  24.5 0.7 collective-permute-start
  25.2 1.3 %collective-permute-start.3 = (bf16[16,5,16,256]{3,2,1,0:T(8,128)(2,1)S(1)}, bf16[16,5,16,256]{3,2,1,0:T(8,128)(2,1)S(1)}, u32[]{:S(2)}, u32[]{:S(2)}) collective-permute-start(bf16[16,5,16,256]{3,2,1,0:T(8,128)(2,1)S(1)} %all-to-all-done.near), channel_id=1, source_target_pairs={{0,1},{2,3},{4,5},{6,7},{8,9},{10,11},{12,13},{14,15},{16,17},{18,... | collective-permute-start | bytes 1966088 | tf_op jit(solution)/shard_map/ppermute | solution.py:294
  26.5 0.0 collective-permute-done.received
  26.5 0.9 shard_map.86
  27.4 10.8 %all_to_all.25.arrived = bf16[16,32,256]{2,1,0:T(8,128)(2,1)S(1)} all-to-all(bf16[16,32,256]{2,1,0:T(8,128)(2,1)S(1)} %get-tuple-element.48), channel_id=1, replica_groups=mesh['section'=16,'chip'=16,'core'=2] {'chip'}, dimensions={0} | all-to-all | bytes 524288 | tf_op jit(solution)/shard_map/all_to_all | solution.py:311
  38.2 3.8 %collective-permute-start.1 = (bf16[32,256]{1,0:T(8,128)(2,1)S(1)}, bf16[32,256]{1,0:T(8,128)(2,1)S(1)}, u32[]{:S(2)}, u32[]{:S(2)}) collective-permute-start(bf16[32,256]{1,0:T(8,128)(2,1)S(1)} %shard_map.87.refs_1_.second), channel_id=1, source_target_pairs={{0,32},{2,34},{4,36},{6,38},{8,40},{10,42},{12,44},{14,46},{16,48}... | collective-permute-start | bytes 49160 | tf_op jit(solution)/shard_map/ppermute | solution.py:292
  42.1 0.9 collective-permute-done.1.received
  43.0 0.9 shard_map.88
  43.9 10.2 %all_to_all.26.arrived = bf16[16,32,256]{2,1,0:T(8,128)(2,1)S(1)} all-to-all(bf16[16,32,256]{2,1,0:T(8,128)(2,1)S(1)} %get-tuple-element.53), channel_id=1, replica_groups=mesh['section'=16,'chip'=16,'core'=2] {'chip'}, dimensions={0} | all-to-all | bytes 524288 | tf_op jit(solution)/shard_map/all_to_all | solution.py:311
  54.1 4.8 %collective-permute-start.2 = (bf16[32,256]{1,0:T(8,128)(2,1)S(1)}, bf16[32,256]{1,0:T(8,128)(2,1)S(1)}, u32[]{:S(2)}, u32[]{:S(2)}) collective-permute-start(bf16[32,256]{1,0:T(8,128)(2,1)S(1)} %shard_map.89.refs_2_.third), channel_id=1, source_target_pairs={{0,32},{2,34},{4,36},{6,38},{8,40},{10,42},{12,44},{14,46},{16,48}... | collective-permute-start | bytes 49160 | tf_op jit(solution)/shard_map/ppermute | solution.py:292
  58.9 0.0 collective-permute-done.3.far
  58.9 1.0 %shard_map.90 = (f32[32,256]{1,0:T(8,128)S(1)}, f32[32,256]{1,0:T(8,128)S(1)}) custom-call(bf16[864,512]{1,0:T(8,128)(2,1)S(1)} %all_gather.16.filters, bf16[16,5,16,256]{3,2,1,0:T(8,128)(2,1)S(1)} %all-to-all-done.near, bf16[16,5,16,256]{3,2,1,0:T(8,128)(2,1)S(1)} %collective-permute-done.3.far), custom_call_target="tpu_custom_call" | custom-call | flops 1 | bytes 1 | tf_op jit(solution)/shard_map/pallas_call | solution.py:296
  59.9 0.0 collective-permute-done.2.received
  59.9 0.9 shard_map.91
  60.8 10.2 %all_to_all.27.arrived = bf16[16,32,256]{2,1,0:T(8,128)(2,1)S(1)} all-to-all(bf16[16,32,256]{2,1,0:T(8,128)(2,1)S(1)} %get-tuple-element.62), channel_id=1, replica_groups=mesh['section'=16,'chip'=16,'core'=2] {'chip'}, dimensions={0} | all-to-all | bytes 524288 | tf_op jit(solution)/shard_map/all_to_all | solution.py:311
  71.0 4.6 %collective-permute-start.4 = (bf16[32,256]{1,0:T(8,128)(2,1)S(1)}, bf16[32,256]{1,0:T(8,128)(2,1)S(1)}, u32[]{:S(2)}, u32[]{:S(2)}) collective-permute-start(bf16[32,256]{1,0:T(8,128)(2,1)S(1)} %shard_map.92.refs_3_.fourth), channel_id=1, source_target_pairs={{33,1},{35,3},{37,5},{39,7},{41,9},{43,11},{45,13},{47,15},{49,17}... | collective-permute-start | bytes 49160 | tf_op jit(solution)/shard_map/ppermute | solution.py:292
  75.7 0.8 collective-permute-done.4.received
  76.5 0.9 shard_map.93
  77.4 0.0 copy-start
  77.4 0.7 copy-done
  78.1 7.7 %collective-permute-start.5 = (bf16[16,5,16,256]{3,2,1,0:T(8,128)(2,1)S(1)}, bf16[16,5,16,256]{3,2,1,0:T(8,128)(2,1)S(1)}, u32[]{:S(2)}, u32[]{:S(2)}) collective-permute-start(bf16[16,5,16,256]{3,2,1,0:T(8,128)(2,1)S(1)} %all-to-all-done.near), channel_id=1, source_target_pairs={{1,0},{3,2},{5,4},{7,6},{9,8},{11,10},{13,12},{15,14},{17,16},{19,... | collective-permute-start | bytes 1966088 | tf_op jit(solution)/shard_map/ppermute | solution.py:318
  85.8 3.7 %all-to-all-start.4 = ((bf16[32,16,256]{2,1,0:T(8,128)(2,1)}), bf16[32,16,256]{2,1,0:T(8,128)(2,1)S(1)}, u32[]{:S(2)}, u32[]{:S(2)}) async-start(bf16[32,16,256]{2,1,0:T(8,128)(2,1)} %copy-done), calls=%async_computation.4 | async-start | bytes 524288 | tf_op jit(solution)/shard_map/all_to_all | solution.py:319
  89.5 2.0 %all-gather = bf16[14,16,256]{2,1,0:T(8,128)(2,1)S(1)} all-gather(bf16[7,16,256]{2,1,0:T(8,128)(2,1)S(1)} %get-tuple-element.78), channel_id=2, replica_groups=mesh['section'=16,'chip'=16,'core'=2] {'core'}, dimensions={0}, use_global_device_ids=true | all-gather | bytes 172032 | tf_op jit(solution)/shard_map/all_gather | solution.py:323
  91.5 0.0 collective-permute-done.5.back_far
  91.5 2.2 %shard_map.95 = (f32[432,512]{1,0:T(8,128)}, bf16[4,16,256]{2,1,0:T(8,128)(2,1)}) custom-call(bf16[16,5,16,256]{3,2,1,0:T(8,128)(2,1)S(1)} %all-to-all-done.near, bf16[16,5,16,256]{3,2,1,0:T(8,128)(2,1)S(1)} %collective-permute-done.3.far, bf16[16,5,16,256]{3,2,1,0:T(8,128)(2,1)S(1)} %collective-permute-done.5.back_far, ...), custom_call_target="tpu_custom_call" | custom-call | flops 1 | bytes 1 | tf_op jit(solution)/shard_map/pallas_call | solution.py:324
  93.7 4.3 %all-to-all-done.4.arrived = bf16[32,16,256]{2,1,0:T(8,128)(2,1)S(1)} async-done(((bf16[32,16,256]{2,1,0:T(8,128)(2,1)}), bf16[32,16,256]{2,1,0:T(8,128)(2,1)S(1)}, u32[]{:S(2)}, u32[]{:S(2)}) %all-to-all-start.4) | async-done | bytes 262176 | tf_op jit(solution)/shard_map/all_to_all | solution.py:319
  98.0 0.6 shard_map.96
  (18 shorter events, 0.2 us)
Async XLA Ops:
  0.6 0.8 copy-start.5
  4.5 6.9 %copy-start.4 = (bf16[4,16,256]{2,1,0:T(8,128)(2,1)S(1)}, bf16[4,16,256]{2,1,0:T(8,128)(2,1)}, u32[]{:S(2)}) copy-start(bf16[4,16,256]{2,1,0:T(8,128)(2,1)} %param.11) | copy-start | bytes 98308
  4.5 6.9 %copy-start.6 = (bf16[1,16,256]{2,1,0:T(8,128)(2,1)S(1)}, bf16[1,16,256]{2,1,0:T(8,128)(2,1)}, u32[]{:S(2)}) copy-start(bf16[1,16,256]{2,1,0:T(8,128)(2,1)} %param.8) | copy-start | bytes 24580
  4.5 7.0 %slice-start.1 = ((bf16[4,16,256]{2,1,0:T(8,128)(2,1)}), bf16[3,16,256]{2,1,0:T(8,128)(2,1)S(1)}, s32[]{:S(2)}) async-start(bf16[4,16,256]{2,1,0:T(8,128)(2,1)} %param.6), calls=%async_computation.6 | async-start | bytes 49152 | tf_op jit(solution)/shard_map/slice | solution.py:274
  4.5 7.0 %slice-start.2 = ((bf16[4,16,256]{2,1,0:T(8,128)(2,1)}), bf16[3,16,256]{2,1,0:T(8,128)(2,1)S(1)}, s32[]{:S(2)}) async-start(bf16[4,16,256]{2,1,0:T(8,128)(2,1)} %param.11), calls=%async_computation.7 | async-start | bytes 49152 | tf_op jit(solution)/shard_map/slice | solution.py:274
  4.5 19.0 %all-to-all-start = ((bf16[16,5,16,256]{3,2,1,0:T(8,128)(2,1)}), bf16[16,5,16,256]{3,2,1,0:T(8,128)(2,1)S(1)}, u32[]{:S(2)}, u32[]{:S(2)}) async-start(bf16[16,5,16,256]{3,2,1,0:T(8,128)(2,1)} %broadcast_in_dim.14), calls=%async_computation | async-start | bytes 1310720 | tf_op jit(solution)/shard_map/all_to_all | solution.py:268
  11.4 3.1 %copy-start.3 = (bf16[1,16,27,512]{3,1,2,0:T(8,128)(2,1)S(1)}, bf16[1,16,27,512]{3,1,2,0:T(8,128)(2,1)}, u32[]{:S(2)}) copy-start(bf16[1,16,27,512]{3,1,2,0:T(8,128)(2,1)} %param.10) | copy-start | bytes 1327108
  13.8 0.7 copy-start.1
  14.5 2.6 %copy-start.2 = (bf16[7,32,256]{2,1,0:T(8,128)(2,1)S(1)}, bf16[7,32,256]{2,1,0:T(8,128)(2,1)}, u32[]{:S(2)}) copy-start(bf16[7,32,256]{2,1,0:T(8,128)(2,1)} %copy-done.1) | copy-start | bytes 344068
  14.5 2.6 %slice-start = ((bf16[7,32,256]{2,1,0:T(8,128)(2,1)}), bf16[3,32,256]{2,1,0:T(8,128)(2,1)S(1)}, s32[]{:S(2)}) async-start(bf16[7,32,256]{2,1,0:T(8,128)(2,1)} %copy-done.1), calls=%async_computation.5 | async-start | bytes 98304 | tf_op jit(solution)/shard_map/slice | solution.py:277
  24.5 2.0 %collective-permute-start = (bf16[32,256]{1,0:T(8,128)(2,1)S(1)}, bf16[32,256]{1,0:T(8,128)(2,1)S(1)}, u32[]{:S(2)}, u32[]{:S(2)}) collective-permute-start(bf16[32,256]{1,0:T(8,128)(2,1)S(1)} %get-tuple-element.45.refs_0_), channel_id=1, source_target_pairs={{0,32},{2,34},{4,36},{6,38},{8,40},{10,42},{12,44},{14,46},{16,48}... | collective-permute-start | bytes 49160 | tf_op jit(solution)/shard_map/ppermute | solution.py:292
  25.2 33.7 %collective-permute-start.3 = (bf16[16,5,16,256]{3,2,1,0:T(8,128)(2,1)S(1)}, bf16[16,5,16,256]{3,2,1,0:T(8,128)(2,1)S(1)}, u32[]{:S(2)}, u32[]{:S(2)}) collective-permute-start(bf16[16,5,16,256]{3,2,1,0:T(8,128)(2,1)S(1)} %all-to-all-done.near), channel_id=1, source_target_pairs={{0,1},{2,3},{4,5},{6,7},{8,9},{10,11},{12,13},{14,15},{16,17},{18,... | collective-permute-start | bytes 1966088 | tf_op jit(solution)/shard_map/ppermute | solution.py:294
  38.2 4.8 %collective-permute-start.1 = (bf16[32,256]{1,0:T(8,128)(2,1)S(1)}, bf16[32,256]{1,0:T(8,128)(2,1)S(1)}, u32[]{:S(2)}, u32[]{:S(2)}) collective-permute-start(bf16[32,256]{1,0:T(8,128)(2,1)S(1)} %shard_map.87.refs_1_.second), channel_id=1, source_target_pairs={{0,32},{2,34},{4,36},{6,38},{8,40},{10,42},{12,44},{14,46},{16,48}... | collective-permute-start | bytes 49160 | tf_op jit(solution)/shard_map/ppermute | solution.py:292
  54.1 5.8 %collective-permute-start.2 = (bf16[32,256]{1,0:T(8,128)(2,1)S(1)}, bf16[32,256]{1,0:T(8,128)(2,1)S(1)}, u32[]{:S(2)}, u32[]{:S(2)}) collective-permute-start(bf16[32,256]{1,0:T(8,128)(2,1)S(1)} %shard_map.89.refs_2_.third), channel_id=1, source_target_pairs={{0,32},{2,34},{4,36},{6,38},{8,40},{10,42},{12,44},{14,46},{16,48}... | collective-permute-start | bytes 49160 | tf_op jit(solution)/shard_map/ppermute | solution.py:292
  71.0 5.5 %collective-permute-start.4 = (bf16[32,256]{1,0:T(8,128)(2,1)S(1)}, bf16[32,256]{1,0:T(8,128)(2,1)S(1)}, u32[]{:S(2)}, u32[]{:S(2)}) collective-permute-start(bf16[32,256]{1,0:T(8,128)(2,1)S(1)} %shard_map.92.refs_3_.fourth), channel_id=1, source_target_pairs={{33,1},{35,3},{37,5},{39,7},{41,9},{43,11},{45,13},{47,15},{49,17}... | collective-permute-start | bytes 49160 | tf_op jit(solution)/shard_map/ppermute | solution.py:292
  77.4 0.7 copy-start
  78.1 13.4 %collective-permute-start.5 = (bf16[16,5,16,256]{3,2,1,0:T(8,128)(2,1)S(1)}, bf16[16,5,16,256]{3,2,1,0:T(8,128)(2,1)S(1)}, u32[]{:S(2)}, u32[]{:S(2)}) collective-permute-start(bf16[16,5,16,256]{3,2,1,0:T(8,128)(2,1)S(1)} %all-to-all-done.near), channel_id=1, source_target_pairs={{1,0},{3,2},{5,4},{7,6},{9,8},{11,10},{13,12},{15,14},{17,16},{19,... | collective-permute-start | bytes 1966088 | tf_op jit(solution)/shard_map/ppermute | solution.py:318
  85.8 12.2 %all-to-all-start.4 = ((bf16[32,16,256]{2,1,0:T(8,128)(2,1)}), bf16[32,16,256]{2,1,0:T(8,128)(2,1)S(1)}, u32[]{:S(2)}, u32[]{:S(2)}) async-start(bf16[32,16,256]{2,1,0:T(8,128)(2,1)} %copy-done), calls=%async_computation.4 | async-start | bytes 524288 | tf_op jit(solution)/shard_map/all_to_all | solution.py:319
